TPU v7x, 32 devices: a whole 2x2x4 slice. The times are simulated.
32 devices in a mesh: rows: 8 (over z, x), seq: 4 (over y, core).
Axes of the slice: x: 2, y: 2, z: 4, core: 2. Of those that a mesh axis runs over, the one named last changes fastest.
Arguments:
- inputs: bfloat16 [8, 2048, 1024], P('rows', 'seq'), may hold values from -6 to 6
- skip_feats: bfloat16 [8, 2048, 1024], P('rows', 'seq'), may hold values from -6 to 6
- seg_ids: int32 [8, 2048], P('rows'), may hold values from 0 to 5, never falling along the last dimension, each value on 1 to 682 neighbouring positions
- frame_valid: int32 [8, 2048], P('rows'), may hold values 0 or 1
- w_skip: bfloat16 [2048, 1024], replicated, may hold values from -0.125 to 0.125
- gain_one: bfloat16 [1024], replicated, may hold values from 0.5 to 1.5
- w_qkv: bfloat16 [1024, 3072], replicated, may hold values from -0.1875 to 0.1875
- w_out: bfloat16 [1024, 1024], replicated, may hold values from -0.5 to 0.5
- gain_two: bfloat16 [1024], replicated, may hold values from 0.5 to 1.5
- w_up: bfloat16 [1024, 4096], replicated, may hold values from -0.1875 to 0.1875
- b_up: bfloat16 [4096], replicated, may hold values from -3 to 3
- w_down: bfloat16 [4096, 1024], replicated, may hold values from -0.09375 to 0.09375
- b_down: bfloat16 [1024], replicated, may hold values from -2 to 2
- cotangent: bfloat16 [8, 2048, 1024], P('rows', 'seq'), may hold values from -6 to 6
Outputs:
- output: bfloat16 [8, 2048, 1024], P('rows', 'seq')
- input_grad: bfloat16 [8, 2048, 1024], P('rows', 'seq')
- skip_grad: bfloat16 [8, 2048, 1024], P('rows', 'seq')
- w_skip_grad: float32 [2048, 1024], P(('rows', 'seq'))
- gain_one_grad: float32 [1024], P(('rows', 'seq'))
- w_qkv_grad: float32 [1024, 3072], P(('rows', 'seq'))
- w_out_grad: float32 [1024, 1024], P(('rows', 'seq'))
- gain_two_grad: float32 [1024], P(('rows', 'seq'))
- w_up_grad: float32 [1024, 4096], P(('rows', 'seq'))
- b_up_grad: float32 [4096], P(('rows', 'seq'))
- w_down_grad: float32 [4096, 1024], P(('rows', 'seq'))
- b_down_grad: float32 [1024], P(('rows', 'seq'))
Inputs may be any that keep to these rules, and one draw needn't show every extreme that they name: `seg_ids`: in each row the segment numbers never fall along the frames; every segment has 1 to 682 frames and one has exactly 682.
All inputs are finite; a program needn't handle non-finite values. No bound on the sum of `frame_valid` on one device may be relied on, other than what follows from the above.
Results may differ from a plain program's by a relative error of at most 0.015.
Values may be sent and summed in bfloat16 or wider, within the bound.
A program may use at most 192 MiB of HBM per device.

v0:
```python
import functools
import math

import jax
import jax.numpy as jnp
from jax import lax
from jax.experimental import pallas as pl
from jax.experimental.pallas import tpu as pltpu
from jax.sharding import PartitionSpec as P

D = 1024
H = 16
HD = 64
MOST = 682

epsilon = 1e-05

F32 = jnp.float32
BF16 = jnp.bfloat16
LOG2E = 1.4426950408889634
ROWS = 32
CHIP = 1024
HALO = 768
FRAMES = 512
HALF = HALO // 2
EDGE = CHIP - HALO
WIDTH = D // 2
SKIPS = 4
SKIP_COLS = D // SKIPS
FAR = 1e30
MESH = pl.DeviceIdType.MESH
VMEM = pltpu.MemorySpace.VMEM
SMEM = pltpu.MemorySpace.SMEM
HBM = pltpu.MemorySpace.HBM


def norm_forward(value, gain_vec):
    center = value - jnp.mean(value, axis=-1, keepdims=True)
    spread = jnp.mean(center * center, axis=-1, keepdims=True)
    inverse = lax.rsqrt(spread + epsilon)
    unit = center * inverse
    return (unit, inverse, unit * gain_vec)


def norm_backward(upstream, unit, inverse, gain_vec):
    scaled = upstream * gain_vec
    gain_grad = jnp.sum(upstream * unit, axis=tuple(range(upstream.ndim - 1)))
    inner = (
        scaled
        - jnp.mean(scaled, axis=-1, keepdims=True)
        - unit * jnp.mean(scaled * unit, axis=-1, keepdims=True)
    )
    return (inverse * inner, gain_grad)


def gelu_exact(value):
    return jax.nn.gelu(value, approximate=False)


def mm(equation, left, right):
    return jnp.einsum(equation, left, right, preferred_element_type=F32)


def dot(left, right):
    return jnp.dot(left, right, preferred_element_type=F32)


def dot_nt(left, right):
    return lax.dot_general(left, right, (((1,), (1,)), ((), ())), preferred_element_type=F32)


def dot_tn(left, right):
    return lax.dot_general(left, right, (((0,), (0,)), ((), ())), preferred_element_type=F32)


class Links:
    def __init__(self, sends, recvs):
        row, col = lax.axis_index("rows"), lax.axis_index("seq")
        self.z, self.x, self.y, self.c = row // 2, row % 2, col // 2, col % 2
        z, x, y, c = self.z, self.x, self.y, self.c
        self.high, self.low = z // 2, z % 2
        self.core = (row, y * 2 + 1 - c)
        self.over_y = (row, (1 - y) * 2 + c)
        self.over_x = (z * 2 + 1 - x, col)
        self.over_low = ((self.high * 2 + 1 - self.low) * 2 + x, col)
        self.over_high = (((1 - self.high) * 2 + self.low) * 2 + x, col)
        self.sends, self.recvs, self.count, self.started = sends, recvs, 0, []

    def greet(self, near=False):
        barrier = pltpu.get_barrier_semaphore()
        peers = [self.core, self.over_y] if near else [self.core, self.over_y, self.over_x, self.over_low, self.over_high]
        for peer in peers:
            pl.semaphore_signal(barrier, inc=1, device_id=peer, device_id_type=MESH)
        pl.semaphore_wait(barrier, len(peers))

    def reserve(self, number):
        self.count += number
        return self.count - number

    def copy(self, src, dst, at, peer):
        return pltpu.make_async_remote_copy(
            src, dst, self.sends.at[at], self.recvs.at[at], device_id=peer, device_id_type=MESH
        )

    def send(self, src, dst, peer):
        copy = self.copy(src, dst, self.reserve(1), peer)
        copy.start()
        self.started.append(copy)
        return copy

    def drain(self):
        assert self.count <= self.sends.shape[0]
        for copy in self.started:
            copy.wait_send()


def head_columns(wqkv, part, core):
    return wqkv.at[:, pl.ds(pl.multiple_of(D * part + WIDTH * core, WIDTH), WIDTH)]


def front_kernel(*refs):
    first_in, second_in, wskip_in, gain, wqkv_in = refs[:5]
    outs = refs[5:10]
    first, second, wskip, wq, wkv, o_stem, o_seen, o_q, o_kv, o_joint, loads, stores, sends, recvs = refs[10:]
    storing = []

    def store(k, *at):
        src, dst = (o_stem, o_seen, o_q, o_kv, o_joint)[k].at[*at], outs[k].at[*at]
        copy = pltpu.make_async_copy(src, dst, stores.at[len(storing)])
        copy.start()
        storing.append(copy)

    links = Links(sends, recvs)
    y, c = links.y, links.c
    loading = []

    def load(src, dst):
        copy = pltpu.make_async_copy(src, dst, loads.at[len(loading)])
        copy.start()
        loading.append(copy)
        return copy

    got = [load(first_in, first), load(second_in, second), load(wskip_in, wskip)]
    got_wkv = [
        load(head_columns(wqkv_in, 1 + i, c), wkv.at[:, pl.ds(WIDTH * i, WIDTH)]) for i in (0, 1)
    ]
    got_wq = load(head_columns(wqkv_in, 0, c), wq)
    links.greet(near=True)
    for copy in got:
        copy.wait()
    gains = gain[0:1, :]
    base = jnp.where(y == 0, EDGE, 0) + HALF * c

    def piece(i, chip):
        return 128 * jnp.where(chip == 0, i, 2 - i)

    def send_piece(i):
        at = lax.rem(base + piece(i, y) + FRAMES * c, CHIP)
        there = CHIP + HALF * c + piece(i, y)
        src = o_seen.at[pl.ds(pl.multiple_of(at, 128), 128)]
        dst = o_seen.at[pl.ds(pl.multiple_of(there, 128), 128)]
        return links.send(src, dst, links.over_y)

    pieces, across = [], []
    for turn in range(2):
        at = pl.multiple_of(256 * (1 - c if turn == 0 else c), 256)
        rows = pl.ds(at, 256)
        value = dot(first[rows, :], wskip[:D, :]) + dot(second[rows, :], wskip[D:, :])
        o_stem[rows, :] = value
        center = value - jnp.mean(value, axis=-1, keepdims=True)
        rate = lax.rsqrt(jnp.mean(center * center, axis=-1, keepdims=True) + epsilon)
        o_seen[rows, :] = (center * rate * gains).astype(BF16)
        pieces.append(send_piece(turn))
        there = o_seen.at[pl.ds(pl.multiple_of(FRAMES + at, 256), 256)]
        across.append(links.send(o_seen.at[rows], there, links.core))
    store(0, pl.ds(0, FRAMES))
    for copy in across:
        copy.wait_recv()
    pieces.append(send_piece(2))
    store(1, pl.ds(0, CHIP))
    for copy in (*got_wkv, got_wq):
        copy.wait()

    def own_part(i, _):
        rows = pl.ds(pl.multiple_of(256 * i, 256), 256)
        o_q[rows, :] = dot(o_seen[rows, :], wq[...]).astype(BF16)
        o_kv[rows, :] = dot(o_seen[rows, :], wkv[...]).astype(BF16)
        return 0

    lax.fori_loop(0, 4, own_part, 0)
    store(2, pl.ds(0, CHIP))
    store(3, pl.ds(0, CHIP))
    o_joint[:D, :] = first[...].T
    forward = []

    def far_part(i, core):
        at = pl.multiple_of(CHIP + HALF * core + piece(i, 1 - y), 128)
        rows = pl.ds(at, 128)
        o_kv[rows, :] = dot(o_seen[rows, :], wkv[...]).astype(BF16)

    for i in range(3):
        pieces[i].wait_recv()
        at = pl.multiple_of(CHIP + HALF * c + piece(i, 1 - y), 128)
        rows = o_seen.at[pl.ds(at, 128)]
        forward.append(links.send(rows, rows, links.core))
        if i == 0:
            o_joint[D:, :] = second[...].T
            store(4, pl.ds(0, 2 * D))
        far_part(i, c)
        if i > 0:
            forward[i - 1].wait_recv()
            far_part(i - 1, 1 - c)
    forward[2].wait_recv()
    store(1, pl.ds(CHIP, HALO))
    far_part(2, 1 - c)
    store(3, pl.ds(CHIP, HALO))
    links.drain()
    for copy in storing:
        copy.wait()


def front(first, second, wskip, gain, wqkv):
    hbm, vm = pl.BlockSpec(memory_space=HBM), pl.BlockSpec(memory_space=VMEM)
    low = lambda *shape: pltpu.VMEM(shape, BF16)
    return pl.pallas_call(
        front_kernel,
        out_shape=[
            jax.ShapeDtypeStruct((FRAMES, D), F32),
            jax.ShapeDtypeStruct((CHIP + HALO, D), BF16),
            jax.ShapeDtypeStruct((CHIP, WIDTH), BF16),
            jax.ShapeDtypeStruct((CHIP + HALO, 2 * WIDTH), BF16),
            jax.ShapeDtypeStruct((2 * D, FRAMES), BF16),
        ],
        in_specs=[hbm] * 3 + [vm, hbm],
        out_specs=[hbm] * 5,
        scratch_shapes=[
            low(FRAMES, D),
            low(FRAMES, D),
            low(2 * D, D),
            low(D, WIDTH),
            low(D, 2 * WIDTH),
            pltpu.VMEM((FRAMES, D), F32),
            low(CHIP + HALO, D),
            low(CHIP, WIDTH),
            low(CHIP + HALO, 2 * WIDTH),
            low(2 * D, FRAMES),
            pltpu.SemaphoreType.DMA((6,)),
            pltpu.SemaphoreType.DMA((7,)),
            pltpu.SemaphoreType.DMA((8,)),
            pltpu.SemaphoreType.DMA((8,)),
        ],
        name="front",
        cost_estimate=pl.CostEstimate(
            flops=8_000_000_000, bytes_accessed=24_000_000, transcendentals=0
        ),
        compiler_params=pltpu.CompilerParams(
            collective_id=2, has_side_effects=True, vmem_limit_bytes=63 << 20
        ),
    )(first, second, wskip, gain, wqkv)


class Frames:
    def __init__(self, seg_at, seg, valid, key_code, query_seg):
        here = lax.axis_index("seq")
        self.seg_at = seg_at
        self.own, self.other = FRAMES * here, FRAMES * (here + 1 - 2 * (here % 2))
        self.halo = jnp.where(here // 2 == 0, CHIP, CHIP - HALO)
        self.core = here % 2
        places = [(0, FRAMES, self.own), (FRAMES, FRAMES, self.other), (CHIP, HALO, self.halo)]
        for at, count, frame in places:
            span = pl.ds(pl.multiple_of(frame, 256), count)
            code = jnp.where(valid[0:1, span] == 1, seg[0:1, span], -1).astype(F32)
            key_code[pl.ds(at, count), :] = jnp.broadcast_to(code, (128, count)).T
            if at < CHIP:
                query_seg[:, pl.ds(at, count)] = jnp.broadcast_to(
                    seg[0:1, span].astype(F32), (8, count)
                )

    def frame(self, at):
        late = jnp.where(at < CHIP, self.other - FRAMES, self.halo - CHIP)
        return at + jnp.where(at < FRAMES, self.own, late)

    def meet(self, keys_at, keys, queries_at, queries):
        k, q = self.frame(keys_at), self.frame(queries_at)
        return (self.seg_at[0, k] <= self.seg_at[0, q + queries - 1]) & (
            self.seg_at[0, k + keys - 1] >= self.seg_at[0, q]
        )

    def slope(self, h):
        values = [LOG2E * 2.0 ** (-8.0 * (core * H // 2 + h + 1) / H) for core in (0, 1)]
        return jnp.where(self.core == 0, values[0], values[1])


def set_distances(dist, key_at, query_at, key_code, query_seg):
    keys, queries = dist.shape
    rows = lax.broadcasted_iota(jnp.int32, (keys, queries), 0) + key_at
    cols = lax.broadcasted_iota(jnp.int32, (keys, queries), 1) + query_at
    apart = jnp.abs(rows - cols)
    allowed = (key_code == query_seg) | (apart == 0)
    dist[...] = jnp.where(allowed, apart.astype(F32), FAR)


def wide(code, queries):
    return jnp.concatenate([code] * (queries // 128), axis=1) if queries > 128 else code


def both_heads(ref, pair, queries):
    first = ref[pl.ds(128 * pair, HD), queries]
    second = ref[pl.ds(128 * pair + HD, HD), queries]
    blank = jnp.zeros_like(first)
    return jnp.concatenate(
        [
            jnp.concatenate([first, blank], axis=0),
            jnp.concatenate([blank, second], axis=0),
        ],
        axis=1,
    )


def both_slopes(dist, frames, pair):
    value = dist[...]
    return jnp.concatenate(
        [value * frames.slope(2 * pair), value * frames.slope(2 * pair + 1)], axis=1
    )


def attend_kernel(
    bq,
    bk,
    heads,
    seg_at,
    q_in,
    kv_in,
    seg,
    valid,
    o_out,
    o_outt,
    lse,
    q,
    kv,
    out,
    outt,
    loads,
    stores,
    kcode,
    qseg,
    qt,
    vt,
    dist,
    acc,
    top,
    total,
    heads_q,
    scores,
    probs,
):
    width = heads * HD
    pairs = range(heads // 2)
    c1 = LOG2E / math.sqrt(HD)
    keys, values = pl.ds(0, width), pl.ds(width, width)
    got = [
        pltpu.make_async_copy(q_in, q, loads.at[0]),
        pltpu.make_async_copy(kv_in.at[:, values], kv.at[:, values], loads.at[1]),
        pltpu.make_async_copy(kv_in.at[:, keys], kv.at[:, keys], loads.at[2]),
    ]
    for copy in got:
        copy.start()
    frames = Frames(seg_at, seg, valid, kcode, qseg)
    got[0].wait()
    qt[...] = q[...].T
    got[1].wait()
    vt[...] = kv[:, width:].T
    got[2].wait()

    def results(i):
        rows = pl.ds(pl.multiple_of(i * bq, bq), bq)
        return [
            pltpu.make_async_copy(out.at[rows], o_out.at[rows], stores.at[0, i]),
            pltpu.make_async_copy(outt.at[:, rows], o_outt.at[:, rows], stores.at[1, i]),
        ]

    def q_block(i, _):
        queries = pl.ds(pl.multiple_of(i * bq, bq), bq)
        acc[...] = jnp.zeros_like(acc)
        total[...] = jnp.zeros_like(total)
        top[...] = jnp.full_like(top, -3e38)
        for pair in pairs:
            heads_q[pair] = both_heads(qt, pair, queries)

        def k_block(j, _):
            @pl.when(frames.meet(j * bk, bk, i * bq, bq))
            def _():
                ks = pl.ds(pl.multiple_of(j * bk, bk), bk)
                set_distances(
                    dist,
                    frames.frame(j * bk),
                    frames.frame(i * bq),
                    wide(kcode[ks, :], bq),
                    qseg[0:1, queries],
                )
                for pair in pairs:
                    scores[pair] = dot(kv[ks, pl.ds(128 * pair, 128)], heads_q[pair])
                fades = []
                for pair in pairs:
                    line = pl.ds(pair, 1)
                    score = scores[pair] * c1 - both_slopes(dist, frames, pair)
                    was = top[line, :]
                    now = jnp.maximum(was, jnp.max(score, axis=0, keepdims=True))
                    prob = jnp.exp2(score - now)
                    fade = jnp.exp2(was - now)
                    total[line, :] = total[line, :] * fade + jnp.sum(prob, axis=0, keepdims=True)
                    top[line, :] = now
                    probs[pair] = prob.astype(BF16)
                    fades.append(fade)
                for pair in pairs:
                    value = dot(vt[pl.ds(128 * pair, 128), ks], probs[pair])
                    for e in range(2):
                        at, lanes = pl.ds(128 * pair + HD * e, HD), slice(bq * e, bq * (e + 1))
                        acc[at, :] = (
                            acc[at, :] * fades[pair][:, lanes]
                            + value[HD * e : HD * (e + 1), lanes]
                        )

            return 0

        lax.fori_loop(0, kv.shape[0] // bk, k_block, 0)
        for pair in pairs:
            rate = 1.0 / total[pl.ds(pair, 1), :]
            for e in range(2):
                at = pl.ds(128 * pair + HD * e, HD)
                acc[at, :] = acc[at, :] * rate[:, bq * e : bq * (e + 1)]
        lse[:, pl.ds(pl.multiple_of(2 * i * bq, 2 * bq), 2 * bq)] = top[...] + jnp.log2(total[...])
        out[queries, :] = acc[...].T.astype(BF16)
        outt[:, queries] = acc[...].astype(BF16)
        for copy in results(i):
            copy.start()
        return 0

    count = q.shape[0] // bq
    lax.fori_loop(0, count, q_block, 0)

    def settle(i, _):
        for copy in results(i):
            copy.wait()
        return 0

    lax.fori_loop(0, count, settle, 0)


def attend(q, kv, seg, valid, bq, bk, heads):
    frames = q.shape[0]
    vm, sm, hbm = [pl.BlockSpec(memory_space=m) for m in (VMEM, SMEM, HBM)]
    return pl.pallas_call(
        functools.partial(attend_kernel, bq, bk, heads),
        out_shape=(
            jax.ShapeDtypeStruct((frames, heads * HD), BF16),
            jax.ShapeDtypeStruct((heads * HD, frames), BF16),
            jax.ShapeDtypeStruct((heads // 2, 2 * frames), F32),
        ),
        in_specs=[sm, hbm, hbm, vm, vm],
        out_specs=(hbm, hbm, vm),
        scratch_shapes=[
            pltpu.VMEM(q.shape, BF16),
            pltpu.VMEM(kv.shape, BF16),
            pltpu.VMEM((frames, heads * HD), BF16),
            pltpu.VMEM((heads * HD, frames), BF16),
            pltpu.SemaphoreType.DMA((3,)),
            pltpu.SemaphoreType.DMA((2, frames // bq)),
            pltpu.VMEM((kv.shape[0], 128), F32),
            pltpu.VMEM((8, frames), F32),
            pltpu.VMEM((heads * HD, frames), BF16),
            pltpu.VMEM((heads * HD, kv.shape[0]), BF16),
            pltpu.VMEM((bk, bq), F32),
            pltpu.VMEM((heads * HD, bq), F32),
            pltpu.VMEM((heads // 2, 2 * bq), F32),
            pltpu.VMEM((heads // 2, 2 * bq), F32),
            pltpu.VMEM((heads // 2, 2 * HD, 2 * bq), BF16),
            pltpu.VMEM((heads // 2, bk, 2 * bq), F32),
            pltpu.VMEM((heads // 2, bk, 2 * bq), BF16),
        ],
        name="attend",
        cost_estimate=pl.CostEstimate(
            flops=8_000_000_000, bytes_accessed=8_000_000, transcendentals=4_000_000
        ),
        compiler_params=pltpu.CompilerParams(vmem_limit_bytes=63 << 20),
    )(seg, q, kv, seg, valid)


def attend_back_kernel(
    bq,
    bk,
    heads,
    seg_at,
    q_in,
    kv_in,
    grad_in,
    outt_in,
    lse,
    seg,
    valid,
    passed_in,
    o_dq,
    o_dkv,
    o_passed,
    q,
    kv,
    grad,
    outt,
    passed,
    dq,
    dkv,
    loads,
    stores,
    kcode,
    qseg,
    qt,
    kt,
    gradt,
    delta,
    dist,
    dqt,
    sums,
    heads_q,
    heads_g,
    rows_q,
    rows_g,
    scores,
    prob_grads,
    probs,
    score_grads,
):
    width = heads * HD
    pairs = range(heads // 2)
    c1 = LOG2E / math.sqrt(HD)
    scale = 1.0 / math.sqrt(HD)
    lane = lax.broadcasted_iota(jnp.int32, (bq, 128), 1)
    places = [(q_in, q), (grad_in, grad), (outt_in, outt), (kv_in, kv), (passed_in, passed)]
    got = [pltpu.make_async_copy(a, b, loads.at[i]) for i, (a, b) in enumerate(places)]
    for copy in got:
        copy.start()
    sums[...] = jnp.zeros_like(sums)
    frames = Frames(seg_at, seg, valid, kcode, qseg)
    got[0].wait()
    qt[...] = q[...].T
    got[1].wait()
    gradt[...] = grad[...].T
    got[2].wait()
    got[3].wait()
    kt[...] = kv[:, :width].T
    got[4].wait()
    stored = [pltpu.make_async_copy(passed, o_passed, stores.at[0])]
    stored[0].start()

    def dq_copy(i):
        rows = pl.ds(pl.multiple_of(i * bq, bq), bq)
        return pltpu.make_async_copy(dq.at[rows], o_dq.at[rows], stores.at[1 + i])

    def q_block(i, _):
        qs = pl.multiple_of(i * bq, bq)
        queries = pl.ds(qs, bq)
        dqt[...] = jnp.zeros_like(dqt)
        for pair in pairs:
            at = pl.ds(128 * pair, 128)
            heads_q[pair] = both_heads(qt, pair, queries)
            heads_g[pair] = both_heads(gradt, pair, queries)
            product = outt[at, queries].astype(F32) * gradt[at, queries].astype(F32)
            for e in range(2):
                rows = pl.ds(bq * e, bq)
                keep = (lane < HD) if e == 0 else (lane >= HD)
                for to, ref in ((rows_q, q), (rows_g, grad)):
                    value = ref[queries, at]
                    to[pair, rows, :] = jnp.where(keep, value, jnp.zeros_like(value))
                delta[pl.ds(pair, 1), rows] = jnp.sum(
                    product[HD * e : HD * (e + 1)], axis=0, keepdims=True
                )

        def k_block(j, _):
            @pl.when(frames.meet(j * bk, bk, i * bq, bq))
            def _():
                ks = pl.ds(pl.multiple_of(j * bk, bk), bk)
                set_distances(
                    dist,
                    frames.frame(j * bk),
                    frames.frame(i * bq),
                    wide(kcode[ks, :], bq),
                    qseg[0:1, queries],
                )
                for pair in pairs:
                    scores[pair] = dot(kv[ks, pl.ds(128 * pair, 128)], heads_q[pair])
                    prob_grads[pair] = dot(
                        kv[ks, pl.ds(width + 128 * pair, 128)], heads_g[pair]
                    )
                lines = pl.ds(pl.multiple_of(2 * qs, 2 * bq), 2 * bq)
                for pair in pairs:
                    line = pl.ds(pair, 1)
                    prob = jnp.exp2(
                        scores[pair] * c1 - both_slopes(dist, frames, pair) - lse[line, lines]
                    )
                    probs[pair] = prob.astype(BF16)
                    score_grads[pair] = (prob * (prob_grads[pair] - delta[line, :])).astype(BF16)
                for pair in pairs:
                    at = pl.ds(128 * pair, 128)
                    sums[ks, pl.ds(width + 128 * pair, 128)] += dot(probs[pair], rows_g[pair])
                    sums[ks, at] += dot(score_grads[pair], rows_q[pair])
                    value = dot(kt[at, ks], score_grads[pair])
                    for e in range(2):
                        dqt[pl.ds(128 * pair + HD * e, HD), :] += value[
                            HD * e : HD * (e + 1), bq * e : bq * (e + 1)
                        ]

            return 0

        lax.fori_loop(0, kv.shape[0] // bk, k_block, 0)
        dq[pl.ds(qs, bq), :] = (dqt[...] * scale).T.astype(BF16)
        dq_copy(i).start()
        return 0

    count = q.shape[0] // bq
    lax.fori_loop(0, count, q_block, 0)
    parts = [(CHIP, HALO), (0, FRAMES), (FRAMES, FRAMES)]
    for i, (at, rows) in enumerate(parts):
        part = pl.ds(at, rows)
        dkv[part, :width] = (sums[part, :width] * scale).astype(BF16)
        dkv[part, width:] = sums[part, width:].astype(BF16)
        copy = pltpu.make_async_copy(dkv.at[part], o_dkv.at[part], stores.at[1 + count + i])
        copy.start()
        stored.append(copy)
    for copy in [*stored, *[dq_copy(i) for i in range(count)]]:
        copy.wait()


def attend_back(q, kv, grad, outt, lse, seg, valid, passed, bq, bk, heads):
    vm, sm, hbm = [pl.BlockSpec(memory_space=m) for m in (VMEM, SMEM, HBM)]
    return pl.pallas_call(
        functools.partial(attend_back_kernel, bq, bk, heads),
        out_shape=(
            jax.ShapeDtypeStruct(q.shape, BF16),
            jax.ShapeDtypeStruct(kv.shape, BF16),
            jax.ShapeDtypeStruct(passed.shape, passed.dtype),
        ),
        in_specs=[sm] + [hbm] * 4 + [vm] * 3 + [hbm],
        out_specs=(hbm, hbm, hbm),
        scratch_shapes=[
            pltpu.VMEM(q.shape, BF16),
            pltpu.VMEM(kv.shape, BF16),
            pltpu.VMEM(grad.shape, BF16),
            pltpu.VMEM(outt.shape, BF16),
            pltpu.VMEM(passed.shape, passed.dtype),
            pltpu.VMEM(q.shape, BF16),
            pltpu.VMEM(kv.shape, BF16),
            pltpu.SemaphoreType.DMA((5,)),
            pltpu.SemaphoreType.DMA((4 + q.shape[0] // bq,)),
            pltpu.VMEM((kv.shape[0], 128), F32),
            pltpu.VMEM((8, q.shape[0]), F32),
            pltpu.VMEM((heads * HD, q.shape[0]), BF16),
            pltpu.VMEM((heads * HD, kv.shape[0]), BF16),
            pltpu.VMEM((heads * HD, q.shape[0]), BF16),
            pltpu.VMEM((heads // 2, 2 * bq), F32),
            pltpu.VMEM((bk, bq), F32),
            pltpu.VMEM((heads * HD, bq), F32),
            pltpu.VMEM(kv.shape, F32),
            *[pltpu.VMEM((heads // 2, 2 * HD, 2 * bq), BF16)] * 2,
            *[pltpu.VMEM((heads // 2, 2 * bq, 2 * HD), BF16)] * 2,
            *[pltpu.VMEM((heads // 2, bk, 2 * bq), F32)] * 2,
            *[pltpu.VMEM((heads // 2, bk, 2 * bq), BF16)] * 2,
        ],
        name="attend_back",
        cost_estimate=pl.CostEstimate(
            flops=20_000_000_000, bytes_accessed=16_000_000, transcendentals=4_000_000
        ),
        compiler_params=pltpu.CompilerParams(vmem_limit_bytes=63 << 20),
    )(seg, q, kv, grad, outt, lse, seg, valid, passed)


def add_into(value, other):
    def step(i, _):
        value[i] = value[i] + other[i]
        return 0

    lax.fori_loop(0, value.shape[0], step, 0)


class Unit:
    def __init__(self, links, own, came, y_first, done):
        self.links, self.own, self.came, self.y_first, self.done = links, own, came, y_first, done

    def add_core(self, r0):
        for k in range(2):
            for i in range(2):
                for j in range(2):
                    add_into(self.own.at[k, i, j], r0.at[k, i, j])

    def send_first(self):
        n, a = self.links, self.own
        if self.y_first:
            self.first = n.send(a.at[:, :, :, 1 - n.y], self.came[0], n.over_y)
        else:
            self.first = n.send(a.at[:, :, 1 - n.x], self.came[0], n.over_x)

    def turn_first(self):
        self.first.wait_recv()
        n, a, b = self.links, self.own, self.came[0]
        for k in range(2):
            for i in range(2):
                part = a.at[k, i, :, n.y] if self.y_first else a.at[k, i, n.x]
                add_into(part, b.at[k, i])
        if self.y_first:
            self.second = n.send(a.at[:, :, 1 - n.x, n.y], self.came[1], n.over_x)
        else:
            self.second = n.send(a.at[:, :, n.x, 1 - n.y], self.came[1], n.over_y)

    def chip(self, *at):
        return self.own.at[*at, self.links.x, self.links.y]

    def turn_second(self):
        self.second.wait_recv()
        self.after_second()

    def after_second(self):
        n = self.links
        for k in range(2):
            add_into(self.chip(k, slice(None)), self.came[1].at[k])
        self.third = n.send(self.chip(slice(None), 1 - n.low), self.came[2], n.over_low)

    def turn_third(self):
        n = self.links
        self.third.wait_recv()
        add_into(self.chip(slice(None), n.low), self.came[2])
        self.fourth = n.send(self.chip(1 - n.high, n.low), self.came[3], n.over_high)

    def finish(self):
        n = self.links
        self.fourth.wait_recv()
        self.done(self.chip(n.high, n.low)[...].astype(F32) + self.came[3][...].astype(F32))


class LateUnit(Unit):
    def chip(self, *at):
        return self.own.at[*at]

    def turn_second(self, *loads):
        for copy in loads:
            copy.wait()
        self.after_second()


class Small:
    def __init__(self, links, steps, into, done):
        self.links, self.steps, self.into, self.done, self.at = links, steps, into, done, 0
        self.stages = [links.core, links.over_y, links.over_x, links.over_low, links.over_high]

    def send(self):
        self.flying = self.links.send(
            self.steps.at[self.at], self.into.at[self.at], self.stages[self.at]
        )

    def turn(self):
        self.flying.wait_recv()
        value = self.steps[self.at] + self.into[self.at]
        self.at += 1
        if self.at == len(self.stages):
            self.done(value)
        else:
            self.steps[self.at] = value
            self.send()


STEPS = 8
STEP = 256


def middle_kernel(*refs):
    (
        att_in_hbm,
        stem_in,
        wout_in,
        gain,
        up_hbm,
        down_hbm,
        bias_up,
        bias_down,
        cot_in,
    ) = refs[:9]
    o_out, o_grad, o_heads, o_wo, o_down, o_down_away, o_up, o_up_away, o_small = refs[9:18]
    (
        att,
        att_came,
        stem,
        wout,
        ups,
        downs,
        cot,
        second,
        second_t,
        unit,
        inverse,
        active,
        hidden_grad,
        out_sum,
        grad_sum,
        low,
        swap_out,
        swap_in,
        down_send,
        down_keep,
        down_came,
        up_send,
        up_keep,
        up_came,
        loads,
        sends,
        recvs,
    ) = refs[18:]
    links = Links(sends, recvs)
    x, y, c = links.x, links.y, links.c
    loading = []

    def load(src, dst):
        copy = pltpu.make_async_copy(src, dst, loads.at[len(loading)])
        copy.start()
        loading.append(copy)
        return copy

    own, other = pl.ds(0, FRAMES), pl.ds(FRAMES, FRAMES)
    got_att = load(att_in_hbm.at[own], att)
    got_wout = load(wout_in, wout)
    got_stem = load(stem_in, stem)
    got_cot = load(cot_in, cot.at[own])
    got_ups, got_downs = [], []
    for i in range(STEPS):
        for j in range(2):
            at = pl.multiple_of(128 * (4 * i + 2 * j + c), 128)
            part = pl.ds(128 * j, 128)
            got_ups.append(load(up_hbm.at[:, pl.ds(at, 128)], ups.at[i, :, part]))
            got_downs.append(load(down_hbm.at[pl.ds(at, 128), :], downs.at[i, part, :]))
    links.greet()
    att_core = links.send(att_in_hbm.at[other], att_came, links.core)
    cot_core = links.send(cot_in, cot.at[other], links.core)
    mine = pl.ds(pl.multiple_of(WIDTH * c, WIDTH), WIDTH)
    theirs = pl.ds(pl.multiple_of(WIDTH * (1 - c), WIDTH), WIDTH)

    got_att.wait()
    got_wout.wait()
    got_stem.wait()
    att_core.wait_recv()
    gains = gain[0:1, :]
    second_core = []
    for part in range(2):
        rows = pl.ds(256 * part, 256)
        value = stem[rows, :] + dot(att[rows, :], wout[mine, :]) + dot(att_came[rows, :], wout[theirs, :])
        stem[rows, :] = value
        center = value - jnp.mean(value, axis=-1, keepdims=True)
        rate = lax.rsqrt(jnp.mean(center * center, axis=-1, keepdims=True) + epsilon)
        normal = center * rate
        unit[rows, :] = normal
        inverse[rows, :] = jnp.broadcast_to(rate, (256, 128))
        second[rows, :] = (normal * gains).astype(BF16)
        second_core.append(
            links.send(second.at[rows], second.at[pl.ds(FRAMES + 256 * part, 256)], links.core)
        )
    second_t[:, :FRAMES] = second[own, :].T
    out_sum[...] = jnp.zeros_like(out_sum)
    grad_sum[...] = jnp.zeros_like(grad_sum)
    o_small[...] = jnp.zeros_like(o_small)
    for copy in [got_cot, *got_ups, *got_downs]:
        copy.wait()
    cot_core.wait_recv()
    for copy in second_core:
        copy.wait_recv()
    second_t[:, FRAMES:] = second[other, :].T

    down_at, up_at = links.reserve(STEPS), links.reserve(STEPS)

    def down_copy(i):
        return links.copy(down_send.at[i], down_came.at[i], down_at + i, links.over_y)

    def up_copy(i):
        return links.copy(up_send.at[i], up_came.at[i], up_at + i, links.over_x)

    def feed_step(i, _):
        up, down = ups[i], downs[i]
        bias = bias_up[0:1, pl.ds(pl.multiple_of(STEP * i, STEP), STEP)]
        total = jnp.zeros((1, STEP), F32)
        for half in (own, other):
            hidden = dot(second[half, :], up) + bias
            active_grad = dot_nt(cot[half, :], down)
            share = 0.5 + 0.5 * lax.erf(hidden * math.sqrt(0.5))
            slope = share + hidden * (
                jnp.exp(-0.5 * hidden * hidden) * (1.0 / math.sqrt(2.0 * math.pi))
            )
            a = (hidden * share).astype(BF16)
            g = (active_grad * slope).astype(BF16)
            active[half, :] = a
            hidden_grad[half, :] = g
            total = total + jnp.sum(g.astype(F32), axis=0, keepdims=True)
            out_sum[half, :] += dot(a, down)
            grad_sum[half, :] += dot_nt(g, up)
        for j in range(2):
            o_small[pl.ds(4 * i + 2 * j + c, 1), :] = total[:, 128 * j : 128 * (j + 1)]
        value = dot_tn(active[...], cot[...]).astype(BF16)
        down_send[i] = jnp.where(y == 0, value[128:], value[:128])
        down_keep[i] = jnp.where(y == 0, value[:128], value[128:])
        down_copy(i).start()
        value = dot(second_t[...], hidden_grad[...]).astype(BF16)
        for k in range(4):
            first, last = value[256 * k : 256 * k + 128], value[256 * k + 128 : 256 * (k + 1)]
            up_send[i, k] = jnp.where(x == 0, last, first)
            up_keep[i, k] = jnp.where(x == 0, first, last)
        up_copy(i).start()
        return 0

    lax.fori_loop(0, STEPS, feed_step, 0)

    swap_out[0] = grad_sum[other, :].astype(BF16)
    grad_core = links.send(swap_out.at[0], swap_in.at[0], links.core)
    swap_out[1] = out_sum[other, :].astype(BF16)
    out_core = links.send(swap_out.at[1], swap_in.at[1], links.core)
    grad_core.wait_recv()

    def norm_rows(i, totals):
        rows = pl.ds(pl.multiple_of(128 * i, 128), 128)
        upstream = grad_sum[rows, :] + swap_in[0, rows, :].astype(F32)
        normal = unit[rows, :]
        scaled = upstream * gains
        inner = (
            scaled
            - jnp.mean(scaled, axis=-1, keepdims=True)
            - normal * jnp.mean(scaled * normal, axis=-1, keepdims=True)
        )
        value = cot[rows, :].astype(F32)
        grad = value + inverse[rows, 0:1] * inner
        o_grad[rows, :] = grad
        low[rows, :] = grad.astype(BF16)
        return (
            totals[0] + jnp.sum(upstream * normal, axis=0, keepdims=True),
            totals[1] + jnp.sum(value, axis=0, keepdims=True),
        )

    zero = jnp.zeros((1, D), F32)
    totals = lax.fori_loop(0, 4, norm_rows, (zero, zero))
    for k, value in enumerate(totals):
        for j in range(8):
            o_small[pl.ds(32 + 8 * k + j, 1), :] = value[:, 128 * j : 128 * (j + 1)]
    swap_out[2, :, :WIDTH] = dot_nt(low[...], wout[theirs, :]).astype(BF16)
    heads_core = links.send(
        swap_out.at[2, :, pl.ds(0, WIDTH)], swap_in.at[2, :, pl.ds(0, WIDTH)], links.core
    )
    o_heads[own, :] = dot_nt(low[...], wout[mine, :]).astype(BF16)
    o_wo[mine, :] = dot_tn(att[...], low[...]).astype(BF16)
    o_wo[theirs, :] = dot_tn(att_came[...], low[...]).astype(BF16)
    out_core.wait_recv()

    def out_rows(i, _):
        rows = pl.ds(pl.multiple_of(128 * i, 128), 128)
        o_out[rows, :] = (
            stem[rows, :]
            + (out_sum[rows, :] + swap_in[1, rows, :].astype(F32))
            + bias_down[0:1, :]
        ).astype(BF16)
        return 0

    lax.fori_loop(0, 4, out_rows, 0)
    heads_core.wait_recv()
    o_heads[other, :] = swap_in[2, :, :WIDTH]

    def add_step(i, _):
        down_copy(i).wait()
        value = down_keep[i] + down_came[i]
        stays = lax.rem(i + x, 2) == 0

        @pl.when(stays)
        def _():
            o_down[i // 2] = value

        @pl.when(jnp.logical_not(stays))
        def _():
            o_down_away[i // 2] = value

        up_copy(i).wait()
        columns = pl.ds(pl.multiple_of(STEP * i, STEP), STEP)
        for k in range(4):
            value = up_keep[i, k] + up_came[i, k]
            o_up[k, :, columns] = jnp.where(y == 0, value[:64], value[64:])
            o_up_away[k, :, columns] = jnp.where(y == 0, value[64:], value[:64])
        return 0

    lax.fori_loop(0, STEPS, add_step, 0)
    links.drain()


def middle(att, stem, wout, gain, w_up, w_down, bias_up, bias_down, cot):
    hbm, vm = pl.BlockSpec(memory_space=HBM), pl.BlockSpec(memory_space=VMEM)
    low = lambda *shape: pltpu.VMEM(shape, BF16)
    full = lambda *shape: pltpu.VMEM(shape, F32)
    copies = 24
    return pl.pallas_call(
        middle_kernel,
        out_shape=[
            jax.ShapeDtypeStruct((FRAMES, D), BF16),
            jax.ShapeDtypeStruct((FRAMES, D), F32),
            jax.ShapeDtypeStruct((CHIP, WIDTH), BF16),
            jax.ShapeDtypeStruct((D, D), BF16),
            *[jax.ShapeDtypeStruct((4, 128, D), BF16)] * 2,
            *[jax.ShapeDtypeStruct((4, 64, 2 * D), BF16)] * 2,
            jax.ShapeDtypeStruct((48, 128), F32),
        ],
        in_specs=[hbm] * 3 + [vm] + [hbm] * 2 + [vm] * 2 + [hbm],
        out_specs=[vm] * 9,
        scratch_shapes=[
            low(FRAMES, WIDTH),
            low(FRAMES, WIDTH),
            full(FRAMES, D),
            low(D, D),
            low(STEPS, D, STEP),
            low(STEPS, STEP, D),
            low(CHIP, D),
            low(CHIP, D),
            low(D, CHIP),
            full(FRAMES, D),
            full(FRAMES, 128),
            low(CHIP, STEP),
            low(CHIP, STEP),
            full(CHIP, D),
            full(CHIP, D),
            low(FRAMES, D),
            low(3, FRAMES, D),
            low(3, FRAMES, D),
            low(STEPS, 128, D),
            low(STEPS, 128, D),
            low(STEPS, 128, D),
            low(STEPS, 4, 128, STEP),
            low(STEPS, 4, 128, STEP),
            low(STEPS, 4, 128, STEP),
            pltpu.SemaphoreType.DMA((4 + 4 * STEPS,)),
            pltpu.SemaphoreType.DMA((copies,)),
            pltpu.SemaphoreType.DMA((copies,)),
        ],
        name="middle",
        cost_estimate=pl.CostEstimate(
            flops=28_000_000_000, bytes_accessed=40_000_000, transcendentals=4_000_000
        ),
        compiler_params=pltpu.CompilerParams(
            collective_id=1, has_side_effects=True, vmem_limit_bytes=63 << 20
        ),
    )(att, stem, wout, gain, w_up, w_down, bias_up, bias_down, cot)


def tail_kernel(*refs):
    (
        down_in,
        down_came,
        up_in,
        up_came,
        wo_in,
        small_in,
        dq_in,
        dkv_in,
        seen_in,
        wqkv_in,
        joint_in,
        stem_in,
        grad_in,
        gain,
        wskip_in,
    ) = refs[:15]
    o_in, o_skip, o_down, o_up, o_qkv, o_wo, o_wskip, o_small, o_gain = refs[15:24]
    (
        dq,
        dkv,
        wide_buf,
        wq,
        wkv,
        joint,
        stem,
        grad,
        chip_out,
        chip_in,
        chip_own,
        halo_out,
        halo_in,
        halo_sum,
        halo,
        low,
        down_own,
        down_r2,
        down_r3,
        down_r4,
        up_own,
        up_r2,
        up_r3,
        up_r4,
        up_out,
        up_in_last,
        unit_own,
        unit_r1,
        unit_r2,
        unit_r3,
        unit_r4,
        wo_r0,
        join_out,
        skip_own,
        skip_out,
        skip_r0,
        skip_r1,
        skip_r2,
        skip_r3,
        skip_r4,
        small_steps,
        small_into,
        gain_steps,
        gain_into,
        loads,
        sends,
        recvs,
    ) = refs[24:]
    links = Links(sends, recvs)
    y, c = links.y, links.c
    loading = []

    def load(src, dst):
        copy = pltpu.make_async_copy(src, dst, loads.at[len(loading)])
        copy.start()
        loading.append(copy)
        return copy

    seen = wide_buf.at[pl.ds(0, CHIP + HALO)]
    far, near = pl.ds(CHIP, HALO), pl.ds(0, CHIP)
    got_wkv = [load(head_columns(wqkv_in, 1 + i, c), wkv.at[:, pl.ds(WIDTH * i, WIDTH)]) for i in (0, 1)]
    got_far = load(dkv_in.at[far], dkv.at[far])
    links.greet()
    wo_core = links.send(wo_in.at[:, :, :, :, 1 - c], wo_r0, links.core)
    got_dq = load(dq_in, dq)
    got_near = load(dkv_in.at[near], dkv.at[near])
    got_seen = load(seen_in, seen)
    got_wo = load(wo_in.at[:, :, :, :, c], unit_own.at[0])
    got_small = load(small_in, small_steps.at[0])
    got_down = [
        [
            load(down_in.at[:, :, pl.ds(64 * i, 64)], down_own.at[i]),
            load(down_came.at[:, :, pl.ds(64 * i, 64)], down_r2.at[i]),
        ]
        for i in range(2)
    ]
    got_up = []
    for i, core in enumerate((1 - c, c)):
        rows = pl.ds(pl.multiple_of(32 * core, 32), 32)
        got_up.append(
            [
                load(up_in.at[:, :, rows], up_own.at[i]),
                load(up_came.at[:, :, rows], up_r2.at[i]),
            ]
        )
    got_wq = load(head_columns(wqkv_in, 0, c), wq)
    got_stem = load(stem_in, stem)
    got_grad = load(grad_in, grad)
    got_joint = load(joint_in, joint)
    halo[pl.ds(0, EDGE), :] = jnp.zeros((EDGE, D), BF16)
    halo[pl.ds(EDGE + HALO, EDGE), :] = jnp.zeros((EDGE, D), BF16)

    def to_down(i):
        def done(value):
            o_down[pl.ds(64 * i, 64), :] = value

        return done

    def to_up_other(value):
        up_out[...] = value
        up_last.append(links.send(up_out, up_in_last, links.core))

    def to_up_mine(value):
        for b in range(16):
            at = pl.multiple_of(256 * b + 128 * c, 128)
            o_up[:, pl.ds(at, 128)] = value[:, 128 * b : 128 * (b + 1)]

    up_last = []
    downs = [
        LateUnit(
            links,
            down_own.at[i],
            (None, down_r2.at[i], down_r3.at[i], down_r4.at[i]),
            True,
            to_down(i),
        )
        for i in range(2)
    ]
    ups = [
        LateUnit(
            links, up_own.at[i], (None, up_r2.at[i], up_r3.at[i], up_r4.at[i]), False, done
        )
        for i, done in enumerate((to_up_other, to_up_mine))
    ]

    def to_wo(value):
        o_wo[...] = value

    def to_qkv(i):
        def done(value):
            o_qkv[:, pl.ds(D * i, D)] = value

        return done

    def to_wskip(q, half):
        def done(value):
            o_wskip[pl.ds(ROWS * half, ROWS), pl.ds(SKIP_COLS * q, SKIP_COLS)] = value

        return done

    def unit(k, y_first, done):
        came = (unit_r1.at[k], unit_r2.at[k], unit_r3.at[k], unit_r4.at[k])
        return Unit(links, unit_own.at[k], came, y_first, done)

    wo = unit(0, False, to_wo)
    unit_q, unit_k, unit_v = [unit(1 + i, i == 1, to_qkv(i)) for i in range(3)]

    def skip_unit(k, y_first, done):
        came = (skip_r1.at[k], skip_r2.at[k], skip_r3.at[k], skip_r4.at[k])
        return Unit(links, skip_own.at[k], came, y_first, done)

    skips = [
        [skip_unit(2 * q + half, half == 0, to_wskip(q, half)) for half in range(2)]
        for q in range(SKIPS)
    ]

    def to_small(value):
        o_small[...] = value

    def to_gain(value):
        o_gain[...] = value

    small = Small(links, small_steps, small_into, to_small)
    gain_sum = Small(links, gain_steps, gain_into, to_gain)

    for copy in (*got_wkv, got_far):
        copy.wait()

    def halo_part(core):
        at = pl.multiple_of(CHIP + HALF * core, 128)
        return dot_nt(dkv[pl.ds(at, HALF), :], wkv[...])

    halo_out[...] = halo_part(1 - c).astype(BF16)
    halo_core = links.send(halo_out, halo_in, links.core)
    mine = halo_part(c)
    halo_core.wait_recv()
    halo_sum[...] = (mine + halo_in[...].astype(F32)).astype(BF16)
    part_at = pl.ds(pl.multiple_of(EDGE + HALF * c, 128), HALF)
    part = halo.at[part_at]
    halo_y = links.send(halo_sum, part, links.over_y)
    got_near.wait()
    got_seen.wait()
    columns = pl.ds(pl.multiple_of(WIDTH * c, WIDTH), WIDTH)

    def place(k, i, value):
        value = value.astype(BF16)
        for j in range(2):
            for m in range(2):
                at = 128 * j + 64 * m
                first, second = value[at : at + 32], value[at + 32 : at + 64]
                mine, theirs = jnp.where(c == 0, first, second), jnp.where(c == 0, second, first)
                unit_own[1 + k, i // 2, i % 2, j, m, :, columns] = mine
                join_out[k, i // 2, i % 2, j, m] = theirs

    def join(k):
        there = unit_own.at[1 + k, :, :, :, :, :, columns]
        return links.send(join_out.at[k], there, links.core)

    def kv_rows(i, _):
        value = dot(seen[:, pl.ds(pl.multiple_of(256 * i, 256), 256)].T, dkv[...])
        place(1, i, value[:, :WIDTH])
        place(2, i, value[:, WIDTH:])
        return 0

    def q_rows(i, _):
        place(0, i, dot(seen[near, pl.ds(pl.multiple_of(256 * i, 256), 256)].T, dq[...]))
        return 0

    got_wo.wait()
    wo_core.wait_recv()
    wo.add_core(wo_r0)
    wo.send_first()
    lax.fori_loop(0, 4, kv_rows, 0)
    join_v, join_k = join(2), join(1)
    for one, got in zip(downs + ups, got_down + got_up):
        one.turn_second(*got)
    got_small.wait()
    small.send()
    join_v.wait_recv()
    unit_v.send_first()
    join_k.wait_recv()
    unit_k.send_first()
    got_dq.wait()
    lax.fori_loop(0, 4, q_rows, 0)
    join_q = join(0)
    got_wskip = load(wskip_in, wide_buf)
    wo.turn_first()
    join_q.wait_recv()
    unit_q.send_first()

    got_wq.wait()

    def chip_part(at):
        rows = pl.ds(at, 256)
        return dot_nt(dq[rows, :], wq[...]) + dot_nt(dkv[rows, :], wkv[...])

    def other_frames(i, _):
        at = pl.multiple_of(256 * i, 256)
        chip_out[pl.ds(at, 256), :] = chip_part(FRAMES + at).astype(BF16)
        return 0

    lax.fori_loop(0, 2, other_frames, 0)
    chip_core = links.send(chip_out, chip_in, links.core)
    small.turn()

    def own_frames(i, _):
        at = pl.multiple_of(256 * i, 256)
        chip_own[pl.ds(at, 256), :] = chip_part(at)
        return 0

    lax.fori_loop(0, 2, own_frames, 0)
    for one in downs:
        one.turn_third()

    halo_y.wait_recv()
    halo_rest = links.send(part, part, links.core)
    chip_core.wait_recv()
    got_stem.wait()
    got_grad.wait()
    halo_rest.wait_recv()
    gains = gain[0:1, :]

    def norm_rows(i, total):
        at = pl.multiple_of(128 * i, 128)
        rows = pl.ds(at, 128)
        upstream = (
            chip_own[rows, :]
            + chip_in[rows, :].astype(F32)
            + halo[pl.ds(pl.multiple_of(at + 256 * (2 * c + y), 128), 128), :].astype(F32)
        )
        value = stem[rows, :]
        center = value - jnp.mean(value, axis=-1, keepdims=True)
        inverse = lax.rsqrt(jnp.mean(center * center, axis=-1, keepdims=True) + epsilon)
        unit_value = center * inverse
        scaled = upstream * gains
        inner = (
            scaled
            - jnp.mean(scaled, axis=-1, keepdims=True)
            - unit_value * jnp.mean(scaled * unit_value, axis=-1, keepdims=True)
        )
        low[rows, :] = (grad[rows, :] + inverse * inner).astype(BF16)
        return total + jnp.sum(upstream * unit_value, axis=0, keepdims=True)

    total = lax.fori_loop(0, 4, norm_rows, jnp.zeros((1, D), F32))
    gain_steps[0] = jnp.concatenate([total[:, 128 * i : 128 * (i + 1)] for i in range(8)], axis=0)
    gain_sum.send()
    got_joint.wait()

    skip_core = []
    for q in range(SKIPS):

        def skip_rows(i, _, q=q):
            value = dot(
                joint[pl.ds(pl.multiple_of(512 * i, 512), 512), :],
                low[:, SKIP_COLS * q : SKIP_COLS * (q + 1)],
            ).astype(BF16)
            for j in range(2):
                for m in range(2):
                    for half in range(2):
                        at = 256 * j + 128 * m + 32 * half
                        first, second = value[at : at + 32], value[at + 64 : at + 96]
                        skip_own[2 * q + half, i // 2, i % 2, j, m] = jnp.where(c == 0, first, second)
                        skip_out[2 * q + half, i // 2, i % 2, j, m] = jnp.where(c == 0, second, first)
            return 0

        lax.fori_loop(0, 4, skip_rows, 0)
        both = pl.ds(2 * q, 2)
        skip_core.append(links.send(skip_out.at[both], skip_r0.at[both], links.core))
        if q > 0:
            skip_core[q - 1].wait_recv()
            for half in range(2):
                skips[q - 1][half].add_core(skip_r0.at[2 * (q - 1) + half])
                skips[q - 1][half].send_first()
    q = SKIPS - 1
    skip_core[q].wait_recv()
    for half in range(2):
        skips[q][half].add_core(skip_r0.at[2 * q + half])
        skips[q][half].send_first()

    got_wskip.wait()

    def joined_part(i):
        value = dot_nt(low[...], wide_buf[pl.ds(256 * i, 256), :]).astype(BF16)
        out = o_in if i < 4 else o_skip
        out[:, pl.ds(256 * (i % 4), 256)] = value

    unit_v.turn_first()
    joined_part(0)
    for one in ups:
        one.turn_third()
    joined_part(1)
    joined_part(2)
    gain_sum.turn()
    small.turn()
    joined_part(3)
    unit_q.turn_first()
    unit_k.turn_first()
    joined_part(4)
    gain_sum.turn()
    small.turn()
    wo.turn_second()
    joined_part(5)
    joined_part(6)
    for one in downs:
        one.finish()
    joined_part(7)
    gain_sum.turn()
    small.turn()
    for one in ups:
        one.finish()
    for q in range(SKIPS):
        skips[q][1].turn_first()
    unit_v.turn_second()
    gain_sum.turn()
    small.turn()
    wo.turn_third()
    unit_q.turn_second()
    for q in range(SKIPS):
        skips[q][0].turn_first()
    unit_k.turn_second()
    unit_v.turn_third()
    up_last[0].wait_recv()
    for b in range(16):
        at = pl.multiple_of(256 * b + 128 * (1 - c), 128)
        o_up[:, pl.ds(at, 128)] = up_in_last[:, 128 * b : 128 * (b + 1)]
    gain_sum.turn()
    wo.finish()
    unit_q.turn_third()
    for q in range(SKIPS):
        skips[q][1].turn_second()
    unit_v.finish()
    unit_k.turn_third()
    for q in range(SKIPS):
        skips[q][0].turn_second()
    unit_q.finish()
    for q in range(SKIPS):
        skips[q][1].turn_third()
    unit_k.finish()
    for q in range(SKIPS):
        skips[q][0].turn_third()
    for q in range(SKIPS):
        skips[q][1].finish()
    for q in range(SKIPS):
        skips[q][0].finish()
    links.drain()


def tail(down, down_came, up, up_came, wo, small, dq, dkv, seen, wqkv, joint, stem, grad, gain, wskip):
    hbm, vm = pl.BlockSpec(memory_space=HBM), pl.BlockSpec(memory_space=VMEM)
    n_small = small.shape[0]
    out_shape = [
        jax.ShapeDtypeStruct((FRAMES, D), BF16),
        jax.ShapeDtypeStruct((FRAMES, D), BF16),
        jax.ShapeDtypeStruct((128, D), F32),
        jax.ShapeDtypeStruct((32, 4096), F32),
        jax.ShapeDtypeStruct((32, 3 * D), F32),
        jax.ShapeDtypeStruct((32, D), F32),
        jax.ShapeDtypeStruct((64, D), F32),
        jax.ShapeDtypeStruct((n_small, 128), F32),
        jax.ShapeDtypeStruct((8, 128), F32),
    ]
    low = lambda *shape: pltpu.VMEM(shape, BF16)
    full = lambda *shape: pltpu.VMEM(shape, F32)
    skip = (ROWS, SKIP_COLS)
    copies = 104
    scratch = [
        low(CHIP, WIDTH),
        low(CHIP + HALO, D),
        low(2 * D, D),
        low(D, WIDTH),
        low(D, D),
        low(2 * D, FRAMES),
        full(FRAMES, D),
        full(FRAMES, D),
        low(FRAMES, D),
        low(FRAMES, D),
        full(FRAMES, D),
        low(HALF, D),
        low(HALF, D),
        low(HALF, D),
        low(HALO + 2 * EDGE, D),
        low(FRAMES, D),
        low(2, 2, 2, 64, D),
        low(2, 2, 2, 64, D),
        low(2, 2, 64, D),
        low(2, 64, D),
        low(2, 2, 2, 32, 2 * D),
        low(2, 2, 2, 32, 2 * D),
        low(2, 2, 32, 2 * D),
        low(2, 32, 2 * D),
        full(32, 2 * D),
        full(32, 2 * D),
        low(4, 2, 2, 2, 2, ROWS, D),
        low(4, 2, 2, 2, ROWS, D),
        low(4, 2, 2, ROWS, D),
        low(4, 2, ROWS, D),
        low(4, ROWS, D),
        low(2, 2, 2, 2, ROWS, D),
        low(3, 2, 2, 2, 2, ROWS, WIDTH),
        low(2 * SKIPS, 2, 2, 2, 2, *skip),
        low(2 * SKIPS, 2, 2, 2, 2, *skip),
        low(2 * SKIPS, 2, 2, 2, 2, *skip),
        low(2 * SKIPS, 2, 2, 2, *skip),
        low(2 * SKIPS, 2, 2, *skip),
        low(2 * SKIPS, 2, *skip),
        low(2 * SKIPS, *skip),
        full(5, n_small, 128),
        full(5, n_small, 128),
        full(5, 8, 128),
        full(5, 8, 128),
        pltpu.SemaphoreType.DMA((24,)),
        pltpu.SemaphoreType.DMA((copies,)),
        pltpu.SemaphoreType.DMA((copies,)),
    ]
    return pl.pallas_call(
        tail_kernel,
        out_shape=out_shape,
        in_specs=[hbm] * 13 + [vm, hbm],
        out_specs=[vm] * 9,
        scratch_shapes=scratch,
        name="tail",
        cost_estimate=pl.CostEstimate(
            flops=17_000_000_000, bytes_accessed=60_000_000, transcendentals=0
        ),
        compiler_params=pltpu.CompilerParams(
            collective_id=0, has_side_effects=True, vmem_limit_bytes=63 << 20
        ),
    )(
        down.reshape(2, 2, 128, D),
        down_came.reshape(2, 2, 128, D),
        up.reshape(2, 2, 64, 2 * D),
        up_came.reshape(2, 2, 64, 2 * D),
        wo.reshape(2, 2, 2, 2, 2, 32, D),
        small,
        dq,
        dkv,
        seen,
        wqkv,
        joint,
        stem,
        grad,
        gain,
        wskip,
    )


def finish_kernel(count, *refs):
    ins, small, gain = refs[:count], refs[count], refs[count + 1]
    outs, o_small = refs[count + 2 : 2 * count + 2], refs[2 * count + 2]
    held, loads, stores = refs[2 * count + 3 : 3 * count + 3], refs[-2], refs[-1]
    got = [pltpu.make_async_copy(a, b, loads.at[i]) for i, (a, b) in enumerate(zip(ins, held))]
    for copy in got:
        copy.start()
    device = lax.axis_index("rows") * 4 + lax.axis_index("seq")
    o_small[0:1, :] = small[pl.ds(device, 1), :]
    row, lane = device // 4, lax.rem(device, 4) * 32
    values = [gain[pl.ds(row, 1), :], small[pl.ds(32 + row, 1), :], small[pl.ds(40 + row, 1), :]]
    for i, value in enumerate(values):
        o_small[1 + i : 2 + i, :] = pltpu.roll(value, lax.rem(128 - lane, 128), 1)
    put = [pltpu.make_async_copy(a, b, stores.at[i]) for i, (a, b) in enumerate(zip(held, outs))]
    for copy, after in zip(got, put):
        copy.wait()
        after.start()
    for copy in put:
        copy.wait()


def finish(results, small, gain):
    hbm, vm = pl.BlockSpec(memory_space=HBM), pl.BlockSpec(memory_space=VMEM)
    count = len(results)
    return pl.pallas_call(
        functools.partial(finish_kernel, count),
        out_shape=[
            *[jax.ShapeDtypeStruct(a.shape, a.dtype) for a in results],
            jax.ShapeDtypeStruct((8, 128), F32),
        ],
        in_specs=[hbm] * count + [vm] * 2,
        out_specs=[hbm] * count + [vm],
        scratch_shapes=[
            *[pltpu.VMEM(a.shape, a.dtype) for a in results],
            pltpu.SemaphoreType.DMA((count,)),
            pltpu.SemaphoreType.DMA((count,)),
        ],
        name="finish",
        compiler_params=pltpu.CompilerParams(vmem_limit_bytes=63 << 20),
    )(*results, small, gain)


def swap_x(value):
    return lax.ppermute(value, "rows", [(r, r ^ 1) for r in range(8)])


def swap_chip(value):
    return lax.ppermute(value, "seq", [(i, i ^ 2) for i in range(4)])


def body_chips(
    inputs,
    skip_feats,
    seg_ids,
    frame_valid,
    w_skip,
    gain_one,
    w_qkv,
    w_out,
    gain_two,
    w_up,
    b_up,
    w_down,
    b_down,
    cotangent,
):
    here = lax.axis_index("seq")
    c = here % 2
    heads = H // 2
    first, second_in, cot = inputs[0], skip_feats[0], cotangent[0]
    gain_first = jnp.broadcast_to(gain_one.astype(F32), (8, D))
    gain_second = jnp.broadcast_to(gain_two.astype(F32), (8, D))
    stem_out, normed_seen, q, kv, joint = front(first, second_in, w_skip, gain_first, w_qkv)
    attended, attended_t, lse = attend(q, kv, seg_ids, frame_valid, 128, 256, heads)
    bias = lax.dynamic_index_in_dim(b_up.astype(F32).reshape(16, 2, 128), c, 1, keepdims=False)
    output, middle_grad, grad_heads, out_grad, down_sum, down_away, up_sum, up_away, small = middle(
        attended,
        stem_out,
        w_out,
        gain_second,
        w_up,
        w_down,
        jnp.broadcast_to(bias.reshape(1, -1), (8, 2 * D)),
        jnp.broadcast_to(b_down.astype(F32), (8, D)),
        cot,
    )
    down_came, up_came = swap_x(down_away), swap_chip(up_away)
    dq, dkv, output = attend_back(
        q, kv, grad_heads, attended_t, lse, seg_ids, frame_valid, output, 128, 256, heads
    )
    *results, small_sum, gain_sum = tail(
        down_sum,
        down_came,
        up_sum,
        up_came,
        out_grad,
        small,
        dq,
        dkv,
        normed_seen,
        w_qkv,
        joint,
        stem_out,
        middle_grad,
        gain_first,
        w_skip,
    )
    results = finish(results, small_sum, gain_sum)
    input_grad, skip_grad, down_share, up_share, qkv_share, out_share, skip_share, mine = results
    return (
        output[None],
        input_grad[None],
        skip_grad[None],
        skip_share,
        mine[1, :32],
        qkv_share,
        out_share,
        mine[2, :32],
        up_share,
        mine[0],
        down_share,
        mine[3, :32],
    )


def block_scores(q_blk, pos_blk, seg_blk, all_keys, seg_row, valid_row, slopes, score_scale):
    key_pos = jnp.arange(all_keys.shape[0])
    scores = (
        jnp.einsum("qhd,khd->hqk", q_blk, all_keys, preferred_element_type=jnp.float32)
        * score_scale
    )
    distance = jnp.abs(pos_blk[:, None] - key_pos[None, :]).astype(jnp.float32)
    scores = scores - slopes[:, None, None] * distance[None]
    allowed = (seg_blk[:, None] == seg_row[None, :]) & (
        (valid_row[None, :] == 1) | (pos_blk[:, None] == key_pos[None, :])
    )
    return jnp.where(allowed[None], scores, -jnp.inf)


def split_row(packed_row, heads_local):
    length = packed_row.shape[0]
    qkv_rows = packed_row.reshape(length, 3, heads_local, HD)
    return (qkv_rows[:, 0], qkv_rows[:, 1], qkv_rows[:, 2])


def attend_row(packed_row, seg_row, valid_row, slopes, heads_local, block_rows, score_scale):
    length = packed_row.shape[0]
    queries, all_keys, all_values = split_row(packed_row, heads_local)
    count = length // block_rows
    positions = jnp.arange(length)

    def one_block(block_in):
        q_blk, pos_blk, seg_blk = block_in
        scores = block_scores(
            q_blk, pos_blk, seg_blk, all_keys, seg_row, valid_row, slopes, score_scale
        )
        peak = jnp.max(scores, axis=-1, keepdims=True)
        log_total = peak + jnp.log(jnp.sum(jnp.exp(scores - peak), axis=-1, keepdims=True))
        attn_probs = jnp.exp(scores - log_total).astype(jnp.bfloat16)
        attended = jnp.einsum(
            "hqk,khd->qhd", attn_probs, all_values, preferred_element_type=jnp.float32
        )
        return (attended.astype(jnp.bfloat16), log_total[..., 0])

    attended, log_total = lax.map(
        one_block,
        (
            queries.reshape(count, block_rows, heads_local, HD),
            positions.reshape(count, block_rows),
            seg_row.reshape(count, block_rows),
        ),
    )
    return (attended.reshape(length, 1, heads_local * HD), log_total)


def attend_row_back(
    packed_row,
    log_total,
    grad_row,
    seg_row,
    valid_row,
    slopes,
    heads_local,
    block_rows,
    score_scale,
):
    length = packed_row.shape[0]
    queries, all_keys, all_values = split_row(packed_row, heads_local)
    count = length // block_rows
    positions = jnp.arange(length)
    grad_out = grad_row.reshape(count, block_rows, heads_local, HD)

    def one_block(carry, block_in):
        key_grad, value_grad = carry
        q_blk, pos_blk, seg_blk, total_blk, grad_blk = block_in
        scores = block_scores(
            q_blk, pos_blk, seg_blk, all_keys, seg_row, valid_row, slopes, score_scale
        )
        soft = jnp.exp(scores - total_blk[..., None])
        value_grad = value_grad + jnp.einsum(
            "hqk,qhd->khd", soft.astype(jnp.bfloat16), grad_blk, preferred_element_type=jnp.float32
        )
        prob_grad = jnp.einsum(
            "qhd,khd->hqk", grad_blk, all_values, preferred_element_type=jnp.float32
        )
        score_grad = (
            soft * (prob_grad - jnp.sum(soft * prob_grad, axis=-1, keepdims=True))
        ).astype(jnp.bfloat16)
        query_grad = (
            jnp.einsum("hqk,khd->qhd", score_grad, all_keys, preferred_element_type=jnp.float32)
            * score_scale
        )
        key_grad = (
            key_grad
            + jnp.einsum("hqk,qhd->khd", score_grad, q_blk, preferred_element_type=jnp.float32)
            * score_scale
        )
        return ((key_grad, value_grad), query_grad)

    zero_rows = jnp.zeros((length, heads_local, HD), jnp.float32)
    (key_grad, value_grad), query_grad = lax.scan(
        one_block,
        (zero_rows, zero_rows),
        (
            queries.reshape(count, block_rows, heads_local, HD),
            positions.reshape(count, block_rows),
            seg_row.reshape(count, block_rows),
            log_total,
            grad_out,
        ),
    )
    stacked = jnp.stack([query_grad.reshape(length, heads_local, HD), key_grad, value_grad], axis=1)
    return stacked.astype(jnp.bfloat16).reshape(length, 3, 1, heads_local * HD)


def body(
    inputs,
    skip_feats,
    seg_ids,
    frame_valid,
    w_skip,
    gain_one,
    w_qkv,
    w_out,
    gain_two,
    w_up,
    b_up,
    w_down,
    b_down,
    cotangent,
):
    parts = lax.axis_size("seq")
    heads_local = H // parts
    width_local = heads_local * HD
    rows_here = inputs.shape[0]
    frames = inputs.shape[1]
    length = frames * parts
    block_rows = min(512, length)
    score_scale = 1.0 / math.sqrt(HD)
    first_head = lax.axis_index("seq") * heads_local
    slopes = jnp.exp2(-8.0 * (first_head + jnp.arange(heads_local) + 1).astype(jnp.float32) / H)
    gain_first = gain_one.astype(jnp.float32)
    gain_second = gain_two.astype(jnp.float32)
    bias_up = b_up.astype(jnp.float32)
    joined = jnp.concatenate([inputs, skip_feats], axis=-1)
    stem_out = jnp.einsum("rfc,cd->rfd", joined, w_skip, preferred_element_type=jnp.float32)
    unit_one, inverse_one, normed = norm_forward(stem_out, gain_first)
    normed = normed.astype(jnp.bfloat16)
    packed = jnp.einsum("rfd,de->rfe", normed, w_qkv, preferred_element_type=jnp.float32).astype(
        jnp.bfloat16
    )
    packed = packed.reshape(rows_here, frames, 3, parts, width_local)
    by_heads = lax.all_to_all(packed, "seq", split_axis=3, concat_axis=1, tiled=True)

    def forward_row(row_data):
        return attend_row(
            row_data[0], row_data[1], row_data[2], slopes, heads_local, block_rows, score_scale
        )

    attended, log_total = lax.map(forward_row, (by_heads, seg_ids, frame_valid))
    by_frames = lax.all_to_all(attended, "seq", split_axis=1, concat_axis=2, tiled=True)
    mixed_out = by_frames.reshape(rows_here, frames, D)
    middle = stem_out + jnp.einsum(
        "rfd,de->rfe", mixed_out, w_out, preferred_element_type=jnp.float32
    )
    unit_two, inverse_two, second = norm_forward(middle, gain_second)
    second = second.astype(jnp.bfloat16)
    hidden = jnp.einsum("rfd,dk->rfk", second, w_up, preferred_element_type=jnp.float32) + bias_up
    active_full, gelu_back = jax.vjp(gelu_exact, hidden)
    active = active_full.astype(jnp.bfloat16)
    result = (
        middle
        + jnp.einsum("rfk,kd->rfd", active, w_down, preferred_element_type=jnp.float32)
        + b_down.astype(jnp.float32)
    )
    output = result.astype(jnp.bfloat16)
    cot_full = cotangent.astype(jnp.float32)
    down_grad = jnp.einsum("rfk,rfd->kd", active, cotangent, preferred_element_type=jnp.float32)
    bias_down_grad = jnp.sum(cot_full, axis=(0, 1))
    active_grad = jnp.einsum("rfd,kd->rfk", cotangent, w_down, preferred_element_type=jnp.float32)
    hidden_grad = gelu_back(active_grad)[0].astype(jnp.bfloat16)
    up_grad = jnp.einsum("rfd,rfk->dk", second, hidden_grad, preferred_element_type=jnp.float32)
    bias_up_grad = jnp.sum(hidden_grad.astype(jnp.float32), axis=(0, 1))
    second_grad = jnp.einsum("rfk,dk->rfd", hidden_grad, w_up, preferred_element_type=jnp.float32)
    middle_part, gain_two_grad = norm_backward(second_grad, unit_two, inverse_two, gain_second)
    middle_grad = cot_full + middle_part
    middle_low = middle_grad.astype(jnp.bfloat16)
    out_grad = jnp.einsum("rfd,rfe->de", mixed_out, middle_low, preferred_element_type=jnp.float32)
    mixed_grad = jnp.einsum(
        "rfe,de->rfd", middle_low, w_out, preferred_element_type=jnp.float32
    ).astype(jnp.bfloat16)
    grad_heads = lax.all_to_all(
        mixed_grad.reshape(rows_here, frames, parts, width_local),
        "seq",
        split_axis=2,
        concat_axis=1,
        tiled=True,
    )

    def backward_row(row_data):
        return attend_row_back(
            row_data[0],
            row_data[1],
            row_data[2],
            row_data[3],
            row_data[4],
            slopes,
            heads_local,
            block_rows,
            score_scale,
        )

    packed_grad = lax.map(backward_row, (by_heads, log_total, grad_heads, seg_ids, frame_valid))
    packed_back = lax.all_to_all(packed_grad, "seq", split_axis=1, concat_axis=3, tiled=True)
    packed_back = packed_back.reshape(rows_here, frames, 3 * D)
    qkv_grad = jnp.einsum("rfd,rfe->de", normed, packed_back, preferred_element_type=jnp.float32)
    normed_grad = jnp.einsum("rfe,de->rfd", packed_back, w_qkv, preferred_element_type=jnp.float32)
    stem_part, gain_one_grad = norm_backward(normed_grad, unit_one, inverse_one, gain_first)
    stem_low = (middle_grad + stem_part).astype(jnp.bfloat16)
    skip_w_grad = jnp.einsum("rfc,rfd->cd", joined, stem_low, preferred_element_type=jnp.float32)
    joined_grad = jnp.einsum("rfd,cd->rfc", stem_low, w_skip, preferred_element_type=jnp.float32)
    input_grad = joined_grad[..., :D].astype(jnp.bfloat16)
    skip_grad = joined_grad[..., D:].astype(jnp.bfloat16)
    (
        skip_share,
        gain_one_share,
        qkv_share,
        out_share,
        gain_two_share,
        up_share,
        bias_up_share,
        down_share,
        bias_down_share,
    ) = (
        lax.psum_scatter(skip_w_grad, ("rows", "seq"), scatter_dimension=0, tiled=True),
        lax.psum_scatter(gain_one_grad, ("rows", "seq"), scatter_dimension=0, tiled=True),
        lax.psum_scatter(qkv_grad, ("rows", "seq"), scatter_dimension=0, tiled=True),
        lax.psum_scatter(out_grad, ("rows", "seq"), scatter_dimension=0, tiled=True),
        lax.psum_scatter(gain_two_grad, ("rows", "seq"), scatter_dimension=0, tiled=True),
        lax.psum_scatter(up_grad, ("rows", "seq"), scatter_dimension=0, tiled=True),
        lax.psum_scatter(bias_up_grad, ("rows", "seq"), scatter_dimension=0, tiled=True),
        lax.psum_scatter(down_grad, ("rows", "seq"), scatter_dimension=0, tiled=True),
        lax.psum_scatter(bias_down_grad, ("rows", "seq"), scatter_dimension=0, tiled=True),
    )
    return (
        output,
        input_grad,
        skip_grad,
        skip_share,
        gain_one_share,
        qkv_share,
        out_share,
        gain_two_share,
        up_share,
        bias_up_share,
        down_share,
        bias_down_share,
    )


def solution(mesh):
    fits = (mesh.shape["rows"], mesh.shape["seq"]) == (8, 4)
    return jax.shard_map(
        body_chips if fits else body,
        mesh=mesh,
        in_specs=(
            P("rows", "seq", None),
            P("rows", "seq", None),
            P("rows", None),
            P("rows", None),
            P(),
            P(),
            P(),
            P(),
            P(),
            P(),
            P(),
            P(),
            P(),
            P("rows", "seq", None),
        ),
        out_specs=(
            P("rows", "seq", None),
            P("rows", "seq", None),
            P("rows", "seq", None),
            P(("rows", "seq"), None),
            P(("rows", "seq")),
            P(("rows", "seq"), None),
            P(("rows", "seq"), None),
            P(("rows", "seq")),
            P(("rows", "seq"), None),
            P(("rows", "seq")),
            P(("rows", "seq"), None),
            P(("rows", "seq")),
        ),
        check_vma=False,
    )
```

profile of v0, /device:TPU:0, one launch (start us, length us, event | category | flops | bytes accessed | tf_op | source)
XLA Modules:
  0.0 258.0 jit_solution(4194674793073491689)
XLA Ops:
  0.7 0.7 dynamic-slice_convert_fusion
  1.4 1.3 broadcast_in_dim.25.refs_3_.refs_13_
  2.7 28.5 %front.1 = (f32[512,1024]{1,0:T(8,128)}, bf16[1792,1024]{1,0:T(8,128)(2,1)}, bf16[1024,512]{1,0:T(8,128)(2,1)}, bf16[1792,1024]{1,0:T(8,128)(2,1)}, bf16[2048,512]{1,0:T(8,128)(2,1)}) custom-call(bf16[512,1024]{1,0:T(8,128)(2,1)} %bitcast.24, bf16[512,1024]{1,0:T(8,128)(2,1)} %bitcast.25, bf16[2048,1024]{1,0:T(8,128)(2,1)} %refs_14_.1, ...), custom_call_target="tpu_custom_call" | custom-call | flops 8000000000 | bytes 24000000 | tf_op jit(solution)/shard_map/front/pallas_call | solution.py:225
  31.1 0.0 copy-start
  31.1 0.0 copy-start.1
  31.2 21.6 %attend.1 = (bf16[1024,512]{1,0:T(8,128)(2,1)}, bf16[512,1024]{1,0:T(8,128)(2,1)}, f32[4,2048]{1,0:T(4,128)}) custom-call(s32[1,2048]{1,0:T(1,128)} %seg.3, bf16[1024,512]{1,0:T(8,128)(2,1)} %get-tuple-element.49.q_in, bf16[1792,1024]{1,0:T(8,128)(2,1)} %get-tuple-element.50.kv_in, s32[1,2048]{1,0:T(1,128)} %seg.3, s32[1,2048]{1,0:T(1,128)} %valid.3), custom_call_target="tpu_custom_call" | custom-call | flops 8000000000 | bytes 8000000 | tf_op jit(solution)/shard_map/attend/pallas_call | solution.py:453
  52.8 0.0 copy-done
  52.8 0.6 broadcast_in_dim.26.refs_3_
  53.4 0.0 copy-done.1
  53.4 0.6 broadcast_in_dim.29.refs_7_
  54.0 0.6 broadcast_in_dim.28.refs_6_
  54.6 66.3 %middle.1 = (bf16[512,1024]{1,0:T(8,128)(2,1)}, f32[512,1024]{1,0:T(8,128)}, bf16[1024,512]{1,0:T(8,128)(2,1)}, bf16[1024,1024]{1,0:T(8,128)(2,1)}, bf16[4,128,1...) custom-call(bf16[1024,512]{1,0:T(8,128)(2,1)} %get-tuple-element.51., ...), custom_call_target="tpu_custom_call" | custom-call | flops 28000000000 | bytes 40000000 | tf_op jit(solution)/shard_map/middle/pallas_call | solution.py:996
  121.0 0.8 collective-permute-start
  121.8 1.5 collective-permute-start.1
  123.3 29.1 %attend_back.1 = (bf16[1024,512]{1,0:T(8,128)(2,1)}, bf16[1792,1024]{1,0:T(8,128)(2,1)}, bf16[512,1024]{1,0:T(8,128)(2,1)}) custom-call(s32[1,2048]{1,0:T(1,128)} %seg.3, bf16[1024,512]{1,0:T(8,128)(2,1)} %get-tuple-element.49.q_in, bf16[1792,1024]{1,0:T(8,128)(2,1)} %get-tuple-element.50.kv_in, bf16[1024,512]{1,0:T(8,128)(2,1)} %get-tuple-element.53.grad_in, ...), custom_call_target="tpu_custom_call" | custom-call | flops 20000000000 | bytes 16000000 | tf_op jit(solution)/shard_map/attend_back/pallas_call | solution.py:634
  152.4 0.0 collective-permute-done
  152.5 0.0 collective-permute-done.1
  152.5 98.5 %tail.1 = (bf16[512,1024]{1,0:T(8,128)(2,1)}, bf16[512,1024]{1,0:T(8,128)(2,1)}, f32[128,1024]{1,0:T(8,128)}, f32[32,4096]{1,0:T(8,128)}, f32[32,3072]{1,0:T(8,1...) custom-call(bf16[2,2,128,1024]{3,2,1,0:T(8,128)(2,1)} %bitcast.31, ...), custom_call_target="tpu_custom_call" | custom-call | flops 16999999488 | bytes 60000000 | tf_op jit(solution)/shard_map/tail/pallas_call | solution.py:1522
  250.9 4.6 %finish.1 = (bf16[512,1024]{1,0:T(8,128)(2,1)}, bf16[512,1024]{1,0:T(8,128)(2,1)}, f32[128,1024]{1,0:T(8,128)}, f32[32,4096]{1,0:T(8,128)}, f32[32,3072]{1,0:T(8...) custom-call(bf16[512,1024]{1,0:T(8,128)(2,1)} %get-tuple-element.69.refs_0_, ...), custom_call_target="tpu_custom_call" | custom-call | tf_op jit(solution)/shard_map/finish/pallas_call | solution.py:1578
  255.5 1.2 slice_bitcast_fusion.1
  256.7 1.3 slice_bitcast_fusion
Async XLA Ops:
  31.1 21.6 %copy-start = (bf16[1024]{0:T(1024)(128)(2,1)S(1)}, bf16[1024]{0:T(1024)(128)(2,1)}, u32[]{:S(2)}) copy-start(bf16[1024]{0:T(1024)(128)(2,1)} %param.22) | copy-start | bytes 6148
  31.1 22.2 %copy-start.1 = (bf16[1024]{0:T(1024)(128)(2,1)S(1)}, bf16[1024]{0:T(1024)(128)(2,1)}, u32[]{:S(2)}) copy-start(bf16[1024]{0:T(1024)(128)(2,1)} %param.26) | copy-start | bytes 6148
  121.0 31.5 %collective-permute-start = (bf16[4,128,1024]{2,1,0:T(8,128)(2,1)}, bf16[4,128,1024]{2,1,0:T(8,128)(2,1)}, u32[]{:S(2)}, u32[]{:S(2)}) collective-permute-start(bf16[4,128,1024]{2,1,0:T(8,128)(2,1)} %get-tuple-element.59), channel_id=1, source_target_pairs={{0,4},{4,0},{8,12},{12,8},{16,20},{20,16},{24,28},{28,24},{1,5},{5... | collective-permute-start | bytes 3145736 | tf_op jit(solution)/shard_map/ppermute | solution.py:1597
  121.8 30.7 %collective-permute-start.1 = (bf16[4,64,2048]{2,1,0:T(8,128)(2,1)}, bf16[4,64,2048]{2,1,0:T(8,128)(2,1)}, u32[]{:S(2)}, u32[]{:S(2)}) collective-permute-start(bf16[4,64,2048]{2,1,0:T(8,128)(2,1)} %get-tuple-element.61), channel_id=1, source_target_pairs={{0,2},{1,3},{2,0},{3,1},{4,6},{5,7},{6,4},{7,5},{8,10},{9,11},{10,... | collective-permute-start | bytes 3145736 | tf_op jit(solution)/shard_map/ppermute | solution.py:1601
where the time goes:
time: 260 us; the launch traced here: 258 us
  Pallas kernels  249 us (96%)
  local copies, waits for them, and re-layouts  5.69 us (2%)
    pallas_call x1, Pallas kernels, tail(): pl.pallas_call(tail_kernel, out_shape=out_shape, in_specs=[hbm] * 13 + [v...  98.5 us
    pallas_call x1, Pallas kernels, middle(): pl.pallas_call(middle_kernel, out_shape=[jax.ShapeDtypeStruct((FRAMES, D)...  66.3 us
    pallas_call x1, Pallas kernels, attend_back(): pl.pallas_call(functools.partial(attend_back_kernel, bq, bk, heads), out_...  29.1 us
    pallas_call x1, Pallas kernels, front(): pl.pallas_call(front_kernel, out_shape=[jax.ShapeDtypeStruct((FRAMES, D),...  28.5 us
    pallas_call x1, Pallas kernels, attend(): pl.pallas_call(functools.partial(attend_kernel, bq, bk, heads), out_shape...  21.6 us
  transfers between devices with their start and end apart: 2, of which 0 were waited for; matrix products, arithmetic and copies ran while one was open for 0% of the time, Pallas kernels for 11%

commit v1 on v0

--- a/solution.py
+++ b/solution.py
@@ -79,16 +79,21 @@
         self.z, self.x, self.y, self.c = row // 2, row % 2, col // 2, col % 2
         z, x, y, c = self.z, self.x, self.y, self.c
         self.high, self.low = z // 2, z % 2
+        self.is_end = z == 3 * self.high
+        self.is_inner = z == 1 + self.high
         self.core = (row, y * 2 + 1 - c)
         self.over_y = (row, (1 - y) * 2 + c)
         self.over_x = (z * 2 + 1 - x, col)
         self.over_low = ((self.high * 2 + 1 - self.low) * 2 + x, col)
         self.over_high = (((1 - self.high) * 2 + self.low) * 2 + x, col)
+        self.over_mirror = ((3 - z) * 2 + x, col)
         self.sends, self.recvs, self.count, self.started = sends, recvs, 0, []
 
     def greet(self, near=False):
         barrier = pltpu.get_barrier_semaphore()
-        peers = [self.core, self.over_y] if near else [self.core, self.over_y, self.over_x, self.over_low, self.over_high]
+        peers = [self.core, self.over_y]
+        if not near:
+            peers += [self.over_x, self.over_low, self.over_high, self.over_mirror]
         for peer in peers:
             pl.semaphore_signal(barrier, inc=1, device_id=peer, device_id_type=MESH)
         pl.semaphore_wait(barrier, len(peers))
@@ -102,16 +107,22 @@
             src, dst, self.sends.at[at], self.recvs.at[at], device_id=peer, device_id_type=MESH
         )
 
-    def send(self, src, dst, peer):
+    def send(self, src, dst, peer, here=None):
         copy = self.copy(src, dst, self.reserve(1), peer)
-        copy.start()
-        self.started.append(copy)
+        if here is None:
+            copy.start()
+        else:
+            pl.when(here)(copy.start)
+        self.started.append((copy, here))
         return copy
 
     def drain(self):
         assert self.count <= self.sends.shape[0]
-        for copy in self.started:
-            copy.wait_send()
+        for copy, here in self.started:
+            if here is None:
+                copy.wait_send()
+            else:
+                pl.when(here)(copy.wait_send)
 
 
 def head_columns(wqkv, part, core):
@@ -681,67 +692,158 @@
 
 
 class Unit:
-    def __init__(self, links, own, came, y_first, done):
-        self.links, self.own, self.came, self.y_first, self.done = links, own, came, y_first, done
+    def __init__(self, links, own, came, sums, y_first, done, straight=False):
+        self.links, self.own, self.came, self.sums = links, own, came, sums
+        self.y_first, self.done, self.straight = y_first, done, straight
 
     def add_core(self, r0):
-        for k in range(2):
+        for k in range(4):
             for i in range(2):
-                for j in range(2):
-                    add_into(self.own.at[k, i, j], r0.at[k, i, j])
+                add_into(self.own.at[k, i], r0.at[k, i])
 
     def send_first(self):
         n, a = self.links, self.own
         if self.y_first:
-            self.first = n.send(a.at[:, :, :, 1 - n.y], self.came[0], n.over_y)
+            self.first = n.send(a.at[:, :, 1 - n.y], self.came[0], n.over_y)
         else:
-            self.first = n.send(a.at[:, :, 1 - n.x], self.came[0], n.over_x)
+            self.first = n.send(a.at[:, 1 - n.x], self.came[0], n.over_x)
 
     def turn_first(self):
         self.first.wait_recv()
         n, a, b = self.links, self.own, self.came[0]
-        for k in range(2):
-            for i in range(2):
-                part = a.at[k, i, :, n.y] if self.y_first else a.at[k, i, n.x]
-                add_into(part, b.at[k, i])
+        for k in range(4):
+            add_into(a.at[k, :, n.y] if self.y_first else a.at[k, n.x], b.at[k])
         if self.y_first:
-            self.second = n.send(a.at[:, :, 1 - n.x, n.y], self.came[1], n.over_x)
+            self.second = n.send(a.at[:, 1 - n.x, n.y], self.came[1], n.over_x)
         else:
-            self.second = n.send(a.at[:, :, n.x, 1 - n.y], self.came[1], n.over_y)
-
-    def chip(self, *at):
-        return self.own.at[*at, self.links.x, self.links.y]
+            self.second = n.send(a.at[:, n.x, 1 - n.y], self.came[1], n.over_y)
+
+    def chip(self, at):
+        return self.own.at[at, self.links.x, self.links.y]
 
     def turn_second(self):
         self.second.wait_recv()
         self.after_second()
 
     def after_second(self):
+        n, to = self.links, self.came[2]
+        add_into(self.chip(slice(None)), self.came[1])
+        if self.straight:
+            low, high = 1 - n.low, 1 - n.high
+            places = [(2 * n.high + low, n.over_low), (2 * high + n.low, n.over_high), (3 - n.z, n.over_mirror)]
+            self.third = [n.send(self.chip(p), to.at[j], peer) for j, (p, peer) in enumerate(places)]
+        else:
+            part = self.chip(pl.ds(1 - n.high, 3))
+            self.third = n.send(part, to.at[pl.ds(0, 3)], n.over_low, n.is_end)
+
+    def turn_third(self):
+        n = self.links
+
+        @pl.when(n.is_inner)
+        def _():
+            self.third.wait_recv()
+            add_into(self.chip(pl.ds(1 - n.high, 3)), self.came[2].at[pl.ds(0, 3)])
+
+        part = self.chip(pl.ds(2 - 2 * n.high, 2))
+        self.fourth = n.send(part, self.came[2].at[pl.ds(3, 2)], n.over_mirror, n.is_inner)
+
+    def turn_fourth(self):
+        n = self.links
+
+        @pl.when(n.is_inner)
+        def _():
+            self.fourth.wait_recv()
+            add_into(self.chip(pl.ds(2 * n.high, 2)), self.came[2].at[pl.ds(3, 2)])
+
+        self.fifth = n.send(self.chip(3 * n.high), self.came[2].at[5], n.over_low, n.is_inner)
+
+    def finish(self):
+        n = self.links
+        if self.straight:
+            for copy in self.third:
+                copy.wait_recv()
+            value = self.chip(n.z)[...].astype(F32)
+            for j in range(3):
+                value = value + self.came[2][j].astype(F32)
+            self.done(value)
+            return
+        self.sums[...] = self.chip(n.z)[...].astype(F32)
+
+        @pl.when(n.is_end)
+        def _():
+            self.fifth.wait_recv()
+            self.sums[...] += self.came[2][5].astype(F32)
+
+        self.done(self.sums[...])
+
+
+class LowUnit(Unit):
+    def send_first(self):
+        n = self.links
+        self.first = n.send(self.own.at[:, 1 - n.low], self.came[0], n.over_low)
+
+    def turn_first(self):
+        self.first.wait_recv()
         n = self.links
         for k in range(2):
-            add_into(self.chip(k, slice(None)), self.came[1].at[k])
-        self.third = n.send(self.chip(slice(None), 1 - n.low), self.came[2], n.over_low)
+            for i in range(2):
+                add_into(self.own.at[k, n.low, i], self.came[0].at[k, i])
+        self.second = n.send(self.own.at[:, n.low, 1 - n.x], self.came[1], n.over_x)
+
+    def turn_second(self):
+        self.second.wait_recv()
+        n = self.links
+        for k in range(2):
+            add_into(self.own.at[k, n.low, n.x], self.came[1].at[k])
+        self.third = n.send(self.own.at[:, n.low, n.x, 1 - n.y], self.came[2], n.over_y)
+
+    def turn_third(self):
+        self.third.wait_recv()
+        n = self.links
+        add_into(self.own.at[:, n.low, n.x, n.y], self.came[2])
+        self.fourth = n.send(self.own.at[1 - n.high, n.low, n.x, n.y], self.came[3], n.over_high)
+
+    def finish(self):
+        self.fourth.wait_recv()
+        n = self.links
+        value = self.own[n.high, n.low, n.x, n.y].astype(F32)
+        self.done(value + self.came[3][...].astype(F32))
+
+
+class LateUnit(Unit):
+    def chip(self, at):
+        return self.own.at[at]
+
+    def begin(self, *loads):
+        for copy in loads:
+            copy.wait()
+        self.after_second()
+
+
+class PairUnit:
+    def __init__(self, links, own, came, over_x, done):
+        self.links, self.own, self.came, self.done = links, own, came, done
+        self.at, self.peer = (links.x, links.over_x) if over_x else (links.y, links.over_y)
+
+    def begin(self, *loads):
+        for copy in loads:
+            copy.wait()
+        for k in range(2):
+            add_into(self.own.at[k], self.came[0].at[k])
+        self.third = self.links.send(self.own.at[:, 1 - self.at], self.came[1], self.peer)
 
     def turn_third(self):
         n = self.links
         self.third.wait_recv()
-        add_into(self.chip(slice(None), n.low), self.came[2])
-        self.fourth = n.send(self.chip(1 - n.high, n.low), self.came[3], n.over_high)
+        for k in range(2):
+            value = self.own.at[k, self.at]
+            value[...] = value[...] + self.came[1][k]
+        self.fourth = n.send(self.own.at[1 - n.high, self.at], self.came[2], n.over_high)
 
     def finish(self):
-        n = self.links
         self.fourth.wait_recv()
-        self.done(self.chip(n.high, n.low)[...].astype(F32) + self.came[3][...].astype(F32))
-
-
-class LateUnit(Unit):
-    def chip(self, *at):
-        return self.own.at[*at]
-
-    def turn_second(self, *loads):
-        for copy in loads:
-            copy.wait()
-        self.after_second()
+        value = self.own[self.links.high, self.at].astype(F32)
+        self.done(value + self.came[2][...].astype(F32))
 
 
 class Small:
@@ -767,6 +869,9 @@
 
 STEPS = 8
 STEP = 256
+P_COLS = 640
+X_STEPS = 6
+X_COLS = STEP * X_STEPS
 
 
 def middle_kernel(*refs):
@@ -781,7 +886,8 @@
         bias_down,
         cot_in,
     ) = refs[:9]
-    o_out, o_grad, o_heads, o_wo, o_down, o_down_away, o_up, o_up_away, o_small = refs[9:18]
+    o_out, o_grad, o_heads, o_wo, o_small = refs[9:14]
+    o_p, o_p_away, o_q, o_q_away, o_x, o_x_away, o_z, o_z_away = refs[14:22]
     (
         att,
         att_came,
@@ -801,16 +907,22 @@
         low,
         swap_out,
         swap_in,
-        down_send,
-        down_keep,
-        down_came,
-        up_send,
-        up_keep,
-        up_came,
+        p_send,
+        p_keep,
+        p_came,
+        q_send,
+        q_keep,
+        q_came,
+        x_send,
+        x_keep,
+        x_came,
+        z_send,
+        z_keep,
+        z_came,
         loads,
         sends,
         recvs,
-    ) = refs[18:]
+    ) = refs[22:]
     links = Links(sends, recvs)
     x, y, c = links.x, links.y, links.c
     loading = []
@@ -869,13 +981,19 @@
         copy.wait_recv()
     second_t[:, FRAMES:] = second[other, :].T
 
-    down_at, up_at = links.reserve(STEPS), links.reserve(STEPS)
-
-    def down_copy(i):
-        return links.copy(down_send.at[i], down_came.at[i], down_at + i, links.over_y)
-
-    def up_copy(i):
-        return links.copy(up_send.at[i], up_came.at[i], up_at + i, links.over_x)
+    p_at, q_at, x_at, z_at = [links.reserve(k) for k in (STEPS, 4, X_STEPS, STEPS - X_STEPS)]
+
+    def p_copy(i):
+        return links.copy(p_send.at[i], p_came.at[i], p_at + i, links.over_y)
+
+    def q_copy(i):
+        return links.copy(q_send.at[i], q_came.at[i], q_at + i, links.over_low)
+
+    def x_copy(i):
+        return links.copy(x_send.at[i], x_came.at[i], x_at + i, links.over_x)
+
+    def z_copy(i):
+        return links.copy(z_send.at[i], z_came.at[i], z_at + i, links.over_low)
 
     def feed_step(i, _):
         up, down = ups[i], downs[i]
@@ -898,15 +1016,41 @@
         for j in range(2):
             o_small[pl.ds(4 * i + 2 * j + c, 1), :] = total[:, 128 * j : 128 * (j + 1)]
         value = dot_tn(active[...], cot[...]).astype(BF16)
-        down_send[i] = jnp.where(y == 0, value[128:], value[:128])
-        down_keep[i] = jnp.where(y == 0, value[:128], value[128:])
-        down_copy(i).start()
+        p_send[i] = jnp.where(y == 0, value[128:, :P_COLS], value[:128, :P_COLS])
+        p_keep[i] = jnp.where(y == 0, value[:128, :P_COLS], value[128:, :P_COLS])
+        p_copy(i).start()
+        stays = lax.rem(i // 2, 2) == links.low
+        slot = 2 * (i // 4) + lax.rem(i, 2)
+        rest = value[:, P_COLS:].reshape(2, 128, D - P_COLS)
+
+        @pl.when(stays)
+        def _():
+            q_keep[slot] = rest
+
+        @pl.when(jnp.logical_not(stays))
+        def _():
+            q_send[slot] = rest
+            q_copy(slot).start()
+
         value = dot(second_t[...], hidden_grad[...]).astype(BF16)
-        for k in range(4):
-            first, last = value[256 * k : 256 * k + 128], value[256 * k + 128 : 256 * (k + 1)]
-            up_send[i, k] = jnp.where(x == 0, last, first)
-            up_keep[i, k] = jnp.where(x == 0, first, last)
-        up_copy(i).start()
+
+        @pl.when(i < X_STEPS)
+        def _():
+            for k in range(4):
+                first, last = value[256 * k : 256 * k + 128], value[256 * k + 128 : 256 * (k + 1)]
+                x_send[i, k] = jnp.where(x == 0, last, first)
+                x_keep[i, k] = jnp.where(x == 0, first, last)
+            x_copy(i).start()
+
+        @pl.when(i >= X_STEPS)
+        def _():
+            j = i - X_STEPS
+            for k in range(2):
+                first, last = value[512 * k : 512 * k + 256], value[512 * k + 256 : 512 * (k + 1)]
+                z_send[j, k] = jnp.where(links.low == 0, last, first)
+                z_keep[j, k] = jnp.where(links.low == 0, first, last)
+            z_copy(j).start()
+
         return 0
 
     lax.fori_loop(0, STEPS, feed_step, 0)
@@ -963,28 +1107,50 @@
     heads_core.wait_recv()
     o_heads[other, :] = swap_in[2, :, :WIDTH]
 
-    def add_step(i, _):
-        down_copy(i).wait()
-        value = down_keep[i] + down_came[i]
-        stays = lax.rem(i + x, 2) == 0
+    def add_p(i, _):
+        p_copy(i).wait()
+        value = p_keep[i] + p_came[i]
+        stays = lax.rem(i, 2) == x
 
         @pl.when(stays)
         def _():
-            o_down[i // 2] = value
+            o_p[i // 2] = value
 
         @pl.when(jnp.logical_not(stays))
         def _():
-            o_down_away[i // 2] = value
-
-        up_copy(i).wait()
-        columns = pl.ds(pl.multiple_of(STEP * i, STEP), STEP)
+            o_p_away[i // 2] = value
+
+        return 0
+
+    def add_q(i, _):
+        q_copy(i).wait()
+        o_q[i // 2, lax.rem(i, 2)] = q_keep[i, y] + q_came[i, y]
+        o_q_away[i // 2, lax.rem(i, 2)] = q_keep[i, 1 - y] + q_came[i, 1 - y]
+        return 0
+
+    def columns(i):
+        return pl.ds(pl.multiple_of(STEP * i, STEP), STEP)
+
+    def add_x(i, _):
+        x_copy(i).wait()
         for k in range(4):
-            value = up_keep[i, k] + up_came[i, k]
-            o_up[k, :, columns] = jnp.where(y == 0, value[:64], value[64:])
-            o_up_away[k, :, columns] = jnp.where(y == 0, value[64:], value[:64])
+            value = x_keep[i, k] + x_came[i, k]
+            o_x[k, :, columns(i)] = jnp.where(y == 0, value[:64], value[64:])
+            o_x_away[k, :, columns(i)] = jnp.where(y == 0, value[64:], value[:64])
         return 0
 
-    lax.fori_loop(0, STEPS, add_step, 0)
+    def add_z(i, _):
+        z_copy(i).wait()
+        for k in range(2):
+            value = z_keep[i, k] + z_came[i, k]
+            o_z[k, :, columns(i)] = jnp.where(x == 0, value[:128], value[128:])
+            o_z_away[k, :, columns(i)] = jnp.where(x == 0, value[128:], value[:128])
+        return 0
+
+    lax.fori_loop(0, STEPS, add_p, 0)
+    lax.fori_loop(0, 4, add_q, 0)
+    lax.fori_loop(0, X_STEPS, add_x, 0)
+    lax.fori_loop(0, STEPS - X_STEPS, add_z, 0)
     links.drain()
 
 
@@ -992,7 +1158,7 @@
     hbm, vm = pl.BlockSpec(memory_space=HBM), pl.BlockSpec(memory_space=VMEM)
     low = lambda *shape: pltpu.VMEM(shape, BF16)
     full = lambda *shape: pltpu.VMEM(shape, F32)
-    copies = 24
+    copies = 28
     return pl.pallas_call(
         middle_kernel,
         out_shape=[
@@ -1000,12 +1166,14 @@
             jax.ShapeDtypeStruct((FRAMES, D), F32),
             jax.ShapeDtypeStruct((CHIP, WIDTH), BF16),
             jax.ShapeDtypeStruct((D, D), BF16),
-            *[jax.ShapeDtypeStruct((4, 128, D), BF16)] * 2,
-            *[jax.ShapeDtypeStruct((4, 64, 2 * D), BF16)] * 2,
             jax.ShapeDtypeStruct((48, 128), F32),
+            *[jax.ShapeDtypeStruct((4, 128, P_COLS), BF16)] * 2,
+            *[jax.ShapeDtypeStruct((2, 2, 128, D - P_COLS), BF16)] * 2,
+            *[jax.ShapeDtypeStruct((4, 64, X_COLS), BF16)] * 2,
+            *[jax.ShapeDtypeStruct((2, 128, 2 * D - X_COLS), BF16)] * 2,
         ],
         in_specs=[hbm] * 3 + [vm] + [hbm] * 2 + [vm] * 2 + [hbm],
-        out_specs=[vm] * 9,
+        out_specs=[vm] * 13,
         scratch_shapes=[
             low(FRAMES, WIDTH),
             low(FRAMES, WIDTH),
@@ -1025,12 +1193,10 @@
             low(FRAMES, D),
             low(3, FRAMES, D),
             low(3, FRAMES, D),
-            low(STEPS, 128, D),
-            low(STEPS, 128, D),
-            low(STEPS, 128, D),
-            low(STEPS, 4, 128, STEP),
-            low(STEPS, 4, 128, STEP),
-            low(STEPS, 4, 128, STEP),
+            *[low(STEPS, 128, P_COLS)] * 3,
+            *[low(4, 2, 128, D - P_COLS)] * 3,
+            *[low(X_STEPS, 4, 128, STEP)] * 3,
+            *[low(STEPS - X_STEPS, 2, 256, STEP)] * 3,
             pltpu.SemaphoreType.DMA((4 + 4 * STEPS,)),
             pltpu.SemaphoreType.DMA((copies,)),
             pltpu.SemaphoreType.DMA((copies,)),
@@ -1047,10 +1213,14 @@
 
 def tail_kernel(*refs):
     (
-        down_in,
-        down_came,
-        up_in,
-        up_came,
+        p_in,
+        p_came,
+        q_in,
+        q_came,
+        x_in,
+        x_came,
+        z_in,
+        z_came,
         wo_in,
         small_in,
         dq_in,
@@ -1062,8 +1232,8 @@
         grad_in,
         gain,
         wskip_in,
-    ) = refs[:15]
-    o_in, o_skip, o_down, o_up, o_qkv, o_wo, o_wskip, o_small, o_gain = refs[15:24]
+    ) = refs[:19]
+    o_in, o_skip, o_down, o_up, o_qkv, o_wo, o_wskip, o_small, o_gain = refs[19:28]
     (
         dq,
         dkv,
@@ -1081,21 +1251,32 @@
         halo_sum,
         halo,
         low,
-        down_own,
-        down_r2,
-        down_r3,
-        down_r4,
-        up_own,
-        up_r2,
-        up_r3,
-        up_r4,
+        low_own,
+        low_r1,
+        low_r2,
+        low_r3,
+        low_r4,
+        join_low,
+        p_own,
+        p_r2,
+        p_r3,
+        q_own,
+        q_r2,
+        q_r3,
+        q_r4,
+        x_own,
+        x_r2,
+        x_r3,
+        z_own,
+        z_r2,
+        z_r3,
+        z_r4,
         up_out,
         up_in_last,
         unit_own,
         unit_r1,
         unit_r2,
         unit_r3,
-        unit_r4,
         wo_r0,
         join_out,
         skip_own,
@@ -1104,7 +1285,7 @@
         skip_r1,
         skip_r2,
         skip_r3,
-        skip_r4,
+        sums,
         small_steps,
         small_into,
         gain_steps,
@@ -1112,7 +1293,7 @@
         loads,
         sends,
         recvs,
-    ) = refs[24:]
+    ) = refs[28:]
     links = Links(sends, recvs)
     y, c = links.y, links.c
     loading = []
@@ -1128,28 +1309,25 @@
     got_wkv = [load(head_columns(wqkv_in, 1 + i, c), wkv.at[:, pl.ds(WIDTH * i, WIDTH)]) for i in (0, 1)]
     got_far = load(dkv_in.at[far], dkv.at[far])
     links.greet()
-    wo_core = links.send(wo_in.at[:, :, :, :, 1 - c], wo_r0, links.core)
+    wo_core = links.send(wo_in.at[:, :, :, 1 - c], wo_r0, links.core)
     got_dq = load(dq_in, dq)
     got_near = load(dkv_in.at[near], dkv.at[near])
     got_seen = load(seen_in, seen)
-    got_wo = load(wo_in.at[:, :, :, :, c], unit_own.at[0])
+    got_wo = load(wo_in.at[:, :, :, c], unit_own.at[0])
     got_small = load(small_in, small_steps.at[0])
-    got_down = [
+    got_p = [
         [
-            load(down_in.at[:, :, pl.ds(64 * i, 64)], down_own.at[i]),
-            load(down_came.at[:, :, pl.ds(64 * i, 64)], down_r2.at[i]),
+            load(p_in.at[:, pl.ds(64 * i, 64)], p_own.at[i]),
+            load(p_came.at[:, pl.ds(64 * i, 64)], p_r2.at[i]),
         ]
         for i in range(2)
     ]
-    got_up = []
+    got_x = []
     for i, core in enumerate((1 - c, c)):
         rows = pl.ds(pl.multiple_of(32 * core, 32), 32)
-        got_up.append(
-            [
-                load(up_in.at[:, :, rows], up_own.at[i]),
-                load(up_came.at[:, :, rows], up_r2.at[i]),
-            ]
-        )
+        got_x.append([load(x_in.at[:, rows], x_own.at[i]), load(x_came.at[:, rows], x_r2.at[i])])
+    got_q = [load(q_in, q_own), load(q_came, q_r2)]
+    got_z = [load(z_in, z_own), load(z_came, z_r2)]
     got_wq = load(head_columns(wqkv_in, 0, c), wq)
     got_stem = load(stem_in, stem)
     got_grad = load(grad_in, grad)
@@ -1159,36 +1337,60 @@
 
     def to_down(i):
         def done(value):
-            o_down[pl.ds(64 * i, 64), :] = value
+            o_down[pl.ds(64 * i, 64), pl.ds(0, P_COLS)] = value
 
         return done
 
+    def to_down_rest(value):
+        o_down[:, pl.ds(P_COLS, D - P_COLS)] = value
+
+    def put_up(b, core, value):
+        o_up[:, pl.ds(pl.multiple_of(256 * b + 128 * core, 128), 128)] = value
+
+    def pass_up(at, value):
+        part = pl.ds(at, value.shape[1])
+        up_out[:, part] = value
+        up_last.append(links.send(up_out.at[:, part], up_in_last.at[:, part], links.core))
+
     def to_up_other(value):
-        up_out[...] = value
-        up_last.append(links.send(up_out, up_in_last, links.core))
+        pass_up(0, value)
 
     def to_up_mine(value):
+        for b in range(X_COLS // 128):
+            put_up(b, c, value[:, 128 * b : 128 * (b + 1)])
+
+    def to_up_rest(value):
+        pass_up(X_COLS, jnp.where(c == 0, value[32:], value[:32]))
+        mine = jnp.where(c == 0, value[:32], value[32:])
+        for b in range(X_COLS // 128, 16):
+            at = 128 * b - X_COLS
+            put_up(b, c, mine[:, at : at + 128])
+
+    def take_up():
+        for copy in up_last:
+            copy.wait_recv()
         for b in range(16):
-            at = pl.multiple_of(256 * b + 128 * c, 128)
-            o_up[:, pl.ds(at, 128)] = value[:, 128 * b : 128 * (b + 1)]
+            put_up(b, 1 - c, up_in_last[:, 128 * b : 128 * (b + 1)])
 
     up_last = []
-    downs = [
+
+    def room(rows, cols):
+        return sums.at[pl.ds(0, rows), pl.ds(0, cols)]
+
+    p0, p1 = [
         LateUnit(
-            links,
-            down_own.at[i],
-            (None, down_r2.at[i], down_r3.at[i], down_r4.at[i]),
-            True,
-            to_down(i),
+            links, p_own.at[i], (None, p_r2.at[i], p_r3.at[i]), room(64, P_COLS), True, to_down(i)
         )
         for i in range(2)
     ]
-    ups = [
+    x0, x1 = [
         LateUnit(
-            links, up_own.at[i], (None, up_r2.at[i], up_r3.at[i], up_r4.at[i]), False, done
+            links, x_own.at[i], (None, x_r2.at[i], x_r3.at[i]), room(32, X_COLS), False, done
         )
         for i, done in enumerate((to_up_other, to_up_mine))
     ]
+    rest_q = PairUnit(links, q_own, (q_r2, q_r3, q_r4), True, to_down_rest)
+    rest_z = PairUnit(links, z_own, (z_r2, z_r3, z_r4), False, to_up_rest)
 
     def to_wo(value):
         o_wo[...] = value
@@ -1206,15 +1408,16 @@
         return done
 
     def unit(k, y_first, done):
-        came = (unit_r1.at[k], unit_r2.at[k], unit_r3.at[k], unit_r4.at[k])
-        return Unit(links, unit_own.at[k], came, y_first, done)
+        came = (unit_r1.at[k], unit_r2.at[k], unit_r3.at[k])
+        return Unit(links, unit_own.at[k], came, room(ROWS, D), y_first, done)
 
     wo = unit(0, False, to_wo)
-    unit_q, unit_k, unit_v = [unit(1 + i, i == 1, to_qkv(i)) for i in range(3)]
+    unit_q, unit_v = unit(1, False, to_qkv(0)), unit(2, True, to_qkv(2))
+    unit_k = LowUnit(links, low_own, (low_r1, low_r2, low_r3, low_r4), None, False, to_qkv(1))
 
     def skip_unit(k, y_first, done):
-        came = (skip_r1.at[k], skip_r2.at[k], skip_r3.at[k], skip_r4.at[k])
-        return Unit(links, skip_own.at[k], came, y_first, done)
+        came = (skip_r1.at[k], skip_r2.at[k], skip_r3.at[k])
+        return Unit(links, skip_own.at[k], came, None, y_first, done, straight=True)
 
     skips = [
         [skip_unit(2 * q + half, half == 0, to_wskip(q, half)) for half in range(2)]
@@ -1256,12 +1459,20 @@
                 at = 128 * j + 64 * m
                 first, second = value[at : at + 32], value[at + 32 : at + 64]
                 mine, theirs = jnp.where(c == 0, first, second), jnp.where(c == 0, second, first)
-                unit_own[1 + k, i // 2, i % 2, j, m, :, columns] = mine
-                join_out[k, i // 2, i % 2, j, m] = theirs
+                if k == 1:
+                    low_own[i // 2, i % 2, j, m, :, columns] = mine
+                else:
+                    unit_own[1 + k // 2, i, j, m, :, columns] = mine
+                if k == 1:
+                    join_low[i // 2, i % 2, j, m] = theirs
+                else:
+                    join_out[k // 2, i, j, m] = theirs
 
     def join(k):
-        there = unit_own.at[1 + k, :, :, :, :, :, columns]
-        return links.send(join_out.at[k], there, links.core)
+        if k == 1:
+            return links.send(join_low, low_own.at[:, :, :, :, :, columns], links.core)
+        there = unit_own.at[1 + k // 2, :, :, :, :, columns]
+        return links.send(join_out.at[k // 2], there, links.core)
 
     def kv_rows(i, _):
         value = dot(seen[:, pl.ds(pl.multiple_of(256 * i, 256), 256)].T, dkv[...])
@@ -1273,30 +1484,6 @@
         place(0, i, dot(seen[near, pl.ds(pl.multiple_of(256 * i, 256), 256)].T, dq[...]))
         return 0
 
-    got_wo.wait()
-    wo_core.wait_recv()
-    wo.add_core(wo_r0)
-    wo.send_first()
-    lax.fori_loop(0, 4, kv_rows, 0)
-    join_v, join_k = join(2), join(1)
-    for one, got in zip(downs + ups, got_down + got_up):
-        one.turn_second(*got)
-    got_small.wait()
-    small.send()
-    join_v.wait_recv()
-    unit_v.send_first()
-    join_k.wait_recv()
-    unit_k.send_first()
-    got_dq.wait()
-    lax.fori_loop(0, 4, q_rows, 0)
-    join_q = join(0)
-    got_wskip = load(wskip_in, wide_buf)
-    wo.turn_first()
-    join_q.wait_recv()
-    unit_q.send_first()
-
-    got_wq.wait()
-
     def chip_part(at):
         rows = pl.ds(at, 256)
         return dot_nt(dq[rows, :], wq[...]) + dot_nt(dkv[rows, :], wkv[...])
@@ -1306,25 +1493,11 @@
         chip_out[pl.ds(at, 256), :] = chip_part(FRAMES + at).astype(BF16)
         return 0
 
-    lax.fori_loop(0, 2, other_frames, 0)
-    chip_core = links.send(chip_out, chip_in, links.core)
-    small.turn()
-
     def own_frames(i, _):
         at = pl.multiple_of(256 * i, 256)
         chip_own[pl.ds(at, 256), :] = chip_part(at)
         return 0
 
-    lax.fori_loop(0, 2, own_frames, 0)
-    for one in downs:
-        one.turn_third()
-
-    halo_y.wait_recv()
-    halo_rest = links.send(part, part, links.core)
-    chip_core.wait_recv()
-    got_stem.wait()
-    got_grad.wait()
-    halo_rest.wait_recv()
     gains = gain[0:1, :]
 
     def norm_rows(i, total):
@@ -1348,15 +1521,8 @@
         low[rows, :] = (grad[rows, :] + inverse * inner).astype(BF16)
         return total + jnp.sum(upstream * unit_value, axis=0, keepdims=True)
 
-    total = lax.fori_loop(0, 4, norm_rows, jnp.zeros((1, D), F32))
-    gain_steps[0] = jnp.concatenate([total[:, 128 * i : 128 * (i + 1)] for i in range(8)], axis=0)
-    gain_sum.send()
-    got_joint.wait()
-
-    skip_core = []
-    for q in range(SKIPS):
-
-        def skip_rows(i, _, q=q):
+    def skip_part(q):
+        def skip_rows(i, _):
             value = dot(
                 joint[pl.ds(pl.multiple_of(512 * i, 512), 512), :],
                 low[:, SKIP_COLS * q : SKIP_COLS * (q + 1)],
@@ -1366,93 +1532,154 @@
                     for half in range(2):
                         at = 256 * j + 128 * m + 32 * half
                         first, second = value[at : at + 32], value[at + 64 : at + 96]
-                        skip_own[2 * q + half, i // 2, i % 2, j, m] = jnp.where(c == 0, first, second)
-                        skip_out[2 * q + half, i // 2, i % 2, j, m] = jnp.where(c == 0, second, first)
+                        skip_own[2 * q + half, i, j, m] = jnp.where(c == 0, first, second)
+                        skip_out[2 * q + half, i, j, m] = jnp.where(c == 0, second, first)
             return 0
 
         lax.fori_loop(0, 4, skip_rows, 0)
         both = pl.ds(2 * q, 2)
-        skip_core.append(links.send(skip_out.at[both], skip_r0.at[both], links.core))
-        if q > 0:
-            skip_core[q - 1].wait_recv()
-            for half in range(2):
-                skips[q - 1][half].add_core(skip_r0.at[2 * (q - 1) + half])
-                skips[q - 1][half].send_first()
-    q = SKIPS - 1
-    skip_core[q].wait_recv()
-    for half in range(2):
-        skips[q][half].add_core(skip_r0.at[2 * q + half])
-        skips[q][half].send_first()
-
-    got_wskip.wait()
+        return links.send(skip_out.at[both], skip_r0.at[both], links.core)
+
+    def skip_begin(q, copy):
+        copy.wait_recv()
+        for half in range(2):
+            skips[q][half].add_core(skip_r0.at[2 * q + half])
+            skips[q][half].send_first()
 
     def joined_part(i):
         value = dot_nt(low[...], wide_buf[pl.ds(256 * i, 256), :]).astype(BF16)
         out = o_in if i < 4 else o_skip
         out[:, pl.ds(256 * (i % 4), 256)] = value
 
-    unit_v.turn_first()
+    got_wo.wait()
+    wo_core.wait_recv()
+    wo.add_core(wo_r0)
+    wo.send_first()
+    lax.fori_loop(0, 4, kv_rows, 0)
+    join_v, join_k = join(2), join(1)
+    for one, got in ((p0, got_p[0]), (p1, got_p[1]), (x0, got_x[0]), (x1, got_x[1])):
+        one.begin(*got)
+    rest_q.begin(*got_q)
+    rest_z.begin(*got_z)
+    got_small.wait()
+    small.send()
+    join_v.wait_recv()
+    unit_v.send_first()
+    join_k.wait_recv()
+    unit_k.send_first()
+    got_dq.wait()
+    lax.fori_loop(0, 4, q_rows, 0)
+    join_q = join(0)
+    got_wskip = load(wskip_in, wide_buf)
+    got_wq.wait()
+    lax.fori_loop(0, 2, other_frames, 0)
+    chip_core = links.send(chip_out, chip_in, links.core)
+    join_q.wait_recv()
+    unit_q.send_first()
+    lax.fori_loop(0, 2, own_frames, 0)
+    halo_y.wait_recv()
+    halo_rest = links.send(part, part, links.core)
+    small.turn()
+    chip_core.wait_recv()
+    got_stem.wait()
+    got_grad.wait()
+    halo_rest.wait_recv()
+    total = lax.fori_loop(0, 4, norm_rows, jnp.zeros((1, D), F32))
+    gain_steps[0] = jnp.concatenate(
+        [total[:, 128 * i : 128 * (i + 1)] for i in range(8)], axis=0
+    )
+    gain_sum.send()
+    got_joint.wait()
+    wo.turn_first()
+    p0.turn_third()
+    skip_core0 = skip_part(0)
+    skip_core1 = skip_part(1)
+    rest_q.turn_third()
+    skip_begin(0, skip_core0)
+    skip_core2 = skip_part(2)
+    p1.turn_third()
+    skip_begin(1, skip_core1)
+    skip_core3 = skip_part(3)
+    rest_z.turn_third()
+    skip_begin(2, skip_core2)
+    skip_begin(3, skip_core3)
+    got_wskip.wait()
     joined_part(0)
-    for one in ups:
-        one.turn_third()
     joined_part(1)
+    gain_sum.turn()
     joined_part(2)
-    gain_sum.turn()
-    small.turn()
     joined_part(3)
-    unit_q.turn_first()
-    unit_k.turn_first()
+    x0.turn_third()
     joined_part(4)
-    gain_sum.turn()
-    small.turn()
-    wo.turn_second()
     joined_part(5)
     joined_part(6)
-    for one in downs:
-        one.finish()
     joined_part(7)
+    unit_q.turn_first()
+    p0.turn_fourth()
+    skips[0][1].turn_first()
+    unit_v.turn_first()
+    x1.turn_third()
+    small.turn()
+    rest_q.finish()
+    skips[1][1].turn_first()
+    p1.turn_fourth()
+    skips[2][1].turn_first()
+    wo.turn_second()
+    skips[3][1].turn_first()
+    rest_z.finish()
+    p0.finish()
+    skips[0][0].turn_first()
+    p1.finish()
+    unit_k.turn_first()
+    skips[1][0].turn_first()
+    x0.turn_fourth()
+    unit_v.turn_second()
+    small.turn()
+    skips[2][0].turn_first()
+    wo.turn_third()
+    skips[0][0].turn_second()
+    x0.finish()
+    x1.turn_fourth()
+    take_up()
+    skips[3][0].turn_first()
     gain_sum.turn()
+    unit_v.turn_third()
+    x1.finish()
+    wo.turn_fourth()
     small.turn()
-    for one in ups:
-        one.finish()
-    for q in range(SKIPS):
-        skips[q][1].turn_first()
-    unit_v.turn_second()
+    unit_k.turn_second()
+    skips[1][0].turn_second()
+    unit_q.turn_second()
+    skips[0][0].finish()
+    wo.finish()
+    skips[2][0].turn_second()
+    skips[0][1].turn_second()
+    unit_v.turn_fourth()
+    skips[3][0].turn_second()
     gain_sum.turn()
+    skips[1][1].turn_second()
     small.turn()
-    wo.turn_third()
-    unit_q.turn_second()
-    for q in range(SKIPS):
-        skips[q][0].turn_first()
-    unit_k.turn_second()
-    unit_v.turn_third()
-    up_last[0].wait_recv()
-    for b in range(16):
-        at = pl.multiple_of(256 * b + 128 * (1 - c), 128)
-        o_up[:, pl.ds(at, 128)] = up_in_last[:, 128 * b : 128 * (b + 1)]
+    skips[2][1].turn_second()
+    skips[1][0].finish()
+    unit_v.finish()
+    skips[3][1].turn_second()
+    unit_q.turn_third()
+    unit_k.turn_third()
+    skips[2][0].finish()
     gain_sum.turn()
-    wo.finish()
-    unit_q.turn_third()
-    for q in range(SKIPS):
-        skips[q][1].turn_second()
-    unit_v.finish()
-    unit_k.turn_third()
-    for q in range(SKIPS):
-        skips[q][0].turn_second()
+    skips[0][1].finish()
+    unit_q.turn_fourth()
+    skips[3][0].finish()
+    skips[1][1].finish()
     unit_q.finish()
-    for q in range(SKIPS):
-        skips[q][1].turn_third()
     unit_k.finish()
-    for q in range(SKIPS):
-        skips[q][0].turn_third()
-    for q in range(SKIPS):
-        skips[q][1].finish()
-    for q in range(SKIPS):
-        skips[q][0].finish()
+    gain_sum.turn()
+    skips[2][1].finish()
+    skips[3][1].finish()
     links.drain()
 
 
-def tail(down, down_came, up, up_came, wo, small, dq, dkv, seen, wqkv, joint, stem, grad, gain, wskip):
+def tail(late, wo, small, dq, dkv, seen, wqkv, joint, stem, grad, gain, wskip):
     hbm, vm = pl.BlockSpec(memory_space=HBM), pl.BlockSpec(memory_space=VMEM)
     n_small = small.shape[0]
     out_shape = [
@@ -1469,7 +1696,7 @@
     low = lambda *shape: pltpu.VMEM(shape, BF16)
     full = lambda *shape: pltpu.VMEM(shape, F32)
     skip = (ROWS, SKIP_COLS)
-    copies = 104
+    copies = 116
     scratch = [
         low(CHIP, WIDTH),
         low(CHIP + HALO, D),
@@ -1487,42 +1714,53 @@
         low(HALF, D),
         low(HALO + 2 * EDGE, D),
         low(FRAMES, D),
-        low(2, 2, 2, 64, D),
-        low(2, 2, 2, 64, D),
-        low(2, 2, 64, D),
-        low(2, 64, D),
-        low(2, 2, 2, 32, 2 * D),
-        low(2, 2, 2, 32, 2 * D),
-        low(2, 2, 32, 2 * D),
-        low(2, 32, 2 * D),
+        low(2, 2, 2, 2, ROWS, D),
+        low(2, 2, 2, ROWS, D),
+        low(2, 2, ROWS, D),
+        low(2, ROWS, D),
+        low(ROWS, D),
+        low(2, 2, 2, 2, ROWS, WIDTH),
+        low(2, 4, 64, P_COLS),
+        low(2, 4, 64, P_COLS),
+        low(2, 6, 64, P_COLS),
+        low(2, 2, 128, D - P_COLS),
+        low(2, 2, 128, D - P_COLS),
+        low(2, 128, D - P_COLS),
+        low(128, D - P_COLS),
+        low(2, 4, 32, X_COLS),
+        low(2, 4, 32, X_COLS),
+        low(2, 6, 32, X_COLS),
+        low(2, 2, 64, 2 * D - X_COLS),
+        low(2, 2, 64, 2 * D - X_COLS),
+        low(2, 64, 2 * D - X_COLS),
+        low(64, 2 * D - X_COLS),
         full(32, 2 * D),
         full(32, 2 * D),
-        low(4, 2, 2, 2, 2, ROWS, D),
-        low(4, 2, 2, 2, ROWS, D),
+        low(3, 4, 2, 2, ROWS, D),
+        low(3, 4, 2, ROWS, D),
+        low(3, 4, ROWS, D),
+        low(3, 6, ROWS, D),
         low(4, 2, 2, ROWS, D),
-        low(4, 2, ROWS, D),
-        low(4, ROWS, D),
-        low(2, 2, 2, 2, ROWS, D),
-        low(3, 2, 2, 2, 2, ROWS, WIDTH),
-        low(2 * SKIPS, 2, 2, 2, 2, *skip),
-        low(2 * SKIPS, 2, 2, 2, 2, *skip),
-        low(2 * SKIPS, 2, 2, 2, 2, *skip),
-        low(2 * SKIPS, 2, 2, 2, *skip),
-        low(2 * SKIPS, 2, 2, *skip),
-        low(2 * SKIPS, 2, *skip),
-        low(2 * SKIPS, *skip),
+        low(2, 4, 2, 2, ROWS, WIDTH),
+        low(2 * SKIPS, 4, 2, 2, *skip),
+        low(2 * SKIPS, 4, 2, 2, *skip),
+        low(2 * SKIPS, 4, 2, 2, *skip),
+        low(2 * SKIPS, 4, 2, *skip),
+        low(2 * SKIPS, 4, *skip),
+        low(2 * SKIPS, 3, *skip),
+        full(64, X_COLS),
         full(5, n_small, 128),
         full(5, n_small, 128),
         full(5, 8, 128),
         full(5, 8, 128),
-        pltpu.SemaphoreType.DMA((24,)),
+        pltpu.SemaphoreType.DMA((28,)),
         pltpu.SemaphoreType.DMA((copies,)),
         pltpu.SemaphoreType.DMA((copies,)),
     ]
     return pl.pallas_call(
         tail_kernel,
         out_shape=out_shape,
-        in_specs=[hbm] * 13 + [vm, hbm],
+        in_specs=[hbm] * 17 + [vm, hbm],
         out_specs=[vm] * 9,
         scratch_shapes=scratch,
         name="tail",
@@ -1533,11 +1771,9 @@
             collective_id=0, has_side_effects=True, vmem_limit_bytes=63 << 20
         ),
     )(
-        down.reshape(2, 2, 128, D),
-        down_came.reshape(2, 2, 128, D),
-        up.reshape(2, 2, 64, 2 * D),
-        up_came.reshape(2, 2, 64, 2 * D),
-        wo.reshape(2, 2, 2, 2, 2, 32, D),
+        *late[:6],
+        *[value.reshape(2, 2, 64, 2 * D - X_COLS) for value in late[6:]],
+        wo.reshape(4, 2, 2, 2, 32, D),
         small,
         dq,
         dkv,
@@ -1626,7 +1862,7 @@
     stem_out, normed_seen, q, kv, joint = front(first, second_in, w_skip, gain_first, w_qkv)
     attended, attended_t, lse = attend(q, kv, seg_ids, frame_valid, 128, 256, heads)
     bias = lax.dynamic_index_in_dim(b_up.astype(F32).reshape(16, 2, 128), c, 1, keepdims=False)
-    output, middle_grad, grad_heads, out_grad, down_sum, down_away, up_sum, up_away, small = middle(
+    output, middle_grad, grad_heads, out_grad, small, *sums = middle(
         attended,
         stem_out,
         w_out,
@@ -1637,15 +1873,14 @@
         jnp.broadcast_to(b_down.astype(F32), (8, D)),
         cot,
     )
-    down_came, up_came = swap_x(down_away), swap_chip(up_away)
+    late = []
+    for here, away, swap in zip(sums[::2], sums[1::2], (swap_x, swap_chip, swap_chip, swap_x)):
+        late += [here, swap(away)]
     dq, dkv, output = attend_back(
         q, kv, grad_heads, attended_t, lse, seg_ids, frame_valid, output, 128, 256, heads
     )
     *results, small_sum, gain_sum = tail(
-        down_sum,
-        down_came,
-        up_sum,
-        up_came,
+        late,
         out_grad,
         small,
         dq,

time: 260 us -> 257 us (0.988)
  Pallas kernels: 249 us -> 244 us
    pallas_call x1, Pallas kernels: 98.5 us -> 89.3 us  [tail(): pl.pallas_call(tail_kernel, out_shape=out_shape, in_specs=[hbm] * 17 + [v...]
    pallas_call x1, Pallas kernels: 29.1 us -> 33.3 us  [attend_back(): pl.pallas_call(functools.partial(attend_back_kernel, bq, bk, heads), out_...]
    pallas_call x1, Pallas kernels: 21.6 us -> 24.7 us  [attend(): pl.pallas_call(functools.partial(attend_kernel, bq, bk, heads), out_shape...]
  transfers between devices with their start and end apart: 2 -> 4, of which waited for: 0 -> 0; matrix products, arithmetic and copies ran while one was open for 0% -> 0% of each run, Pallas kernels for 11% -> 13%
where the time goes in v1:
time: 257 us; the launch traced here: 256 us
  Pallas kernels  244 us (95%)
  local copies, waits for them, and re-layouts  6.55 us (3%)
  starting transfers between devices  4.12 us (2%)
    pallas_call x1, Pallas kernels, tail(): pl.pallas_call(tail_kernel, out_shape=out_shape, in_specs=[hbm] * 17 + [v...  89.3 us
    pallas_call x1, Pallas kernels, middle(): pl.pallas_call(middle_kernel, out_shape=[jax.ShapeDtypeStruct((FRAMES, D)...  63.8 us
    pallas_call x1, Pallas kernels, attend_back(): pl.pallas_call(functools.partial(attend_back_kernel, bq, bk, heads), out_...  33.3 us
    pallas_call x1, Pallas kernels, front(): pl.pallas_call(front_kernel, out_shape=[jax.ShapeDtypeStruct((FRAMES, D),...  28.5 us
    pallas_call x1, Pallas kernels, attend(): pl.pallas_call(functools.partial(attend_kernel, bq, bk, heads), out_shape...  24.7 us
  transfers between devices with their start and end apart: 4, of which 0 were waited for; matrix products, arithmetic and copies ran while one was open for 0% of the time, Pallas kernels for 13%

profile of v1, /device:TPU:0, one launch (start us, length us, event | category | flops | bytes accessed | tf_op | source)
XLA Modules:
  0.0 256.3 jit_solution(10548413537916648929)
XLA Ops:
  0.7 0.7 dynamic-slice_convert_fusion
  1.4 1.3 broadcast_in_dim.25.refs_3_.refs_17_
  2.7 28.5 %front.1 = (f32[512,1024]{1,0:T(8,128)}, bf16[1792,1024]{1,0:T(8,128)(2,1)}, bf16[1024,512]{1,0:T(8,128)(2,1)}, bf16[1792,1024]{1,0:T(8,128)(2,1)}, bf16[2048,512]{1,0:T(8,128)(2,1)}) custom-call(bf16[512,1024]{1,0:T(8,128)(2,1)} %bitcast.22, bf16[512,1024]{1,0:T(8,128)(2,1)} %bitcast.23, bf16[2048,1024]{1,0:T(8,128)(2,1)} %refs_18_.1, ...), custom_call_target="tpu_custom_call" | custom-call | flops 8000000000 | bytes 24000000 | tf_op jit(solution)/shard_map/front/pallas_call | solution.py:236
  31.1 0.0 copy-start
  31.2 0.0 copy-start.1
  31.2 24.7 %attend.1 = (bf16[1024,512]{1,0:T(8,128)(2,1)}, bf16[512,1024]{1,0:T(8,128)(2,1)}, f32[4,2048]{1,0:T(4,128)}) custom-call(s32[1,2048]{1,0:T(1,128)} %seg.3, bf16[1024,512]{1,0:T(8,128)(2,1)} %get-tuple-element.53.q_in, bf16[1792,1024]{1,0:T(8,128)(2,1)} %get-tuple-element.54.kv_in, s32[1,2048]{1,0:T(1,128)} %seg.3, s32[1,2048]{1,0:T(1,128)} %valid.3), custom_call_target="tpu_custom_call" | custom-call | flops 8000000000 | bytes 8000000 | tf_op jit(solution)/shard_map/attend/pallas_call | solution.py:464
  55.9 0.0 copy-done
  55.9 0.6 broadcast_in_dim.26.refs_3_
  56.5 0.0 copy-done.1
  56.5 0.6 broadcast_in_dim.29.refs_7_
  57.1 0.6 broadcast_in_dim.28.refs_6_
  57.8 63.8 %middle.1 = (bf16[512,1024]{1,0:T(8,128)(2,1)}, f32[512,1024]{1,0:T(8,128)}, bf16[1024,512]{1,0:T(8,128)(2,1)}, bf16[1024,1024]{1,0:T(8,128)(2,1)}, f32[48,128]{...) custom-call(bf16[1024,512]{1,0:T(8,128)(2,1)} %get-tuple-element.55., ...), custom_call_target="tpu_custom_call" | custom-call | flops 28000000000 | bytes 40000000 | tf_op jit(solution)/shard_map/middle/pallas_call | solution.py:1162
  121.6 0.5 collective-permute-start.3
  122.1 0.0 collective-permute-start.1
  122.1 1.6 collective-permute-start
  123.7 2.0 collective-permute-start.2
  125.7 33.3 %attend_back.1 = (bf16[1024,512]{1,0:T(8,128)(2,1)}, bf16[1792,1024]{1,0:T(8,128)(2,1)}, bf16[512,1024]{1,0:T(8,128)(2,1)}) custom-call(s32[1,2048]{1,0:T(1,128)} %seg.3, bf16[1024,512]{1,0:T(8,128)(2,1)} %get-tuple-element.53.q_in, bf16[1792,1024]{1,0:T(8,128)(2,1)} %get-tuple-element.54.kv_in, bf16[1024,512]{1,0:T(8,128)(2,1)} %get-tuple-element.57.grad_in, ...), custom_call_target="tpu_custom_call" | custom-call | flops 20000000000 | bytes 16000000 | tf_op jit(solution)/shard_map/attend_back/pallas_call | solution.py:645
  159.0 0.0 collective-permute-done.3
  159.0 0.0 collective-permute-done.1.refs_3_
  159.0 0.0 collective-permute-done.refs_1_
  159.0 0.0 collective-permute-done.2.refs_5_
  159.0 0.0 copy-start.2
  159.1 0.9 copy-done.2
  159.9 89.3 %tail.1 = (bf16[512,1024]{1,0:T(8,128)(2,1)}, bf16[512,1024]{1,0:T(8,128)(2,1)}, f32[128,1024]{1,0:T(8,128)}, f32[32,4096]{1,0:T(8,128)}, f32[32,3072]{1,0:T(8,1...) custom-call(bf16[4,128,640]{2,1,0:T(8,128)(2,1)} %get-tuple-element.62.refs_0_, ...), custom_call_target="tpu_custom_call" | custom-call | flops 16999999488 | bytes 60000000 | tf_op jit(solution)/shard_map/tail/pallas_call | solution.py:1760
  249.2 4.6 %finish.1 = (bf16[512,1024]{1,0:T(8,128)(2,1)}, bf16[512,1024]{1,0:T(8,128)(2,1)}, f32[128,1024]{1,0:T(8,128)}, f32[32,4096]{1,0:T(8,128)}, f32[32,3072]{1,0:T(8...) custom-call(bf16[512,1024]{1,0:T(8,128)(2,1)} %get-tuple-element.77.refs_0_, ...), custom_call_target="tpu_custom_call" | custom-call | tf_op jit(solution)/shard_map/finish/pallas_call | solution.py:1814
  253.8 1.2 slice_bitcast_fusion.1
  255.0 1.3 slice_bitcast_fusion
Async XLA Ops:
  31.1 24.7 %copy-start = (bf16[1024]{0:T(1024)(128)(2,1)S(1)}, bf16[1024]{0:T(1024)(128)(2,1)}, u32[]{:S(2)}) copy-start(bf16[1024]{0:T(1024)(128)(2,1)} %param.22) | copy-start | bytes 6148
  31.2 25.4 %copy-start.1 = (bf16[1024]{0:T(1024)(128)(2,1)S(1)}, bf16[1024]{0:T(1024)(128)(2,1)}, u32[]{:S(2)}) copy-start(bf16[1024]{0:T(1024)(128)(2,1)} %param.26) | copy-start | bytes 6148
  121.6 37.4 %collective-permute-start.3 = (bf16[2,128,512]{2,1,0:T(8,128)(2,1)}, bf16[2,128,512]{2,1,0:T(8,128)(2,1)}, u32[]{:S(2)}, u32[]{:S(2)}) collective-permute-start(bf16[2,128,512]{2,1,0:T(8,128)(2,1)} %get-tuple-element.69), channel_id=1, source_target_pairs={{0,4},{4,0},{8,12},{12,8},{16,20},{20,16},{24,28},{28,24},{1,5},{5... | collective-permute-start | bytes 786440 | tf_op jit(solution)/shard_map/ppermute | solution.py:1833
  122.1 37.0 %collective-permute-start.1 = (bf16[2,2,128,384]{3,2,1,0:T(8,128)(2,1)}, bf16[2,2,128,384]{3,2,1,0:T(8,128)(2,1)}, u32[]{:S(2)}, u32[]{:S(2)}) collective-permute-start(bf16[2,2,128,384]{3,2,1,0:T(8,128)(2,1)} %get-tuple-element.65), channel_id=1, source_target_pairs={{0,2},{1,3},{2,0},{3,1},{4,6},{5,7},{6,4},{7,5},{8,10},{9,11},{10,... | collective-permute-start | bytes 1179656 | tf_op jit(solution)/shard_map/ppermute | solution.py:1837
  122.1 37.0 %collective-permute-start = (bf16[4,128,640]{2,1,0:T(8,128)(2,1)}, bf16[4,128,640]{2,1,0:T(8,128)(2,1)}, u32[]{:S(2)}, u32[]{:S(2)}) collective-permute-start(bf16[4,128,640]{2,1,0:T(8,128)(2,1)} %get-tuple-element.63), channel_id=1, source_target_pairs={{0,4},{4,0},{8,12},{12,8},{16,20},{20,16},{24,28},{28,24},{1,5},{5... | collective-permute-start | bytes 1966088 | tf_op jit(solution)/shard_map/ppermute | solution.py:1833
  123.7 35.3 %collective-permute-start.2 = (bf16[4,64,1536]{2,1,0:T(8,128)(2,1)}, bf16[4,64,1536]{2,1,0:T(8,128)(2,1)S(1)}, u32[]{:S(2)}, u32[]{:S(2)}) collective-permute-start(bf16[4,64,1536]{2,1,0:T(8,128)(2,1)} %get-tuple-element.67), channel_id=1, source_target_pairs={{0,2},{1,3},{2,0},{3,1},{4,6},{5,7},{6,4},{7,5},{8,10},{9,11},{10,... | collective-permute-start | bytes 2359304 | tf_op jit(solution)/shard_map/ppermute | solution.py:1837
  159.0 0.9 copy-start.2

commit v2 on v1

--- a/solution.py
+++ b/solution.py
@@ -159,7 +159,7 @@
     links.greet(near=True)
     for copy in got:
         copy.wait()
-    gains = gain[0:1, :]
+    gains = gain[...].astype(F32).reshape(1, D)
     base = jnp.where(y == 0, EDGE, 0) + HALF * c
 
     def piece(i, chip):
@@ -810,6 +810,38 @@
         self.done(value + self.came[3][...].astype(F32))
 
 
+class HighUnit:
+    def __init__(self, links, own, came, done):
+        self.links, self.own, self.came, self.done = links, own, came, done
+
+    def begin(self, *loads):
+        for copy in loads:
+            copy.wait()
+        n = self.links
+        for k in range(2):
+            for i in range(2):
+                add_into(self.own.at[k, i], self.came[0].at[k, i])
+        self.second = n.send(self.own.at[:, 1 - n.x], self.came[1], n.over_x)
+
+    def turn_second(self):
+        self.second.wait_recv()
+        n = self.links
+        for k in range(2):
+            add_into(self.own.at[k, n.x], self.came[1].at[k])
+        self.third = n.send(self.own.at[:, n.x, 1 - n.y], self.came[2], n.over_y)
+
+    def turn_third(self):
+        self.third.wait_recv()
+        n = self.links
+        add_into(self.own.at[:, n.x, n.y], self.came[2])
+        self.fourth = n.send(self.own.at[1 - n.high, n.x, n.y], self.came[3], n.over_high)
+
+    def finish(self):
+        self.fourth.wait_recv()
+        n = self.links
+        self.done(self.own[n.high, n.x, n.y].astype(F32) + self.came[3][...].astype(F32))
+
+
 class LateUnit(Unit):
     def chip(self, at):
         return self.own.at[at]
@@ -872,6 +904,7 @@
 P_COLS = 640
 X_STEPS = 6
 X_COLS = STEP * X_STEPS
+UP_BLOCKS = [2 * i + j for i in (0, 2, 3, 5, 6, 7, 1, 4) for j in (0, 1)]
 
 
 def middle_kernel(*refs):
@@ -886,8 +919,8 @@
         bias_down,
         cot_in,
     ) = refs[:9]
-    o_out, o_grad, o_heads, o_wo, o_small = refs[9:14]
-    o_p, o_p_away, o_q, o_q_away, o_x, o_x_away, o_z, o_z_away = refs[14:22]
+    o_out, o_grad, o_heads, o_small = refs[9:13]
+    o_p, o_p_away, o_q, o_q_away, o_x, o_x_away, o_z, o_z_away, o_wo, o_wo_away = refs[13:23]
     (
         att,
         att_came,
@@ -919,10 +952,11 @@
         z_send,
         z_keep,
         z_came,
+        biases,
         loads,
         sends,
         recvs,
-    ) = refs[22:]
+    ) = refs[23:]
     links = Links(sends, recvs)
     x, y, c = links.x, links.y, links.c
     loading = []
@@ -955,7 +989,7 @@
     got_wout.wait()
     got_stem.wait()
     att_core.wait_recv()
-    gains = gain[0:1, :]
+    gains = gain[...].astype(F32).reshape(1, D)
     second_core = []
     for part in range(2):
         rows = pl.ds(256 * part, 256)
@@ -971,6 +1005,7 @@
             links.send(second.at[rows], second.at[pl.ds(FRAMES + 256 * part, 256)], links.core)
         )
     second_t[:, :FRAMES] = second[own, :].T
+    biases[...] = bias_up[...].astype(F32)
     out_sum[...] = jnp.zeros_like(out_sum)
     grad_sum[...] = jnp.zeros_like(grad_sum)
     o_small[...] = jnp.zeros_like(o_small)
@@ -997,7 +1032,7 @@
 
     def feed_step(i, _):
         up, down = ups[i], downs[i]
-        bias = bias_up[0:1, pl.ds(pl.multiple_of(STEP * i, STEP), STEP)]
+        bias = jnp.concatenate([biases[pl.ds(4 * i + 2 * j + c, 1), :] for j in (0, 1)], axis=1)
         total = jnp.zeros((1, STEP), F32)
         for half in (own, other):
             hidden = dot(second[half, :], up) + bias
@@ -1034,17 +1069,20 @@
 
         value = dot(second_t[...], hidden_grad[...]).astype(BF16)
 
-        @pl.when(i < X_STEPS)
+        over_z = (lax.rem(i, 3) == 1) & (i < 6)
+
+        @pl.when(jnp.logical_not(over_z))
         def _():
+            j = i - jnp.where(i > 1, 1, 0) - jnp.where(i > 4, 1, 0)
             for k in range(4):
                 first, last = value[256 * k : 256 * k + 128], value[256 * k + 128 : 256 * (k + 1)]
-                x_send[i, k] = jnp.where(x == 0, last, first)
-                x_keep[i, k] = jnp.where(x == 0, first, last)
-            x_copy(i).start()
-
-        @pl.when(i >= X_STEPS)
+                x_send[j, k] = jnp.where(x == 0, last, first)
+                x_keep[j, k] = jnp.where(x == 0, first, last)
+            x_copy(j).start()
+
+        @pl.when(over_z)
         def _():
-            j = i - X_STEPS
+            j = i // 4
             for k in range(2):
                 first, last = value[512 * k : 512 * k + 256], value[512 * k + 256 : 512 * (k + 1)]
                 z_send[j, k] = jnp.where(links.low == 0, last, first)
@@ -1090,8 +1128,21 @@
         swap_out.at[2, :, pl.ds(0, WIDTH)], swap_in.at[2, :, pl.ds(0, WIDTH)], links.core
     )
     o_heads[own, :] = dot_nt(low[...], wout[mine, :]).astype(BF16)
-    o_wo[mine, :] = dot_tn(att[...], low[...]).astype(BF16)
-    o_wo[theirs, :] = dot_tn(att_came[...], low[...]).astype(BF16)
+
+    def out_grad(high, value):
+        value = value.astype(BF16)
+        for low_bit in range(2):
+            for i in range(2):
+                for j in range(2):
+                    at = 256 * low_bit + 128 * i + 64 * j
+                    first, last = value[at : at + 32], value[at + 32 : at + 64]
+                    rows = pl.multiple_of(256 * high + at // 2, 32)
+                    second_t[pl.ds(rows, 32), :] = jnp.where(c == 0, first, last)
+                    second_t[pl.ds(FRAMES + rows, 32), :] = jnp.where(c == 0, last, first)
+
+    out_grad(c, dot_tn(att[...], low[...]))
+    out_grad(1 - c, dot_tn(att_came[...], low[...]))
+    wo_core = links.send(second_t.at[other], second.at[other], links.core)
     out_core.wait_recv()
 
     def out_rows(i, _):
@@ -1099,7 +1150,7 @@
         o_out[rows, :] = (
             stem[rows, :]
             + (out_sum[rows, :] + swap_in[1, rows, :].astype(F32))
-            + bias_down[0:1, :]
+            + bias_down[...].astype(F32).reshape(1, D)
         ).astype(BF16)
         return 0
 
@@ -1147,6 +1198,15 @@
             o_z_away[k, :, columns(i)] = jnp.where(x == 0, value[128:], value[:128])
         return 0
 
+    wo_core.wait_recv()
+    for high in range(2):
+        for i in range(2):
+            for j in range(2):
+                for out, low_bit in ((o_wo, links.low), (o_wo_away, 1 - links.low)):
+                    at = 256 * high + 128 * low_bit + 64 * i + 32 * j
+                    rows = pl.ds(pl.multiple_of(at, 32), 32)
+                    came = pl.ds(pl.multiple_of(FRAMES + at, 32), 32)
+                    out[high, i, j] = second_t[rows, :] + second[came, :]
     lax.fori_loop(0, STEPS, add_p, 0)
     lax.fori_loop(0, 4, add_q, 0)
     lax.fori_loop(0, X_STEPS, add_x, 0)
@@ -1158,22 +1218,22 @@
     hbm, vm = pl.BlockSpec(memory_space=HBM), pl.BlockSpec(memory_space=VMEM)
     low = lambda *shape: pltpu.VMEM(shape, BF16)
     full = lambda *shape: pltpu.VMEM(shape, F32)
-    copies = 28
+    copies = 29
     return pl.pallas_call(
         middle_kernel,
         out_shape=[
             jax.ShapeDtypeStruct((FRAMES, D), BF16),
             jax.ShapeDtypeStruct((FRAMES, D), F32),
             jax.ShapeDtypeStruct((CHIP, WIDTH), BF16),
-            jax.ShapeDtypeStruct((D, D), BF16),
             jax.ShapeDtypeStruct((48, 128), F32),
             *[jax.ShapeDtypeStruct((4, 128, P_COLS), BF16)] * 2,
             *[jax.ShapeDtypeStruct((2, 2, 128, D - P_COLS), BF16)] * 2,
             *[jax.ShapeDtypeStruct((4, 64, X_COLS), BF16)] * 2,
             *[jax.ShapeDtypeStruct((2, 128, 2 * D - X_COLS), BF16)] * 2,
+            *[jax.ShapeDtypeStruct((2, 2, 2, ROWS, D), BF16)] * 2,
         ],
         in_specs=[hbm] * 3 + [vm] + [hbm] * 2 + [vm] * 2 + [hbm],
-        out_specs=[vm] * 13,
+        out_specs=[vm] * 14,
         scratch_shapes=[
             low(FRAMES, WIDTH),
             low(FRAMES, WIDTH),
@@ -1197,6 +1257,7 @@
             *[low(4, 2, 128, D - P_COLS)] * 3,
             *[low(X_STEPS, 4, 128, STEP)] * 3,
             *[low(STEPS - X_STEPS, 2, 256, STEP)] * 3,
+            full(32, 128),
             pltpu.SemaphoreType.DMA((4 + 4 * STEPS,)),
             pltpu.SemaphoreType.DMA((copies,)),
             pltpu.SemaphoreType.DMA((copies,)),
@@ -1222,6 +1283,7 @@
         z_in,
         z_came,
         wo_in,
+        wo_came,
         small_in,
         dq_in,
         dkv_in,
@@ -1232,8 +1294,8 @@
         grad_in,
         gain,
         wskip_in,
-    ) = refs[:19]
-    o_in, o_skip, o_down, o_up, o_qkv, o_wo, o_wskip, o_small, o_gain = refs[19:28]
+    ) = refs[:20]
+    o_in, o_skip, o_down, o_up, o_qkv, o_wo, o_wskip, o_small, o_gain = refs[20:29]
     (
         dq,
         dkv,
@@ -1277,7 +1339,11 @@
         unit_r1,
         unit_r2,
         unit_r3,
-        wo_r0,
+        wo_own,
+        wo_r1,
+        wo_r2,
+        wo_r3,
+        wo_r4,
         join_out,
         skip_own,
         skip_out,
@@ -1293,7 +1359,7 @@
         loads,
         sends,
         recvs,
-    ) = refs[28:]
+    ) = refs[29:]
     links = Links(sends, recvs)
     y, c = links.y, links.c
     loading = []
@@ -1309,11 +1375,10 @@
     got_wkv = [load(head_columns(wqkv_in, 1 + i, c), wkv.at[:, pl.ds(WIDTH * i, WIDTH)]) for i in (0, 1)]
     got_far = load(dkv_in.at[far], dkv.at[far])
     links.greet()
-    wo_core = links.send(wo_in.at[:, :, :, 1 - c], wo_r0, links.core)
+    got_wo = [load(wo_in, wo_own), load(wo_came, wo_r1)]
     got_dq = load(dq_in, dq)
     got_near = load(dkv_in.at[near], dkv.at[near])
     got_seen = load(seen_in, seen)
-    got_wo = load(wo_in.at[:, :, :, c], unit_own.at[0])
     got_small = load(small_in, small_steps.at[0])
     got_p = [
         [
@@ -1356,21 +1421,21 @@
         pass_up(0, value)
 
     def to_up_mine(value):
-        for b in range(X_COLS // 128):
-            put_up(b, c, value[:, 128 * b : 128 * (b + 1)])
+        for t in range(X_COLS // 128):
+            put_up(UP_BLOCKS[t], c, value[:, 128 * t : 128 * (t + 1)])
 
     def to_up_rest(value):
         pass_up(X_COLS, jnp.where(c == 0, value[32:], value[:32]))
         mine = jnp.where(c == 0, value[:32], value[32:])
-        for b in range(X_COLS // 128, 16):
-            at = 128 * b - X_COLS
-            put_up(b, c, mine[:, at : at + 128])
+        for t in range(X_COLS // 128, 16):
+            at = 128 * t - X_COLS
+            put_up(UP_BLOCKS[t], c, mine[:, at : at + 128])
 
     def take_up():
         for copy in up_last:
             copy.wait_recv()
-        for b in range(16):
-            put_up(b, 1 - c, up_in_last[:, 128 * b : 128 * (b + 1)])
+        for t in range(16):
+            put_up(UP_BLOCKS[t], 1 - c, up_in_last[:, 128 * t : 128 * (t + 1)])
 
     up_last = []
 
@@ -1411,8 +1476,8 @@
         came = (unit_r1.at[k], unit_r2.at[k], unit_r3.at[k])
         return Unit(links, unit_own.at[k], came, room(ROWS, D), y_first, done)
 
-    wo = unit(0, False, to_wo)
-    unit_q, unit_v = unit(1, False, to_qkv(0)), unit(2, True, to_qkv(2))
+    wo = HighUnit(links, wo_own, (wo_r1, wo_r2, wo_r3, wo_r4), to_wo)
+    unit_q, unit_v = unit(0, False, to_qkv(0)), unit(1, True, to_qkv(2))
     unit_k = LowUnit(links, low_own, (low_r1, low_r2, low_r3, low_r4), None, False, to_qkv(1))
 
     def skip_unit(k, y_first, done):
@@ -1462,7 +1527,7 @@
                 if k == 1:
                     low_own[i // 2, i % 2, j, m, :, columns] = mine
                 else:
-                    unit_own[1 + k // 2, i, j, m, :, columns] = mine
+                    unit_own[k // 2, i, j, m, :, columns] = mine
                 if k == 1:
                     join_low[i // 2, i % 2, j, m] = theirs
                 else:
@@ -1471,7 +1536,7 @@
     def join(k):
         if k == 1:
             return links.send(join_low, low_own.at[:, :, :, :, :, columns], links.core)
-        there = unit_own.at[1 + k // 2, :, :, :, :, columns]
+        there = unit_own.at[k // 2, :, :, :, :, columns]
         return links.send(join_out.at[k // 2], there, links.core)
 
     def kv_rows(i, _):
@@ -1498,7 +1563,7 @@
         chip_own[pl.ds(at, 256), :] = chip_part(at)
         return 0
 
-    gains = gain[0:1, :]
+    gains = gain[...].astype(F32).reshape(1, D)
 
     def norm_rows(i, total):
         at = pl.multiple_of(128 * i, 128)
@@ -1551,10 +1616,7 @@
         out = o_in if i < 4 else o_skip
         out[:, pl.ds(256 * (i % 4), 256)] = value
 
-    got_wo.wait()
-    wo_core.wait_recv()
-    wo.add_core(wo_r0)
-    wo.send_first()
+    wo.begin(*got_wo)
     lax.fori_loop(0, 4, kv_rows, 0)
     join_v, join_k = join(2), join(1)
     for one, got in ((p0, got_p[0]), (p1, got_p[1]), (x0, got_x[0]), (x1, got_x[1])):
@@ -1577,6 +1639,7 @@
     join_q.wait_recv()
     unit_q.send_first()
     lax.fori_loop(0, 2, own_frames, 0)
+    wo.turn_second()
     halo_y.wait_recv()
     halo_rest = links.send(part, part, links.core)
     small.turn()
@@ -1590,11 +1653,10 @@
     )
     gain_sum.send()
     got_joint.wait()
-    wo.turn_first()
     p0.turn_third()
+    rest_q.turn_third()
     skip_core0 = skip_part(0)
     skip_core1 = skip_part(1)
-    rest_q.turn_third()
     skip_begin(0, skip_core0)
     skip_core2 = skip_part(2)
     p1.turn_third()
@@ -1613,73 +1675,71 @@
     joined_part(4)
     joined_part(5)
     joined_part(6)
+    unit_q.turn_first()
     joined_part(7)
-    unit_q.turn_first()
     p0.turn_fourth()
     skips[0][1].turn_first()
     unit_v.turn_first()
     x1.turn_third()
+    p1.turn_fourth()
+    skips[1][1].turn_first()
+    wo.turn_third()
     small.turn()
-    rest_q.finish()
-    skips[1][1].turn_first()
-    p1.turn_fourth()
     skips[2][1].turn_first()
-    wo.turn_second()
+    skips[0][0].turn_first()
     skips[3][1].turn_first()
-    rest_z.finish()
+    x0.turn_fourth()
     p0.finish()
-    skips[0][0].turn_first()
+    skips[1][0].turn_first()
     p1.finish()
     unit_k.turn_first()
-    skips[1][0].turn_first()
-    x0.turn_fourth()
+    skips[2][0].turn_first()
+    x0.finish()
     unit_v.turn_second()
     small.turn()
-    skips[2][0].turn_first()
-    wo.turn_third()
-    skips[0][0].turn_second()
-    x0.finish()
-    x1.turn_fourth()
-    take_up()
     skips[3][0].turn_first()
     gain_sum.turn()
+    skips[0][0].turn_second()
+    x1.turn_fourth()
+    rest_q.finish()
+    skips[1][0].turn_second()
+    rest_z.finish()
+    unit_q.turn_second()
     unit_v.turn_third()
+    skips[0][1].turn_second()
     x1.finish()
-    wo.turn_fourth()
-    small.turn()
+    wo.finish()
     unit_k.turn_second()
-    skips[1][0].turn_second()
-    unit_q.turn_second()
-    skips[0][0].finish()
-    wo.finish()
+    take_up()
+    skips[1][1].turn_second()
     skips[2][0].turn_second()
-    skips[0][1].turn_second()
+    skips[2][1].turn_second()
     unit_v.turn_fourth()
     skips[3][0].turn_second()
     gain_sum.turn()
-    skips[1][1].turn_second()
+    skips[3][1].turn_second()
     small.turn()
-    skips[2][1].turn_second()
+    unit_k.turn_third()
+    skips[0][0].finish()
     skips[1][0].finish()
+    unit_q.turn_third()
+    skips[0][1].finish()
+    skips[1][1].finish()
     unit_v.finish()
-    skips[3][1].turn_second()
-    unit_q.turn_third()
-    unit_k.turn_third()
+    unit_q.turn_fourth()
     skips[2][0].finish()
     gain_sum.turn()
-    skips[0][1].finish()
-    unit_q.turn_fourth()
+    skips[2][1].finish()
+    unit_q.finish()
     skips[3][0].finish()
-    skips[1][1].finish()
-    unit_q.finish()
+    skips[3][1].finish()
+    small.turn()
+    gain_sum.turn()
     unit_k.finish()
-    gain_sum.turn()
-    skips[2][1].finish()
-    skips[3][1].finish()
     links.drain()
 
 
-def tail(late, wo, small, dq, dkv, seen, wqkv, joint, stem, grad, gain, wskip):
+def tail(late, small, dq, dkv, seen, wqkv, joint, stem, grad, gain, wskip):
     hbm, vm = pl.BlockSpec(memory_space=HBM), pl.BlockSpec(memory_space=VMEM)
     n_small = small.shape[0]
     out_shape = [
@@ -1736,11 +1796,15 @@
         low(64, 2 * D - X_COLS),
         full(32, 2 * D),
         full(32, 2 * D),
-        low(3, 4, 2, 2, ROWS, D),
-        low(3, 4, 2, ROWS, D),
-        low(3, 4, ROWS, D),
-        low(3, 6, ROWS, D),
-        low(4, 2, 2, ROWS, D),
+        low(2, 4, 2, 2, ROWS, D),
+        low(2, 4, 2, ROWS, D),
+        low(2, 4, ROWS, D),
+        low(2, 6, ROWS, D),
+        low(2, 2, 2, ROWS, D),
+        low(2, 2, 2, ROWS, D),
+        low(2, 2, ROWS, D),
+        low(2, ROWS, D),
+        low(ROWS, D),
         low(2, 4, 2, 2, ROWS, WIDTH),
         low(2 * SKIPS, 4, 2, 2, *skip),
         low(2 * SKIPS, 4, 2, 2, *skip),
@@ -1760,7 +1824,7 @@
     return pl.pallas_call(
         tail_kernel,
         out_shape=out_shape,
-        in_specs=[hbm] * 17 + [vm, hbm],
+        in_specs=[hbm] * 18 + [vm, hbm],
         out_specs=[vm] * 9,
         scratch_shapes=scratch,
         name="tail",
@@ -1772,8 +1836,8 @@
         ),
     )(
         *late[:6],
-        *[value.reshape(2, 2, 64, 2 * D - X_COLS) for value in late[6:]],
-        wo.reshape(4, 2, 2, 2, 32, D),
+        *[value.reshape(2, 2, 64, 2 * D - X_COLS) for value in late[6:8]],
+        *late[8:],
         small,
         dq,
         dkv,
@@ -1789,17 +1853,17 @@
 
 def finish_kernel(count, *refs):
     ins, small, gain = refs[:count], refs[count], refs[count + 1]
-    outs, o_small = refs[count + 2 : 2 * count + 2], refs[2 * count + 2]
-    held, loads, stores = refs[2 * count + 3 : 3 * count + 3], refs[-2], refs[-1]
+    outs, smalls = refs[count + 2 : 2 * count + 2], refs[2 * count + 2 : 2 * count + 6]
+    held, loads, stores = refs[2 * count + 6 : 3 * count + 6], refs[-2], refs[-1]
     got = [pltpu.make_async_copy(a, b, loads.at[i]) for i, (a, b) in enumerate(zip(ins, held))]
     for copy in got:
         copy.start()
     device = lax.axis_index("rows") * 4 + lax.axis_index("seq")
-    o_small[0:1, :] = small[pl.ds(device, 1), :]
+    smalls[0][...] = small[pl.ds(device, 1), :]
     row, lane = device // 4, lax.rem(device, 4) * 32
     values = [gain[pl.ds(row, 1), :], small[pl.ds(32 + row, 1), :], small[pl.ds(40 + row, 1), :]]
-    for i, value in enumerate(values):
-        o_small[1 + i : 2 + i, :] = pltpu.roll(value, lax.rem(128 - lane, 128), 1)
+    for out, value in zip(smalls[1:], values):
+        out[...] = pltpu.roll(value, lax.rem(128 - lane, 128), 1)[:, :32]
     put = [pltpu.make_async_copy(a, b, stores.at[i]) for i, (a, b) in enumerate(zip(held, outs))]
     for copy, after in zip(got, put):
         copy.wait()
@@ -1815,10 +1879,10 @@
         functools.partial(finish_kernel, count),
         out_shape=[
             *[jax.ShapeDtypeStruct(a.shape, a.dtype) for a in results],
-            jax.ShapeDtypeStruct((8, 128), F32),
+            *[jax.ShapeDtypeStruct((1, size), F32) for size in (128, 32, 32, 32)],
         ],
         in_specs=[hbm] * count + [vm] * 2,
-        out_specs=[hbm] * count + [vm],
+        out_specs=[hbm] * count + [vm] * 4,
         scratch_shapes=[
             *[pltpu.VMEM(a.shape, a.dtype) for a in results],
             pltpu.SemaphoreType.DMA((count,)),
@@ -1827,6 +1891,10 @@
         name="finish",
         compiler_params=pltpu.CompilerParams(vmem_limit_bytes=63 << 20),
     )(*results, small, gain)
+
+
+def swap_low(value):
+    return lax.ppermute(value, "rows", [(r, r ^ 2) for r in range(8)])
 
 
 def swap_x(value):
@@ -1857,31 +1925,28 @@
     c = here % 2
     heads = H // 2
     first, second_in, cot = inputs[0], skip_feats[0], cotangent[0]
-    gain_first = jnp.broadcast_to(gain_one.astype(F32), (8, D))
-    gain_second = jnp.broadcast_to(gain_two.astype(F32), (8, D))
-    stem_out, normed_seen, q, kv, joint = front(first, second_in, w_skip, gain_first, w_qkv)
+    stem_out, normed_seen, q, kv, joint = front(first, second_in, w_skip, gain_one, w_qkv)
     attended, attended_t, lse = attend(q, kv, seg_ids, frame_valid, 128, 256, heads)
-    bias = lax.dynamic_index_in_dim(b_up.astype(F32).reshape(16, 2, 128), c, 1, keepdims=False)
-    output, middle_grad, grad_heads, out_grad, small, *sums = middle(
+    output, middle_grad, grad_heads, small, *sums = middle(
         attended,
         stem_out,
         w_out,
-        gain_second,
+        gain_two,
         w_up,
         w_down,
-        jnp.broadcast_to(bias.reshape(1, -1), (8, 2 * D)),
-        jnp.broadcast_to(b_down.astype(F32), (8, D)),
+        b_up.reshape(32, 128),
+        b_down,
         cot,
     )
     late = []
-    for here, away, swap in zip(sums[::2], sums[1::2], (swap_x, swap_chip, swap_chip, swap_x)):
+    swaps = (swap_x, swap_chip, swap_chip, swap_x, swap_low)
+    for here, away, swap in zip(sums[::2], sums[1::2], swaps):
         late += [here, swap(away)]
     dq, dkv, output = attend_back(
         q, kv, grad_heads, attended_t, lse, seg_ids, frame_valid, output, 128, 256, heads
     )
     *results, small_sum, gain_sum = tail(
         late,
-        out_grad,
         small,
         dq,
         dkv,
@@ -1890,24 +1955,24 @@
         joint,
         stem_out,
         middle_grad,
-        gain_first,
+        gain_one,
         w_skip,
     )
-    results = finish(results, small_sum, gain_sum)
-    input_grad, skip_grad, down_share, up_share, qkv_share, out_share, skip_share, mine = results
+    *results, up_bias, gain_a, gain_b, down_bias = finish(results, small_sum, gain_sum)
+    input_grad, skip_grad, down_share, up_share, qkv_share, out_share, skip_share = results
     return (
         output[None],
         input_grad[None],
         skip_grad[None],
         skip_share,
-        mine[1, :32],
+        gain_a.reshape(32),
         qkv_share,
         out_share,
-        mine[2, :32],
+        gain_b.reshape(32),
         up_share,
-        mine[0],
+        up_bias.reshape(128),
         down_share,
-        mine[3, :32],
+        down_bias.reshape(32),
     )
 
 

time: 257 us -> 243 us (0.946)
  Pallas kernels: 244 us -> 234 us
  local copies, waits for them, and re-layouts: 6.55 us -> 0.87 us
    pallas_call x1, Pallas kernels: 63.8 us -> 58.3 us  [middle(): pl.pallas_call(middle_kernel, out_shape=[jax.ShapeDtypeStruct((FRAMES, D)...]
    pallas_call x1, Pallas kernels: 89.3 us -> 85.4 us  [tail(): pl.pallas_call(tail_kernel, out_shape=out_shape, in_specs=[hbm] * 18 + [v...]
    broadcast_in_dim x4 -> x0, local copies, waits for them, and re-layouts: 3.17 us -> none  [the longest x1 1.3 us: body_chips(): gain_first = jnp.broadcast_to(gain_one.astype(F32), (8, D))]
  transfers between devices with their start and end apart: 4 -> 5, of which waited for: 0 -> 0; matrix products, arithmetic and copies ran while one was open for 0% -> 0% of each run, Pallas kernels for 13% -> 14%
where the time goes in v2:
time: 243 us; the launch traced here: 241 us
  Pallas kernels  234 us (96%)
  starting transfers between devices  4.67 us (2%)
    pallas_call x1, Pallas kernels, tail(): pl.pallas_call(tail_kernel, out_shape=out_shape, in_specs=[hbm] * 18 + [v...  85.4 us
    pallas_call x1, Pallas kernels, middle(): pl.pallas_call(middle_kernel, out_shape=[jax.ShapeDtypeStruct((FRAMES, D)...  58.3 us
    pallas_call x1, Pallas kernels, attend_back(): pl.pallas_call(functools.partial(attend_back_kernel, bq, bk, heads), out_...  33.3 us
    pallas_call x1, Pallas kernels, front(): pl.pallas_call(front_kernel, out_shape=[jax.ShapeDtypeStruct((FRAMES, D),...  28.4 us
    pallas_call x1, Pallas kernels, attend(): pl.pallas_call(functools.partial(attend_kernel, bq, bk, heads), out_shape...  24.6 us
  transfers between devices with their start and end apart: 5, of which 0 were waited for; matrix products, arithmetic and copies ran while one was open for 0% of the time, Pallas kernels for 14%

profile of v2, /device:TPU:0, one launch (start us, length us, event | category | flops | bytes accessed | tf_op | source)
XLA Modules:
  0.0 240.9 jit_solution(1307590871213449979)
XLA Ops:
  0.6 28.4 %front.1 = (f32[512,1024]{1,0:T(8,128)}, bf16[1792,1024]{1,0:T(8,128)(2,1)}, bf16[1024,512]{1,0:T(8,128)(2,1)}, bf16[1792,1024]{1,0:T(8,128)(2,1)}, bf16[2048,512]{1,0:T(8,128)(2,1)}) custom-call(bf16[512,1024]{1,0:T(8,128)(2,1)} %bitcast.13, bf16[512,1024]{1,0:T(8,128)(2,1)} %bitcast.14, bf16[2048,1024]{1,0:T(8,128)(2,1)} %refs_19_.1, ...), custom_call_target="tpu_custom_call" | custom-call | flops 8000000000 | bytes 24000000 | tf_op jit(solution)/shard_map/front/pallas_call | solution.py:236
  29.1 24.6 %attend.1 = (bf16[1024,512]{1,0:T(8,128)(2,1)}, bf16[512,1024]{1,0:T(8,128)(2,1)}, f32[4,2048]{1,0:T(4,128)}) custom-call(s32[1,2048]{1,0:T(1,128)} %seg.3, bf16[1024,512]{1,0:T(8,128)(2,1)} %get-tuple-element.57.q_in, bf16[1792,1024]{1,0:T(8,128)(2,1)} %get-tuple-element.58.kv_in, s32[1,2048]{1,0:T(1,128)} %seg.3, s32[1,2048]{1,0:T(1,128)} %valid.3), custom_call_target="tpu_custom_call" | custom-call | flops 8000000000 | bytes 8000000 | tf_op jit(solution)/shard_map/attend/pallas_call | solution.py:464
  53.7 58.3 %middle.1 = (bf16[512,1024]{1,0:T(8,128)(2,1)}, f32[512,1024]{1,0:T(8,128)}, bf16[1024,512]{1,0:T(8,128)(2,1)}, f32[48,128]{1,0:T(8,128)}, bf16[4,128,640]{2,1,0...) custom-call(bf16[1024,512]{1,0:T(8,128)(2,1)} %get-tuple-element.59., ...), custom_call_target="tpu_custom_call" | custom-call | flops 28000000000 | bytes 40000000 | tf_op jit(solution)/shard_map/middle/pallas_call | solution.py:1222
  111.9 0.2 collective-permute-start.3
  112.1 0.0 collective-permute-start.1
  112.1 1.1 collective-permute-start.4
  113.2 1.5 collective-permute-start
  114.7 1.9 collective-permute-start.2
  116.6 33.3 %attend_back.1 = (bf16[1024,512]{1,0:T(8,128)(2,1)}, bf16[1792,1024]{1,0:T(8,128)(2,1)}, bf16[512,1024]{1,0:T(8,128)(2,1)}) custom-call(s32[1,2048]{1,0:T(1,128)} %seg.3, bf16[1024,512]{1,0:T(8,128)(2,1)} %get-tuple-element.57.q_in, bf16[1792,1024]{1,0:T(8,128)(2,1)} %get-tuple-element.58.kv_in, bf16[1024,512]{1,0:T(8,128)(2,1)} %get-tuple-element.61.grad_in, ...), custom_call_target="tpu_custom_call" | custom-call | flops 20000000000 | bytes 16000000 | tf_op jit(solution)/shard_map/attend_back/pallas_call | solution.py:645
  149.9 0.0 collective-permute-done.3
  149.9 0.0 collective-permute-done.1.refs_3_
  149.9 0.0 collective-permute-done.4.refs_9_
  149.9 0.0 collective-permute-done.refs_1_
  149.9 0.0 collective-permute-done.2.refs_5_
  149.9 0.0 copy-start
  150.0 0.9 copy-done
  150.8 85.4 %tail.1 = (bf16[512,1024]{1,0:T(8,128)(2,1)}, bf16[512,1024]{1,0:T(8,128)(2,1)}, f32[128,1024]{1,0:T(8,128)}, f32[32,4096]{1,0:T(8,128)}, f32[32,3072]{1,0:T(8,1...) custom-call(bf16[4,128,640]{2,1,0:T(8,128)(2,1)} %get-tuple-element.66.refs_0_, ...), custom_call_target="tpu_custom_call" | custom-call | flops 16999999488 | bytes 60000000 | tf_op jit(solution)/shard_map/tail/pallas_call | solution.py:1824
  236.2 4.5 %finish.1 = (bf16[512,1024]{1,0:T(8,128)(2,1)}, bf16[512,1024]{1,0:T(8,128)(2,1)}, f32[128,1024]{1,0:T(8,128)}, f32[32,4096]{1,0:T(8,128)}, f32[32,3072]{1,0:T(8...) custom-call(bf16[512,1024]{1,0:T(8,128)(2,1)} %get-tuple-element.82., ...), custom_call_target="tpu_custom_call" | custom-call | tf_op jit(solution)/shard_map/finish/pallas_call | solution.py:1878
Async XLA Ops:
  111.9 38.0 %collective-permute-start.3 = (bf16[2,128,512]{2,1,0:T(8,128)(2,1)}, bf16[2,128,512]{2,1,0:T(8,128)(2,1)}, u32[]{:S(2)}, u32[]{:S(2)}) collective-permute-start(bf16[2,128,512]{2,1,0:T(8,128)(2,1)} %get-tuple-element.73), channel_id=1, source_target_pairs={{0,4},{4,0},{8,12},{12,8},{16,20},{20,16},{24,28},{28,24},{1,5},{5... | collective-permute-start | bytes 786440 | tf_op jit(solution)/shard_map/ppermute | solution.py:1901
  112.1 37.8 %collective-permute-start.1 = (bf16[2,2,128,384]{3,2,1,0:T(8,128)(2,1)}, bf16[2,2,128,384]{3,2,1,0:T(8,128)(2,1)}, u32[]{:S(2)}, u32[]{:S(2)}) collective-permute-start(bf16[2,2,128,384]{3,2,1,0:T(8,128)(2,1)} %get-tuple-element.69), channel_id=1, source_target_pairs={{0,2},{1,3},{2,0},{3,1},{4,6},{5,7},{6,4},{7,5},{8,10},{9,11},{10,... | collective-permute-start | bytes 1179656 | tf_op jit(solution)/shard_map/ppermute | solution.py:1905
  112.1 37.8 %collective-permute-start.4 = (bf16[2,2,2,32,1024]{4,3,2,1,0:T(8,128)(2,1)}, bf16[2,2,2,32,1024]{4,3,2,1,0:T(8,128)(2,1)}, u32[]{:S(2)}, u32[]{:S(2)}) collective-permute-start(bf16[2,2,2,32,1024]{4,3,2,1,0:T(8,128)(2,1)} %get-tuple-element.75), channel_id=1, source_target_pairs={{0,8},{4,12},{8,0},{12,4},{16,24},{20,28},{24,16},{28,20},{1,9},{5... | collective-permute-start | bytes 1572872 | tf_op jit(solution)/shard_map/ppermute | solution.py:1897
  113.2 36.8 %collective-permute-start = (bf16[4,128,640]{2,1,0:T(8,128)(2,1)}, bf16[4,128,640]{2,1,0:T(8,128)(2,1)}, u32[]{:S(2)}, u32[]{:S(2)}) collective-permute-start(bf16[4,128,640]{2,1,0:T(8,128)(2,1)} %get-tuple-element.67), channel_id=1, source_target_pairs={{0,4},{4,0},{8,12},{12,8},{16,20},{20,16},{24,28},{28,24},{1,5},{5... | collective-permute-start | bytes 1966088 | tf_op jit(solution)/shard_map/ppermute | solution.py:1901
  114.7 35.2 %collective-permute-start.2 = (bf16[4,64,1536]{2,1,0:T(8,128)(2,1)}, bf16[4,64,1536]{2,1,0:T(8,128)(2,1)S(1)}, u32[]{:S(2)}, u32[]{:S(2)}) collective-permute-start(bf16[4,64,1536]{2,1,0:T(8,128)(2,1)} %get-tuple-element.71), channel_id=1, source_target_pairs={{0,2},{1,3},{2,0},{3,1},{4,6},{5,7},{6,4},{7,5},{8,10},{9,11},{10,... | collective-permute-start | bytes 2359304 | tf_op jit(solution)/shard_map/ppermute | solution.py:1905
  149.9 0.9 copy-start

commit v3 on v2

--- a/solution.py
+++ b/solution.py
@@ -1477,7 +1477,7 @@
         return Unit(links, unit_own.at[k], came, room(ROWS, D), y_first, done)
 
     wo = HighUnit(links, wo_own, (wo_r1, wo_r2, wo_r3, wo_r4), to_wo)
-    unit_q, unit_v = unit(0, False, to_qkv(0)), unit(1, True, to_qkv(2))
+    unit_q, unit_v = unit(0, False, to_qkv(0)), unit(1, False, to_qkv(2))
     unit_k = LowUnit(links, low_own, (low_r1, low_r2, low_r3, low_r4), None, False, to_qkv(1))
 
     def skip_unit(k, y_first, done):
@@ -1664,77 +1664,77 @@
     skip_core3 = skip_part(3)
     rest_z.turn_third()
     skip_begin(2, skip_core2)
+    wo.turn_third()
     skip_begin(3, skip_core3)
     got_wskip.wait()
     joined_part(0)
+    small.turn()
     joined_part(1)
     gain_sum.turn()
     joined_part(2)
     joined_part(3)
     x0.turn_third()
+    unit_v.turn_first()
     joined_part(4)
     joined_part(5)
     joined_part(6)
-    unit_q.turn_first()
     joined_part(7)
     p0.turn_fourth()
-    skips[0][1].turn_first()
-    unit_v.turn_first()
+    skips[0][0].turn_first()
     x1.turn_third()
     p1.turn_fourth()
-    skips[1][1].turn_first()
-    wo.turn_third()
-    small.turn()
-    skips[2][1].turn_first()
-    skips[0][0].turn_first()
-    skips[3][1].turn_first()
-    x0.turn_fourth()
-    p0.finish()
     skips[1][0].turn_first()
-    p1.finish()
-    unit_k.turn_first()
+    unit_q.turn_first()
     skips[2][0].turn_first()
-    x0.finish()
-    unit_v.turn_second()
-    small.turn()
+    skips[0][1].turn_first()
     skips[3][0].turn_first()
     gain_sum.turn()
+    p0.finish()
+    p1.finish()
+    skips[1][1].turn_first()
+    unit_k.turn_first()
+    x0.turn_fourth()
+    skips[2][1].turn_first()
+    unit_v.turn_second()
+    skips[3][1].turn_first()
+    rest_q.finish()
+    small.turn()
     skips[0][0].turn_second()
     x1.turn_fourth()
-    rest_q.finish()
-    skips[1][0].turn_second()
+    x0.finish()
     rest_z.finish()
     unit_q.turn_second()
     unit_v.turn_third()
+    skips[1][0].turn_second()
     skips[0][1].turn_second()
+    skips[2][0].turn_second()
+    wo.finish()
+    skips[1][1].turn_second()
+    unit_q.turn_third()
     x1.finish()
-    wo.finish()
-    unit_k.turn_second()
+    skips[3][0].turn_second()
+    unit_v.turn_fourth()
+    gain_sum.turn()
+    skips[2][1].turn_second()
     take_up()
-    skips[1][1].turn_second()
-    skips[2][0].turn_second()
-    skips[2][1].turn_second()
-    unit_v.turn_fourth()
-    skips[3][0].turn_second()
-    gain_sum.turn()
     skips[3][1].turn_second()
     small.turn()
+    unit_k.turn_second()
+    unit_q.turn_fourth()
+    skips[0][0].finish()
     unit_k.turn_third()
-    skips[0][0].finish()
     skips[1][0].finish()
-    unit_q.turn_third()
+    unit_v.finish()
     skips[0][1].finish()
-    skips[1][1].finish()
-    unit_v.finish()
-    unit_q.turn_fourth()
     skips[2][0].finish()
     gain_sum.turn()
+    skips[1][1].finish()
+    skips[3][0].finish()
+    unit_q.finish()
     skips[2][1].finish()
-    unit_q.finish()
-    skips[3][0].finish()
+    gain_sum.turn()
     skips[3][1].finish()
     small.turn()
-    gain_sum.turn()
     unit_k.finish()
     links.drain()
 

time: 243 us -> 240 us (0.988)
    pallas_call x1, Pallas kernels: 85.4 us -> 90.9 us  [tail(): pl.pallas_call(tail_kernel, out_shape=out_shape, in_specs=[hbm] * 18 + [v...]
    pallas_call x1, Pallas kernels: 33.3 us -> 28.3 us  [attend_back(): pl.pallas_call(functools.partial(attend_back_kernel, bq, bk, heads), out_...]
    pallas_call x1, Pallas kernels: 24.6 us -> 20.8 us  [attend(): pl.pallas_call(functools.partial(attend_kernel, bq, bk, heads), out_shape...]
  transfers between devices with their start and end apart: 5 -> 5, of which waited for: 0 -> 0; matrix products, arithmetic and copies ran while one was open for 0% -> 0% of each run, Pallas kernels for 14% -> 12%
where the time goes in v3:
time: 240 us; the launch traced here: 239 us
  Pallas kernels  232 us (97%)
  starting transfers between devices  4.62 us (2%)
    pallas_call x1, Pallas kernels, tail(): pl.pallas_call(tail_kernel, out_shape=out_shape, in_specs=[hbm] * 18 + [v...  90.9 us
    pallas_call x1, Pallas kernels, middle(): pl.pallas_call(middle_kernel, out_shape=[jax.ShapeDtypeStruct((FRAMES, D)...  59.4 us
    pallas_call x1, Pallas kernels, front(): pl.pallas_call(front_kernel, out_shape=[jax.ShapeDtypeStruct((FRAMES, D),...  28.4 us
    pallas_call x1, Pallas kernels, attend_back(): pl.pallas_call(functools.partial(attend_back_kernel, bq, bk, heads), out_...  28.3 us
    pallas_call x1, Pallas kernels, attend(): pl.pallas_call(functools.partial(attend_kernel, bq, bk, heads), out_shape...  20.8 us
  transfers between devices with their start and end apart: 5, of which 0 were waited for; matrix products, arithmetic and copies ran while one was open for 0% of the time, Pallas kernels for 12%

profile of v3, /device:TPU:0, one launch (start us, length us, event | category | flops | bytes accessed | tf_op | source)
XLA Modules:
  0.0 238.8 jit_solution(3027428808836970784)
XLA Ops:
  0.6 28.4 %front.1 = (f32[512,1024]{1,0:T(8,128)}, bf16[1792,1024]{1,0:T(8,128)(2,1)}, bf16[1024,512]{1,0:T(8,128)(2,1)}, bf16[1792,1024]{1,0:T(8,128)(2,1)}, bf16[2048,512]{1,0:T(8,128)(2,1)}) custom-call(bf16[512,1024]{1,0:T(8,128)(2,1)} %bitcast.13, bf16[512,1024]{1,0:T(8,128)(2,1)} %bitcast.14, bf16[2048,1024]{1,0:T(8,128)(2,1)} %refs_19_.1, ...), custom_call_target="tpu_custom_call" | custom-call | flops 8000000000 | bytes 24000000 | tf_op jit(solution)/shard_map/front/pallas_call | solution.py:236
  29.1 20.8 %attend.1 = (bf16[1024,512]{1,0:T(8,128)(2,1)}, bf16[512,1024]{1,0:T(8,128)(2,1)}, f32[4,2048]{1,0:T(4,128)}) custom-call(s32[1,2048]{1,0:T(1,128)} %seg.3, bf16[1024,512]{1,0:T(8,128)(2,1)} %get-tuple-element.57.q_in, bf16[1792,1024]{1,0:T(8,128)(2,1)} %get-tuple-element.58.kv_in, s32[1,2048]{1,0:T(1,128)} %seg.3, s32[1,2048]{1,0:T(1,128)} %valid.3), custom_call_target="tpu_custom_call" | custom-call | flops 8000000000 | bytes 8000000 | tf_op jit(solution)/shard_map/attend/pallas_call | solution.py:464
  49.9 59.4 %middle.1 = (bf16[512,1024]{1,0:T(8,128)(2,1)}, f32[512,1024]{1,0:T(8,128)}, bf16[1024,512]{1,0:T(8,128)(2,1)}, f32[48,128]{1,0:T(8,128)}, bf16[4,128,640]{2,1,0...) custom-call(bf16[1024,512]{1,0:T(8,128)(2,1)} %get-tuple-element.59., ...), custom_call_target="tpu_custom_call" | custom-call | flops 28000000000 | bytes 40000000 | tf_op jit(solution)/shard_map/middle/pallas_call | solution.py:1222
  109.3 1.6 collective-permute-start.3
  110.9 2.2 collective-permute-start.1
  113.1 0.6 collective-permute-start.4
  113.7 0.2 collective-permute-start
  113.9 0.0 collective-permute-start.2
  113.9 28.3 %attend_back.1 = (bf16[1024,512]{1,0:T(8,128)(2,1)}, bf16[1792,1024]{1,0:T(8,128)(2,1)}, bf16[512,1024]{1,0:T(8,128)(2,1)}) custom-call(s32[1,2048]{1,0:T(1,128)} %seg.3, bf16[1024,512]{1,0:T(8,128)(2,1)} %get-tuple-element.57.q_in, bf16[1792,1024]{1,0:T(8,128)(2,1)} %get-tuple-element.58.kv_in, bf16[1024,512]{1,0:T(8,128)(2,1)} %get-tuple-element.61.grad_in, ...), custom_call_target="tpu_custom_call" | custom-call | flops 20000000000 | bytes 16000000 | tf_op jit(solution)/shard_map/attend_back/pallas_call | solution.py:645
  142.2 0.0 collective-permute-done.3
  142.3 0.0 collective-permute-done.1.refs_3_
  142.3 0.0 collective-permute-done.4.refs_9_
  142.3 0.0 collective-permute-done.refs_1_
  142.3 0.0 collective-permute-done.2.refs_5_
  142.3 0.0 copy-start
  142.3 0.9 copy-done
  143.2 90.9 %tail.1 = (bf16[512,1024]{1,0:T(8,128)(2,1)}, bf16[512,1024]{1,0:T(8,128)(2,1)}, f32[128,1024]{1,0:T(8,128)}, f32[32,4096]{1,0:T(8,128)}, f32[32,3072]{1,0:T(8,1...) custom-call(bf16[4,128,640]{2,1,0:T(8,128)(2,1)} %get-tuple-element.66.refs_0_, ...), custom_call_target="tpu_custom_call" | custom-call | flops 16999999488 | bytes 60000000 | tf_op jit(solution)/shard_map/tail/pallas_call | solution.py:1824
  234.1 4.5 %finish.1 = (bf16[512,1024]{1,0:T(8,128)(2,1)}, bf16[512,1024]{1,0:T(8,128)(2,1)}, f32[128,1024]{1,0:T(8,128)}, f32[32,4096]{1,0:T(8,128)}, f32[32,3072]{1,0:T(8...) custom-call(bf16[512,1024]{1,0:T(8,128)(2,1)} %get-tuple-element.82., ...), custom_call_target="tpu_custom_call" | custom-call | tf_op jit(solution)/shard_map/finish/pallas_call | solution.py:1878
Async XLA Ops:
  109.3 33.0 %collective-permute-start.3 = (bf16[2,128,512]{2,1,0:T(8,128)(2,1)}, bf16[2,128,512]{2,1,0:T(8,128)(2,1)}, u32[]{:S(2)}, u32[]{:S(2)}) collective-permute-start(bf16[2,128,512]{2,1,0:T(8,128)(2,1)} %get-tuple-element.73), channel_id=1, source_target_pairs={{0,4},{4,0},{8,12},{12,8},{16,20},{20,16},{24,28},{28,24},{1,5},{5... | collective-permute-start | bytes 786440 | tf_op jit(solution)/shard_map/ppermute | solution.py:1901
  110.9 31.4 %collective-permute-start.1 = (bf16[2,2,128,384]{3,2,1,0:T(8,128)(2,1)}, bf16[2,2,128,384]{3,2,1,0:T(8,128)(2,1)}, u32[]{:S(2)}, u32[]{:S(2)}) collective-permute-start(bf16[2,2,128,384]{3,2,1,0:T(8,128)(2,1)} %get-tuple-element.69), channel_id=1, source_target_pairs={{0,2},{1,3},{2,0},{3,1},{4,6},{5,7},{6,4},{7,5},{8,10},{9,11},{10,... | collective-permute-start | bytes 1179656 | tf_op jit(solution)/shard_map/ppermute | solution.py:1905
  113.1 29.2 %collective-permute-start.4 = (bf16[2,2,2,32,1024]{4,3,2,1,0:T(8,128)(2,1)}, bf16[2,2,2,32,1024]{4,3,2,1,0:T(8,128)(2,1)}, u32[]{:S(2)}, u32[]{:S(2)}) collective-permute-start(bf16[2,2,2,32,1024]{4,3,2,1,0:T(8,128)(2,1)} %get-tuple-element.75), channel_id=1, source_target_pairs={{0,8},{4,12},{8,0},{12,4},{16,24},{20,28},{24,16},{28,20},{1,9},{5... | collective-permute-start | bytes 1572872 | tf_op jit(solution)/shard_map/ppermute | solution.py:1897
  113.7 28.6 %collective-permute-start = (bf16[4,128,640]{2,1,0:T(8,128)(2,1)}, bf16[4,128,640]{2,1,0:T(8,128)(2,1)}, u32[]{:S(2)}, u32[]{:S(2)}) collective-permute-start(bf16[4,128,640]{2,1,0:T(8,128)(2,1)} %get-tuple-element.67), channel_id=1, source_target_pairs={{0,4},{4,0},{8,12},{12,8},{16,20},{20,16},{24,28},{28,24},{1,5},{5... | collective-permute-start | bytes 1966088 | tf_op jit(solution)/shard_map/ppermute | solution.py:1901
  113.9 28.4 %collective-permute-start.2 = (bf16[4,64,1536]{2,1,0:T(8,128)(2,1)}, bf16[4,64,1536]{2,1,0:T(8,128)(2,1)S(1)}, u32[]{:S(2)}, u32[]{:S(2)}) collective-permute-start(bf16[4,64,1536]{2,1,0:T(8,128)(2,1)} %get-tuple-element.71), channel_id=1, source_target_pairs={{0,2},{1,3},{2,0},{3,1},{4,6},{5,7},{6,4},{7,5},{8,10},{9,11},{10,... | collective-permute-start | bytes 2359304 | tf_op jit(solution)/shard_map/ppermute | solution.py:1905
  142.3 0.9 copy-start

commit v4 on v3

--- a/solution.py
+++ b/solution.py
@@ -28,6 +28,7 @@
 SKIPS = 4
 SKIP_COLS = D // SKIPS
 FAR = 1e30
+VMEM_ALL = 67_043_328
 MESH = pl.DeviceIdType.MESH
 VMEM = pltpu.MemorySpace.VMEM
 SMEM = pltpu.MemorySpace.SMEM
@@ -265,7 +266,7 @@
             flops=8_000_000_000, bytes_accessed=24_000_000, transcendentals=0
         ),
         compiler_params=pltpu.CompilerParams(
-            collective_id=2, has_side_effects=True, vmem_limit_bytes=63 << 20
+            collective_id=2, has_side_effects=True, vmem_limit_bytes=VMEM_ALL
         ),
     )(first, second, wskip, gain, wqkv)
 
@@ -493,7 +494,7 @@
         cost_estimate=pl.CostEstimate(
             flops=8_000_000_000, bytes_accessed=8_000_000, transcendentals=4_000_000
         ),
-        compiler_params=pltpu.CompilerParams(vmem_limit_bytes=63 << 20),
+        compiler_params=pltpu.CompilerParams(vmem_limit_bytes=VMEM_ALL),
     )(seg, q, kv, seg, valid)
 
 
@@ -679,7 +680,7 @@
         cost_estimate=pl.CostEstimate(
             flops=20_000_000_000, bytes_accessed=16_000_000, transcendentals=4_000_000
         ),
-        compiler_params=pltpu.CompilerParams(vmem_limit_bytes=63 << 20),
+        compiler_params=pltpu.CompilerParams(vmem_limit_bytes=VMEM_ALL),
     )(seg, q, kv, grad, outt, lse, seg, valid, passed)
 
 
@@ -1267,7 +1268,7 @@
             flops=28_000_000_000, bytes_accessed=40_000_000, transcendentals=4_000_000
         ),
         compiler_params=pltpu.CompilerParams(
-            collective_id=1, has_side_effects=True, vmem_limit_bytes=63 << 20
+            collective_id=1, has_side_effects=True, vmem_limit_bytes=VMEM_ALL
         ),
     )(att, stem, wout, gain, w_up, w_down, bias_up, bias_down, cot)
 
@@ -1832,7 +1833,7 @@
             flops=17_000_000_000, bytes_accessed=60_000_000, transcendentals=0
         ),
         compiler_params=pltpu.CompilerParams(
-            collective_id=0, has_side_effects=True, vmem_limit_bytes=63 << 20
+            collective_id=0, has_side_effects=True, vmem_limit_bytes=VMEM_ALL
         ),
     )(
         *late[:6],
@@ -1889,7 +1890,7 @@
             pltpu.SemaphoreType.DMA((count,)),
         ],
         name="finish",
-        compiler_params=pltpu.CompilerParams(vmem_limit_bytes=63 << 20),
+        compiler_params=pltpu.CompilerParams(vmem_limit_bytes=VMEM_ALL),
     )(*results, small, gain)
 
 

time: 240 us -> 243 us (1.012); the launches traced: 239 us -> 244 us
  starting transfers between devices: 4.62 us -> 8.04 us
  Pallas kernels: 232 us -> 235 us
    ppermute x2, starting transfers between devices: 2.23 us -> 5.44 us  [swap_chip(): return lax.ppermute(value, 'seq', [(i, i ^ 2) for i in range(4)])]
    pallas_call x1, Pallas kernels: 90.9 us -> 93.9 us  [tail(): pl.pallas_call(tail_kernel, out_shape=out_shape, in_specs=[hbm] * 18 + [v...]
where the time goes in v4:
time: 243 us; the launch traced here: 244 us
  Pallas kernels  235 us (97%)
  starting transfers between devices  8.04 us (3%)
    pallas_call x1, Pallas kernels, tail(): pl.pallas_call(tail_kernel, out_shape=out_shape, in_specs=[hbm] * 18 + [v...  93.9 us
    pallas_call x1, Pallas kernels, middle(): pl.pallas_call(middle_kernel, out_shape=[jax.ShapeDtypeStruct((FRAMES, D)...  59.5 us
    pallas_call x1, Pallas kernels, front(): pl.pallas_call(front_kernel, out_shape=[jax.ShapeDtypeStruct((FRAMES, D),...  28.4 us
    pallas_call x1, Pallas kernels, attend_back(): pl.pallas_call(functools.partial(attend_back_kernel, bq, bk, heads), out_...  28.3 us
    pallas_call x1, Pallas kernels, attend(): pl.pallas_call(functools.partial(attend_kernel, bq, bk, heads), out_shape...  20.8 us
    ppermute x2, starting transfers between devices, swap_chip(): return lax.ppermute(value, 'seq', [(i, i ^ 2) for i in range(4)])  5.44 us
  transfers between devices with their start and end apart: 5, of which 0 were waited for; matrix products, arithmetic and copies ran while one was open for 0% of the time, Pallas kernels for 12%

profile of v4, /device:TPU:0, one launch (start us, length us, event | category | flops | bytes accessed | tf_op | source)
XLA Modules:
  0.0 244.4 jit_solution(15849436863133213104)
XLA Ops:
  0.6 28.4 %front.1 = (f32[512,1024]{1,0:T(8,128)}, bf16[1792,1024]{1,0:T(8,128)(2,1)}, bf16[1024,512]{1,0:T(8,128)(2,1)}, bf16[1792,1024]{1,0:T(8,128)(2,1)}, bf16[2048,512]{1,0:T(8,128)(2,1)}) custom-call(bf16[512,1024]{1,0:T(8,128)(2,1)} %bitcast.13, bf16[512,1024]{1,0:T(8,128)(2,1)} %bitcast.14, bf16[2048,1024]{1,0:T(8,128)(2,1)} %refs_19_.1, ...), custom_call_target="tpu_custom_call" | custom-call | flops 8000000000 | bytes 24000000 | tf_op jit(solution)/shard_map/front/pallas_call | solution.py:237
  29.1 20.8 %attend.1 = (bf16[1024,512]{1,0:T(8,128)(2,1)}, bf16[512,1024]{1,0:T(8,128)(2,1)}, f32[4,2048]{1,0:T(4,128)}) custom-call(s32[1,2048]{1,0:T(1,128)} %seg.3, bf16[1024,512]{1,0:T(8,128)(2,1)} %get-tuple-element.57.q_in, bf16[1792,1024]{1,0:T(8,128)(2,1)} %get-tuple-element.58.kv_in, s32[1,2048]{1,0:T(1,128)} %seg.3, s32[1,2048]{1,0:T(1,128)} %valid.3), custom_call_target="tpu_custom_call" | custom-call | flops 8000000000 | bytes 8000000 | tf_op jit(solution)/shard_map/attend/pallas_call | solution.py:465
  49.9 59.5 %middle.1 = (bf16[512,1024]{1,0:T(8,128)(2,1)}, f32[512,1024]{1,0:T(8,128)}, bf16[1024,512]{1,0:T(8,128)(2,1)}, f32[48,128]{1,0:T(8,128)}, bf16[4,128,640]{2,1,0...) custom-call(bf16[1024,512]{1,0:T(8,128)(2,1)} %get-tuple-element.59., ...), custom_call_target="tpu_custom_call" | custom-call | flops 28000000000 | bytes 40000000 | tf_op jit(solution)/shard_map/middle/pallas_call | solution.py:1223
  109.4 2.0 collective-permute-start.3
  111.4 5.4 %collective-permute-start.1 = (bf16[2,2,128,384]{3,2,1,0:T(8,128)(2,1)}, bf16[2,2,128,384]{3,2,1,0:T(8,128)(2,1)}, u32[]{:S(2)}, u32[]{:S(2)}) collective-permute-start(bf16[2,2,128,384]{3,2,1,0:T(8,128)(2,1)} %get-tuple-element.69), channel_id=1, source_target_pairs={{0,2},{1,3},{2,0},{3,1},{4,6},{5,7},{6,4},{7,5},{8,10},{9,11},{10,... | collective-permute-start | bytes 1179656 | tf_op jit(solution)/shard_map/ppermute | solution.py:1906
  116.8 0.6 collective-permute-start.4
  117.3 0.1 collective-permute-start
  117.4 0.1 collective-permute-start.2
  117.5 28.3 %attend_back.1 = (bf16[1024,512]{1,0:T(8,128)(2,1)}, bf16[1792,1024]{1,0:T(8,128)(2,1)}, bf16[512,1024]{1,0:T(8,128)(2,1)}) custom-call(s32[1,2048]{1,0:T(1,128)} %seg.3, bf16[1024,512]{1,0:T(8,128)(2,1)} %get-tuple-element.57.q_in, bf16[1792,1024]{1,0:T(8,128)(2,1)} %get-tuple-element.58.kv_in, bf16[1024,512]{1,0:T(8,128)(2,1)} %get-tuple-element.61.grad_in, ...), custom_call_target="tpu_custom_call" | custom-call | flops 20000000000 | bytes 16000000 | tf_op jit(solution)/shard_map/attend_back/pallas_call | solution.py:646
  145.8 0.0 collective-permute-done.3
  145.8 0.0 collective-permute-done.1.refs_3_
  145.8 0.0 collective-permute-done.4.refs_9_
  145.8 0.0 collective-permute-done.refs_1_
  145.8 0.0 collective-permute-done.2.refs_5_
  145.8 93.9 %tail.1 = (bf16[512,1024]{1,0:T(8,128)(2,1)}, bf16[512,1024]{1,0:T(8,128)(2,1)}, f32[128,1024]{1,0:T(8,128)}, f32[32,4096]{1,0:T(8,128)}, f32[32,3072]{1,0:T(8,1...) custom-call(bf16[4,128,640]{2,1,0:T(8,128)(2,1)} %get-tuple-element.66.refs_0_, ...), custom_call_target="tpu_custom_call" | custom-call | flops 16999999488 | bytes 60000000 | tf_op jit(solution)/shard_map/tail/pallas_call | solution.py:1825
  239.7 4.5 %finish.1 = (bf16[512,1024]{1,0:T(8,128)(2,1)}, bf16[512,1024]{1,0:T(8,128)(2,1)}, f32[128,1024]{1,0:T(8,128)}, f32[32,4096]{1,0:T(8,128)}, f32[32,3072]{1,0:T(8...) custom-call(bf16[512,1024]{1,0:T(8,128)(2,1)} %get-tuple-element.82., ...), custom_call_target="tpu_custom_call" | custom-call | tf_op jit(solution)/shard_map/finish/pallas_call | solution.py:1879
Async XLA Ops:
  109.4 36.4 %collective-permute-start.3 = (bf16[2,128,512]{2,1,0:T(8,128)(2,1)}, bf16[2,128,512]{2,1,0:T(8,128)(2,1)}, u32[]{:S(2)}, u32[]{:S(2)}) collective-permute-start(bf16[2,128,512]{2,1,0:T(8,128)(2,1)} %get-tuple-element.73), channel_id=1, source_target_pairs={{0,4},{4,0},{8,12},{12,8},{16,20},{20,16},{24,28},{28,24},{1,5},{5... | collective-permute-start | bytes 786440 | tf_op jit(solution)/shard_map/ppermute | solution.py:1902
  111.4 34.4 %collective-permute-start.1 = (bf16[2,2,128,384]{3,2,1,0:T(8,128)(2,1)}, bf16[2,2,128,384]{3,2,1,0:T(8,128)(2,1)}, u32[]{:S(2)}, u32[]{:S(2)}) collective-permute-start(bf16[2,2,128,384]{3,2,1,0:T(8,128)(2,1)} %get-tuple-element.69), channel_id=1, source_target_pairs={{0,2},{1,3},{2,0},{3,1},{4,6},{5,7},{6,4},{7,5},{8,10},{9,11},{10,... | collective-permute-start | bytes 1179656 | tf_op jit(solution)/shard_map/ppermute | solution.py:1906
  116.8 29.1 %collective-permute-start.4 = (bf16[2,2,2,32,1024]{4,3,2,1,0:T(8,128)(2,1)}, bf16[2,2,2,32,1024]{4,3,2,1,0:T(8,128)(2,1)}, u32[]{:S(2)}, u32[]{:S(2)}) collective-permute-start(bf16[2,2,2,32,1024]{4,3,2,1,0:T(8,128)(2,1)} %get-tuple-element.75), channel_id=1, source_target_pairs={{0,8},{4,12},{8,0},{12,4},{16,24},{20,28},{24,16},{28,20},{1,9},{5... | collective-permute-start | bytes 1572872 | tf_op jit(solution)/shard_map/ppermute | solution.py:1898
  117.3 28.5 %collective-permute-start = (bf16[4,128,640]{2,1,0:T(8,128)(2,1)}, bf16[4,128,640]{2,1,0:T(8,128)(2,1)}, u32[]{:S(2)}, u32[]{:S(2)}) collective-permute-start(bf16[4,128,640]{2,1,0:T(8,128)(2,1)} %get-tuple-element.67), channel_id=1, source_target_pairs={{0,4},{4,0},{8,12},{12,8},{16,20},{20,16},{24,28},{28,24},{1,5},{5... | collective-permute-start | bytes 1966088 | tf_op jit(solution)/shard_map/ppermute | solution.py:1902
  117.4 28.4 %collective-permute-start.2 = (bf16[4,64,1536]{2,1,0:T(8,128)(2,1)}, bf16[4,64,1536]{2,1,0:T(8,128)(2,1)}, u32[]{:S(2)}, u32[]{:S(2)}) collective-permute-start(bf16[4,64,1536]{2,1,0:T(8,128)(2,1)} %get-tuple-element.71), channel_id=1, source_target_pairs={{0,2},{1,3},{2,0},{3,1},{4,6},{5,7},{6,4},{7,5},{8,10},{9,11},{10,... | collective-permute-start | bytes 2359304 | tf_op jit(solution)/shard_map/ppermute | solution.py:1906
